TPU v7x, 256 devices: a whole 4x4x8 slice. The times are simulated.
256 devices in a mesh: chan: 16 (over z, core), ket: 4 (over y), bra: 4 (over x).
Axes of the slice: x: 4, y: 4, z: 8, core: 2. Of those that a mesh axis runs over, the one named last changes fastest.
Arguments:
- environment: bfloat16 [16, 2048, 2048], P('chan', 'bra', 'ket'), may hold values from -6 to 6
- ket_tensor: bfloat16 [4, 2048, 2048], P(None, 'chan', 'ket'), may hold values from -0.375 to 0.375
- bra_tensor: bfloat16 [4, 2048, 2048], P(None, 'bra', 'chan'), may hold values from -0.5 to 0.5
- charge_left: int32 [2048], replicated, may hold values from 0 to 5, as said below
- charge_right: int32 [2048], replicated, may hold values from 0 to 7, as said below
- op_in: int32 [128], replicated, may hold values from 0 to 15
- op_out: int32 [128], replicated, may hold values from 0 to 15
- op_bra: int32 [128], replicated, may hold values from 0 to 3
- op_ket: int32 [128], replicated, may hold values from 0 to 3
- op_code: int32 [128], replicated, may hold values from -4 to 4
Outputs:
- new_environment: float32 [16, 2048, 2048], P('chan', 'bra', 'ket')
Inputs may be any that keep to these rules, and one draw needn't show every extreme that they name: `charge_left`: charges never fall along the bond, so each charge sector is one contiguous run of states; every charge from 0 to 5 has a sector of one or more states. `charge_right`: charges never fall along the bond, so each charge sector is one contiguous run of states; every charge from 0 to 7 has a sector of one or more states.
All inputs are finite; a program needn't handle non-finite values.
Results may differ from a plain program's by a relative error of at most 0.004.
Values may be sent and summed in bfloat16 or wider, within the bound.
No kernel may reach another device: no remote copies, remote signals or barrier semaphores. Data moves between devices by JAX's collectives and lax.ppermute only.
A program may use at most 64 MiB of HBM per device.

v0:
```python
import jax
import jax.numpy as jnp
from jax import lax
from jax.sharding import PartitionSpec as P


def from_everyone(x, axis):
    peers = lax.axis_size(axis)
    return lax.all_to_all(jnp.broadcast_to(x[None], (peers, *x.shape)), axis, 0, 0, tiled=True)


def in_order(parts, dim):
    lengths = list(parts.shape[1:])
    lengths[dim] *= parts.shape[0]
    return jnp.moveaxis(parts, 0, dim).reshape(lengths)


def gathered_copies(x, axis, dim):
    parts = from_everyone(x, axis)
    return in_order(parts, dim)


def in_blocks(x, dim, peers):
    before, after = (x.shape[:dim], x.shape[dim + 1 :])
    return jnp.moveaxis(x.reshape(*before, peers, -1, *after), dim, 0)


def piece_ends(length, count):
    step = length // count
    if step >= 8:
        step -= step % 8
    return [step * k for k in range(1, count)]


def exchange_in_pieces(x, axis, pieces, split_dim, concat_dim):
    parts = in_blocks(x, split_dim, lax.axis_size(axis))
    widest = max(range(1, max(2, parts.ndim - 1)), key=lambda d: parts.shape[d])
    outs = []
    for section in jnp.split(parts, piece_ends(parts.shape[widest], pieces), axis=widest):
        if section.size:
            outs.append(lax.all_to_all(section, axis, split_axis=0, concat_axis=0, tiled=True))
    return in_order(jnp.concatenate(outs, axis=widest), concat_dim)


def build_coupling(op_in, op_out, op_bra, op_ket, op_code, channels):
    slots = jnp.arange(4 * channels, dtype=jnp.int32)
    pick_in = ((op_in * 4 + op_ket)[:, None] == slots[None, :]).astype(jnp.float32)
    pick_out = ((op_out * 4 + op_bra)[:, None] == slots[None, :]).astype(jnp.float32)
    weights = op_code.astype(jnp.float32) * 0.25
    table = jnp.dot(pick_in.T, pick_out * weights[:, None], precision=lax.Precision.HIGHEST)
    return table.reshape(channels, 4, channels, 4)


def local(
    environment,
    ket_tensor,
    bra_tensor,
    charge_left,
    charge_right,
    op_in,
    op_out,
    op_bra,
    op_ket,
    op_code,
):
    phys = jnp.array([0, 1, 1, 2], dtype=jnp.int32)
    local_chan, bra_rows, ket_cols = environment.shape
    channels = local_chan * lax.axis_size("chan")
    right_ket = ket_tensor.shape[2]
    slice_cols = right_ket // lax.axis_size("chan")
    right_charge = lax.dynamic_slice_in_dim(
        charge_right, lax.axis_index("ket") * right_ket, right_ket
    )
    left_bra = lax.dynamic_slice_in_dim(charge_left, lax.axis_index("bra") * bra_rows, bra_rows)
    full_env = gathered_copies(environment, "ket", 2)
    piece = lax.all_gather(ket_tensor, "chan", axis=1, tiled=True)
    allowed = charge_left[None, :, None] + phys[:, None, None] == right_charge[None, None, :]
    masked = jnp.where(allowed, piece, jnp.zeros((), piece.dtype))
    partial_value = jnp.einsum(
        "wbk,skq->qwsb", full_env, masked, preferred_element_type=jnp.float32
    )
    rounded = partial_value.astype(jnp.bfloat16).reshape(right_ket, local_chan, 4 * bra_rows)
    received = exchange_in_pieces(rounded, "chan", 2, 0, 1)
    coupling = build_coupling(op_in, op_out, op_bra, op_ket, op_code, channels).astype(jnp.bfloat16)
    spread = received.reshape(slice_cols, channels, 4, bra_rows)
    mixed = jnp.einsum(
        "qwsb,wsvt->qvtb", spread, coupling, preferred_element_type=jnp.float32
    ).astype(jnp.bfloat16)
    piece = lax.all_gather(bra_tensor, "chan", axis=2, tiled=True)
    allowed = left_bra[None, :, None] + phys[:, None, None] == charge_right[None, None, :]
    masked = jnp.where(allowed, piece, jnp.zeros((), piece.dtype))
    terms = jnp.einsum("tbp,qvtb->pvq", masked, mixed, preferred_element_type=jnp.float32)
    summed = lax.psum_scatter(terms, "bra", scatter_dimension=0, tiled=True)
    result = lax.all_to_all(summed, "chan", split_axis=1, concat_axis=2, tiled=True)
    return jnp.transpose(result, (1, 0, 2))


def solution(mesh):
    placed = (
        P("chan", "bra", "ket"),
        P(None, "chan", "ket"),
        P(None, "bra", "chan"),
        P(),
        P(),
        P(),
        P(),
        P(),
        P(),
        P(),
    )
    return jax.shard_map(
        local, mesh=mesh, in_specs=placed, out_specs=P("chan", "bra", "ket"), check_vma=False
    )
```

profile of v0, /device:TPU:1, one launch (start us, length us, event | category | flops | bytes accessed | tf_op | source)
XLA Modules:
  0.0 282.4 jit_solution(7501891300677006788)
XLA Ops:
  6.5 0.7 all-gather.3.cloned.1.call-update
  7.3 0.0 all-gather.5.cloned.1.call-start
  7.3 0.7 all-gather.5.cloned.1.call-update
  8.0 2.5 broadcast_in_dim.13
  10.6 5.0 %all-to-all-start = ((bf16[4,1,512,512]{3,2,1,0:T(8,128)(2,1)}), bf16[4,1,512,512]{3,2,1,0:T(8,128)(2,1)S(1)}, u32[]{:S(2)}, u32[]{:S(2)}) async-start(bf16[4,1,512,512]{3,2,1,0:T(8,128)(2,1)} %broadcast_in_dim.13), calls=%async_computation | async-start | bytes 4194304 | tf_op jit(solution)/shard_map/all_to_all | solution.py:9
  15.6 0.1 dynamic_slice.6
  15.6 0.1 broadcast_add_fusion
  15.7 24.5 %all-to-all-done = bf16[4,1,512,512]{3,2,1,0:T(8,128)(2,1)S(1)} async-done(((bf16[4,1,512,512]{3,2,1,0:T(8,128)(2,1)}), bf16[4,1,512,512]{3,2,1,0:T(8,128)(2,1)S(1)}, u32[]{:S(2)}, u32[]{:S(2)}) %all-to-all-start) | async-done | bytes 2097184 | tf_op jit(solution)/shard_map/all_to_all | solution.py:9
  40.2 3.0 %copy.18 = bf16[1,512,4,512]{3,2,1,0:T(4,128)(2,1)} copy(bf16[1,512,4,512]{3,1,0,2:T(8,128)(2,1)S(1)} %bitcast.45) | data formatting | bytes 4194304 | tf_op jit(solution)/shard_map/transpose | solution.py:15
  43.2 3.3 %reshape.85 = bf16[512,2048,1]{1,0,2:T(8,128)(2,1)S(1)} reshape(bf16[1,512,4,512]{3,2,1,0:T(4,128)(2,1)} %copy.18) | data formatting | bytes 4194304 | tf_op jit(solution)/shard_map/reshape.5
  46.5 22.8 %all-gather.3.cloned.1.call-done = bf16[4,2048,512]{2,1,0:T(8,128)(2,1)} async-done(((bf16[4,128,512]{2,1,0:T(8,128)(2,1)}), bf16[4,2048,512]{2,1,0:T(8,128)(2,1)}) %all-gather.3.cloned.1.call-update) | async-done | bytes 8388624 | tf_op jit(solution)/shard_map/all_gather | solution.py:76
  69.3 8.4 %convert_bitcast_fusion = bf16[512,1,4,512]{3,0,2,1:T(8,128)(2,1)S(1)} fusion(bf16[512,2048,1]{1,0,2:T(8,128)(2,1)S(1)} %reshape.85, bf16[4,2048,512]{2,1,0:T(8,128)(2,1)} %all-gather.3.cloned.1.call-done, s32[512]{0:T(512)S(1)} %dynamic_slice.6, s32[4,2048]{1,0:T(4,128)S(1)} %broadcast_add_fusion), kind=kOutput, calls=%fused_computation.14 | convolution fusion | flops 4304404480 | bytes 12617728 | tf_op jit(solution)/shard_map/wbk,skq->qwsb/dot_general | solution.py:79
  77.7 3.0 %copy.20 = bf16[512,1,4,512]{3,2,0,1:T(4,128)(2,1)} copy(bf16[512,1,4,512]{3,0,2,1:T(8,128)(2,1)S(1)} %convert_bitcast_fusion) | data formatting | bytes 4194304 | tf_op jit(solution)/shard_map/convert_element_type | solution.py:82
  80.7 3.3 %reshape_reshape.6 = bf16[16,32,1,2048]{3,1,0,2:T(8,128)(2,1)S(1)} reshape(bf16[512,1,4,512]{3,2,0,1:T(4,128)(2,1)} %copy.20) | data formatting | bytes 4194304 | tf_op jit(solution)/shard_map/reshape;reshape | solution.py:25
  84.0 1.1 slice_bitcast_fusion.1
  85.1 41.0 %all_to_all.24 = bf16[16,16,1,2048]{3,1,2,0:T(8,128)(2,1)S(1)} all-to-all(bf16[16,16,1,2048]{3,1,2,0:T(8,128)(2,1)S(1)} %get-tuple-element.5), channel_id=1, replica_groups=mesh['chan'=16,'ket'=4,'bra'=4] {'chan'}, dimensions={0} | all-to-all | bytes 2097152 | tf_op jit(solution)/shard_map/all_to_all | solution.py:41
  126.1 4.2 %all-to-all-start.2 = ((bf16[16,16,1,2048]{3,1,2,0:T(8,128)(2,1)}), bf16[16,16,1,2048]{3,1,2,0:T(8,128)(2,1)}, u32[]{:S(2)}, u32[]{:S(2)}) async-start(bf16[16,16,1,2048]{3,1,2,0:T(8,128)(2,1)} %get-tuple-element.6), calls=%async_computation.2 | async-start | bytes 2097152 | tf_op jit(solution)/shard_map/all_to_all | solution.py:41
  130.4 0.2 reduce-scatter.2.cloned.1.call-start
  130.6 0.1 dynamic_slice.7
  130.7 0.3 convolution_convert_fusion
  131.0 0.3 convert_element_type.28
  131.4 0.6 copy.24
  131.9 0.1 broadcast_add_fusion.1
  132.0 33.7 %all-to-all-done.2 = bf16[16,16,1,2048]{3,1,2,0:T(8,128)(2,1)} async-done(((bf16[16,16,1,2048]{3,1,2,0:T(8,128)(2,1)}), bf16[16,16,1,2048]{3,1,2,0:T(8,128)(2,1)}, u32[]{:S(2)}, u32[]{:S(2)}) %all-to-all-start.2) | async-done | bytes 1048608 | tf_op jit(solution)/shard_map/all_to_all | solution.py:41
  165.7 1.4 maximum_bitcast_fusion
  167.1 2.8 reshape.92
  169.9 6.6 %all-gather.5.cloned.1.call-done = bf16[4,512,2048]{2,1,0:T(8,128)(2,1)} async-done(((bf16[4,512,128]{2,1,0:T(8,128)(2,1)}), bf16[4,512,2048]{2,1,0:T(8,128)(2,1)}) %all-gather.5.cloned.1.call-update) | async-done | bytes 8388624 | tf_op jit(solution)/shard_map/all_gather | solution.py:89
  176.6 12.2 %fusion.8 = f32[2048,16,32]{0,1,2:T(8,128)} fusion(bf16[4,512,2048]{2,1,0:T(8,128)(2,1)} %all-gather.5.cloned.1.call-done, s32[2048]{0:T(1024)S(1)} %copy-done.2, s32[4,512]{1,0:T(4,128)S(1)} %broadcast_add_fusion.1, bf16[32,16,4,512,1]{3,2,0,1,4:T(4,128)(2,1)} %bitcast.47, bf16[16,4,16,4]{0,2,1,3:T(8,128)(2,1)S(1)} %copy.24), kind=kOutput, calls=%fused_computation.10 | convolution fusion | flops 4438622208 | bytes 14704640 | tf_op jit(solution)/shard_map/tbp,qvtb->pvq/dot_general | solution.py:92
  188.8 47.9 %reduce-scatter.2.cloned.1.call-done = f32[512,16,32]{0,1,2:T(8,128)} async-done(((f32[2048,16,32]{0,1,2:T(8,128)}), f32[512,16,32]{0,1,2:T(8,128)}) %reduce-scatter.2.cloned.1.call-update) | async-done | bytes 1048592 | tf_op jit(solution)/shard_map/reduce_scatter | solution.py:93
  236.7 1.8 copy.26
  238.6 36.0 %all_to_all.25 = f32[512,16,32]{0,2,1:T(8,128)S(1)} all-to-all(f32[512,16,32]{0,2,1:T(8,128)S(1)} %copy.26), channel_id=1, replica_groups=mesh['chan'=16,'ket'=4,'bra'=4] {'chan'}, dimensions={1} | all-to-all | bytes 2097152 | tf_op jit(solution)/shard_map/all_to_all | solution.py:94
  274.6 1.3 copy.27
  (20 shorter events, 0.1 us)
Async XLA Ops:
  6.5 9.1 %copy-start.1 = (s32[4]{0:T(128)S(1)}, s32[4]{0:T(128)}, u32[]{:S(2)}) copy-start(s32[4]{0:T(128)} %constant.23.clone) | copy-start | bytes 52
  6.5 9.0 %copy-start.2 = (s32[2048]{0:T(1024)S(1)}, s32[2048]{0:T(1024)}, u32[]{:S(2)}) copy-start(s32[2048]{0:T(1024)} %param.15) | copy-start | bytes 24580
  6.5 9.1 %copy-start = (s32[2048]{0:T(1024)S(1)}, s32[2048]{0:T(1024)}, u32[]{:S(2)}) copy-start(s32[2048]{0:T(1024)} %param.14) | copy-start | bytes 24580
  6.5 62.7 %all-gather.3.cloned.1.call-start = ((), (), s32[]{:S(2)}) async-start(), calls=%async_computation.5 | async-start | bytes 8912896 | tf_op jit(solution)/shard_map/all_gather | solution.py:76
  7.3 169.3 %all-gather.5.cloned.1.call-start = ((), (), s32[]{:S(2)}) async-start(), calls=%async_computation.6 | async-start | bytes 8912896 | tf_op jit(solution)/shard_map/all_gather | solution.py:89
  10.6 29.7 %all-to-all-start = ((bf16[4,1,512,512]{3,2,1,0:T(8,128)(2,1)}), bf16[4,1,512,512]{3,2,1,0:T(8,128)(2,1)S(1)}, u32[]{:S(2)}, u32[]{:S(2)}) async-start(bf16[4,1,512,512]{3,2,1,0:T(8,128)(2,1)} %broadcast_in_dim.13), calls=%async_computation | async-start | bytes 4194304 | tf_op jit(solution)/shard_map/all_to_all | solution.py:9
  84.0 46.7 %copy-start.7 = (s32[128]{0:T(128)S(1)}, s32[128]{0:T(128)}, u32[]{:S(2)}) copy-start(s32[128]{0:T(128)} %param.20) | copy-start | bytes 1540
  84.0 46.7 %copy-start.3 = (s32[128]{0:T(128)S(1)}, s32[128]{0:T(128)}, u32[]{:S(2)}) copy-start(s32[128]{0:T(128)} %param.18) | copy-start | bytes 1540
  84.0 46.7 %copy-start.4 = (s32[128]{0:T(128)S(1)}, s32[128]{0:T(128)}, u32[]{:S(2)}) copy-start(s32[128]{0:T(128)} %param.17) | copy-start | bytes 1540
  84.0 46.7 %copy-start.5 = (s32[128]{0:T(128)S(1)}, s32[128]{0:T(128)}, u32[]{:S(2)}) copy-start(s32[128]{0:T(128)} %param.19) | copy-start | bytes 1540
  84.0 46.7 %copy-start.6 = (s32[128]{0:T(128)S(1)}, s32[128]{0:T(128)}, u32[]{:S(2)}) copy-start(s32[128]{0:T(128)} %param.16) | copy-start | bytes 1540
  126.1 39.6 %all-to-all-start.2 = ((bf16[16,16,1,2048]{3,1,2,0:T(8,128)(2,1)}), bf16[16,16,1,2048]{3,1,2,0:T(8,128)(2,1)}, u32[]{:S(2)}, u32[]{:S(2)}) async-start(bf16[16,16,1,2048]{3,1,2,0:T(8,128)(2,1)} %get-tuple-element.6), calls=%async_computation.2 | async-start | bytes 2097152 | tf_op jit(solution)/shard_map/all_to_all | solution.py:41
  130.4 106.4 %reduce-scatter.2.cloned.1.call-start = ((), (), s32[]{:S(2)}) async-start(), calls=%async_computation.7 | async-start | bytes 5242880 | tf_op jit(solution)/shard_map/reduce_scatter | solution.py:93
Sparse Core Ops, SparseCore 0:
  9.2 60.0 all-gather.2
  71.0 105.5 all-gather.4
  189.0 47.7 reduce-scatter.1
where the time goes:
time: 283 us; the launch traced here: 282 us
  waiting for transfers between devices  137 us (48%)
  blocking collectives  77 us (27%)
  local copies, waits for them, and re-layouts  23.2 us (8%)
  matrix products  20.9 us (7%)
  between operations  13.3 us (5%)
  starting transfers between devices  9.51 us (3%)
    reduce_scatter x1, waiting for transfers between devices, local(): summed = lax.psum_scatter(terms, 'bra', scatter_dimension=0, tiled=True)  47.9 us
    all_to_all x1, blocking collectives, exchange_in_pieces(): lax.all_to_all(section, axis, split_axis=0, concat_axis=0, tiled=True)  41 us
    all_to_all x1, blocking collectives, local(): lax.all_to_all(summed, 'chan', split_axis=1, concat_axis=2, tiled=True)  36 us
    all_to_all x1, waiting for transfers between devices, exchange_in_pieces(): lax.all_to_all(section, axis, split_axis=0, concat_axis=0, tiled=True)  33.7 us
    all_to_all x1, waiting for transfers between devices, from_everyone(): lax.all_to_all(jnp.broadcast_to(x[None], (peers, *x.shape)), axis, 0, 0,...  24.5 us
    all_gather x1, waiting for transfers between devices, local(): piece = lax.all_gather(ket_tensor, 'chan', axis=1, tiled=True)  22.8 us
    dot_general x1, matrix products, local(): jnp.einsum('tbp,qvtb->pvq', masked, mixed, preferred_element_type=jnp.flo...  12.2 us
    dot_general x1, matrix products, local(): jnp.einsum('wbk,skq->qwsb', full_env, masked, preferred_element_type=jnp....  8.39 us
  transfers between devices with their start and end apart: 5, of which 5 were waited for; matrix products, arithmetic and copies ran while one was open for 11% of the time, Pallas kernels for 0%

commit v1 on v0

v1 whole, which is shorter than its diff:
```python
import functools

import jax
import jax.numpy as jnp
from jax import lax
from jax.experimental import pallas as pl
from jax.experimental.pallas import tpu as pltpu
from jax.sharding import PartitionSpec as P

BF16 = jnp.bfloat16
PHYS = (0, 1, 1, 2)
PLANE = (0, 0, 1, 0)
CHUNKS = ((0, 256), (256, 256))


def two_planes(x, diff):
    first = jnp.where(diff == 0, x[0], jnp.where(diff == 1, x[1], x[3]))
    return jnp.stack([first, x[2]])


def spread_coupling(op_in, op_out, op_bra, op_ket, op_code):
    rows = jnp.arange(1024, dtype=jnp.int32)
    pick_out = (rows[:, None] // 16 == (op_out * 4 + op_bra)[None, :]).astype(BF16)
    weights = op_code.astype(jnp.float32) * 0.25
    hit = (op_ket * 16 + op_in)[:, None] == rows[None, :] // 16
    pick_in = jnp.where(hit, weights[:, None], 0.0).astype(BF16)
    table = jnp.dot(pick_out, pick_in, preferred_element_type=jnp.float32)
    same = rows[:, None] % 16 == rows[None, :] % 16
    return jnp.where(same, table, 0.0).astype(BF16)


def first_kernel(yb, e0, e1, e2, e3a, e3b, ket, left, right, spread, out, env, masked, parts):
    quarter = e0.shape[1]
    half = e3a.shape[0]
    env[:, 0:quarter] = e0[...]
    env[:, quarter : 2 * quarter] = e1[...]
    env[:, 2 * quarter : 3 * quarter] = e2[...]
    env[0:half, 3 * quarter :] = e3a[...]
    env[half:, 3 * quarter :] = e3b[...]
    cols = right[...]
    for s in range(4):
        for i in range(4):
            block = yb[i] * 4
            for r in range(4):
                rows = left[pl.ds(pl.multiple_of((block + r) * 128, 128), 128), :]
                values = ket[block + r, PLANE[s]]
                allowed = rows + PHYS[s] == cols
                at = i * quarter + r * 128
                masked[at : at + 128, :] = jnp.where(allowed, values, jnp.zeros_like(values))
        product = jnp.dot(env[...], masked[...], preferred_element_type=jnp.float32)
        product = product.astype(BF16).reshape(16, 2, 16, product.shape[1])
        for h in range(2):
            parts[h, s * 256 : (s + 1) * 256, :] = product[:, h].reshape(256, -1)
    for h in range(2):
        mixed = jnp.dot(spread[...], parts[h], preferred_element_type=jnp.float32)
        out[:, h * 64 : (h + 1) * 64, :] = mixed.astype(BF16).reshape(16, 64, -1)


def second_kernel(got, bra, left, right, out, mixed, masked):
    for j in range(16):
        for h in range(2):
            for t in range(4):
                at = t * 512 + j * 32 + h * 16
                mixed[at : at + 16, :] = got[j, h * 64 + t * 16 : h * 64 + (t + 1) * 16, :]
    cols = left[...]

    def step(g, carry):
        for r in range(4):
            rows = right[pl.ds(pl.multiple_of((g * 4 + r) * 128, 128), 128), :]
            for t in range(4):
                values = bra[g * 4 + r, PLANE[t]]
                allowed = cols + PHYS[t] == rows
                masked[r * 128 : (r + 1) * 128, t * 512 : (t + 1) * 512] = jnp.where(
                    allowed, values, jnp.zeros_like(values)
                )
        total = jnp.dot(masked[...], mixed[...], preferred_element_type=jnp.float32)
        out[pl.ds(pl.multiple_of(g * 512, 512), 512), :] = total.astype(BF16)
        return carry

    lax.fori_loop(0, 4, step, 0)


def whole(shape):
    return pl.BlockSpec(shape, lambda i: (0,) * len(shape))


def first_stage(yb, pieces, ket, left, right, spread, start, width):
    column = start // width
    return pl.pallas_call(
        first_kernel,
        grid=(1,),
        out_shape=jax.ShapeDtypeStruct((16, 128, width), BF16),
        in_specs=[pl.BlockSpec(memory_space=pltpu.SMEM)]
        + [whole(p.shape) for p in pieces]
        + [
            pl.BlockSpec((16, 2, 128, width), lambda i: (0, 0, 0, column)),
            whole(left.shape),
            pl.BlockSpec((1, width), lambda i: (0, column)),
            whole(spread.shape),
        ],
        out_specs=whole((16, 128, width)),
        scratch_shapes=[
            pltpu.VMEM((512, 2048), BF16),
            pltpu.VMEM((2048, width), BF16),
            pltpu.VMEM((2, 1024, width), BF16),
        ],
        cost_estimate=pl.CostEstimate(
            flops=2 * 512 * 2048 * 4 * width, bytes_accessed=8 << 20, transcendentals=0
        ),
        name="first_stage",
    )(yb, *pieces, ket, left, right, spread)


def second_stage(got, bra, left, right):
    width = got.shape[2]
    return pl.pallas_call(
        second_kernel,
        grid=(1,),
        out_shape=jax.ShapeDtypeStruct((2048, width), BF16),
        in_specs=[whole(got.shape), whole(bra.shape), whole(left.shape), whole(right.shape)],
        out_specs=whole((2048, width)),
        scratch_shapes=[pltpu.VMEM((2048, width), BF16), pltpu.VMEM((512, 2048), BF16)],
        cost_estimate=pl.CostEstimate(
            flops=2 * 2048 * 2048 * width, bytes_accessed=7 << 20, transcendentals=0
        ),
        name="second_stage",
    )(got, bra, left, right)


def local(
    environment,
    ket_tensor,
    bra_tensor,
    charge_left,
    charge_right,
    op_in,
    op_out,
    op_bra,
    op_ket,
    op_code,
):
    chan, ket, bra = lax.axis_index("chan"), lax.axis_index("ket"), lax.axis_index("bra")
    right_cols = lax.dynamic_slice_in_dim(charge_right, ket * 512, 512)
    left_rows = lax.dynamic_slice_in_dim(charge_left, chan * 128, 128)
    ket_planes = two_planes(ket_tensor, right_cols[None, :] - left_rows[:, None])
    ket_all = lax.all_gather(ket_planes, "chan", axis=0)

    env = lax.all_to_all(environment.reshape(16, 32, 512), "chan", 0, 0, tiled=True)
    env = env.reshape(512, 512)
    up = [(i, (i + 1) % 4) for i in range(4)]
    down = [(i, (i + 3) % 4) for i in range(4)]
    env_below = lax.ppermute(env, "ket", up)
    env_above = lax.ppermute(env, "ket", down)
    far_a = lax.ppermute(env_below[:256], "ket", up)
    far_b = lax.ppermute(env_above[256:], "ket", down)
    yb = (ket + jnp.array([0, 3, 1, 2], jnp.int32)) % 4

    left_bra = lax.dynamic_slice_in_dim(charge_left, bra * 512, 512)
    right_bra = lax.dynamic_slice_in_dim(charge_right, chan * 128, 128)
    bra_planes = two_planes(bra_tensor, right_bra[None, :] - left_bra[:, None])
    bra_all = lax.all_gather(jnp.swapaxes(bra_planes, 1, 2), "chan", axis=0)

    spread = spread_coupling(op_in, op_out, op_bra, op_ket, op_code)
    left_column = charge_left.astype(BF16)[:, None]
    right_column = charge_right.astype(BF16)[:, None]
    left_row = left_bra.astype(BF16)[None, :]
    right_row = right_cols.astype(BF16)[None, :]

    pieces = (env, env_below, env_above, far_a, far_b)
    outs = []
    for start, width in CHUNKS:
        mixed = first_stage(yb, pieces, ket_all, left_column, right_row, spread, start, width)
        got = lax.all_to_all(mixed, "chan", 0, 0, tiled=True)
        terms = second_stage(got, bra_all, left_row, right_column)
        outs.append(lax.psum_scatter(terms, "bra", scatter_dimension=0, tiled=True))
    return jnp.concatenate(outs, axis=1).astype(jnp.float32)[None]


def solution(mesh):
    placed = (
        P("chan", "bra", "ket"),
        P(None, "chan", "ket"),
        P(None, "bra", "chan"),
        P(),
        P(),
        P(),
        P(),
        P(),
        P(),
        P(),
    )
    return jax.shard_map(
        local, mesh=mesh, in_specs=placed, out_specs=P("chan", "bra", "ket"), check_vma=False
    )
```

time: 283 us -> 197 us (0.70)
  blocking collectives: 77 us -> 0 us
  Pallas kernels: 0 us -> 28.8 us
  waiting for transfers between devices: 137 us -> 110 us
  matrix products: 20.9 us -> 2.36 us
  starting transfers between devices: 9.51 us -> 25.7 us
  local copies, waits for them, and re-layouts: 23.2 us -> 8.23 us
  other arithmetic: 1.56 us -> 7.06 us
    all_to_all x2 -> x0, blocking collectives: 77 us -> none  [the longest x1 41 us: exchange_in_pieces(): lax.all_to_all(section, axis, split_axis=0, concat_axis=0, tiled=True)]
    all_gather x2, waiting for transfers between devices: 29.4 us -> 0.02 us  [the longest x1 0.02 us: local(): bra_all = lax.all_gather(jnp.swapaxes(bra_planes, 1, 2), 'chan', axis=0)]
    pallas_call x0 -> x4, Pallas kernels: none -> 28.8 us  [the longest x2 15.2 us: first_stage(): pl.pallas_call(first_kernel, grid=(1,), out_shape=jax.ShapeDtypeStruct((1...]
    reduce_scatter x1 -> x2, waiting for transfers between devices: 47.9 us -> 23.1 us  [local(): outs.append(lax.psum_scatter(terms, 'bra', scatter_dimension=0, tiled=True))]
    dot_general x3 -> x1, matrix products: 20.9 us -> 2.36 us  [spread_coupling(): table = jnp.dot(pick_out, pick_in, preferred_element_type=jnp.float32)]
    ppermute x0 -> x4, waiting for transfers between devices: none -> 17.6 us  [the longest x1 11.1 us: local(): env_above = lax.ppermute(env, 'ket', down)]
    all_to_all x2 -> x3, waiting for transfers between devices: 58.2 us -> 69.2 us  [the longest x2 49.2 us: local(): got = lax.all_to_all(mixed, 'chan', 0, 0, tiled=True)]
    all_to_all x2 -> x3, starting transfers between devices: 9.25 us -> 19.2 us  [the longest x1 9.98 us: local(): lax.all_to_all(environment.reshape(16, 32, 512), 'chan', 0, 0, tiled=True)]
  transfers between devices with their start and end apart: 5 -> 11, of which waited for: 5 -> 7; matrix products, arithmetic and copies ran while one was open for 11% -> 5% of each run, Pallas kernels for 0% -> 15%
where the time goes in v1:
time: 197 us; the launch traced here: 196 us
  waiting for transfers between devices  110 us (56%)
  Pallas kernels  28.8 us (15%)
  starting transfers between devices  25.7 us (13%)
  between operations  13.4 us (7%)
  local copies, waits for them, and re-layouts  8.23 us (4%)
  other arithmetic  7.06 us (4%)
  matrix products  2.36 us (1%)
    all_to_all x2, waiting for transfers between devices, local(): got = lax.all_to_all(mixed, 'chan', 0, 0, tiled=True)  49.2 us
    reduce_scatter x2, waiting for transfers between devices, local(): outs.append(lax.psum_scatter(terms, 'bra', scatter_dimension=0, tiled=True))  23.1 us
    all_to_all x1, waiting for transfers between devices, local(): lax.all_to_all(environment.reshape(16, 32, 512), 'chan', 0, 0, tiled=True)  20 us
    pallas_call x2, Pallas kernels, first_stage(): pl.pallas_call(first_kernel, grid=(1,), out_shape=jax.ShapeDtypeStruct((1...  15.2 us
    pallas_call x2, Pallas kernels, second_stage(): pl.pallas_call(second_kernel, grid=(1,), out_shape=jax.ShapeDtypeStruct((...  13.6 us
    ppermute x1, waiting for transfers between devices, local(): env_above = lax.ppermute(env, 'ket', down)  11.1 us
    all_to_all x1, starting transfers between devices, local(): lax.all_to_all(environment.reshape(16, 32, 512), 'chan', 0, 0, tiled=True)  9.98 us
    all_to_all x2, starting transfers between devices, local(): got = lax.all_to_all(mixed, 'chan', 0, 0, tiled=True)  9.19 us
  transfers between devices with their start and end apart: 11, of which 7 were waited for; matrix products, arithmetic and copies ran while one was open for 5% of the time, Pallas kernels for 15%

profile of v1, /device:TPU:1, one launch (start us, length us, event | category | flops | bytes accessed | tf_op | source)
XLA Modules:
  0.0 195.5 jit_solution(9396002604232988297)
XLA Ops:
  6.6 0.8 dynamic_slice.13
  7.4 0.8 fusion.19
  8.2 1.2 fusion.7
  9.4 0.7 pad_maximum_fusion
  10.3 0.8 dynamic_slice.14
  11.0 1.1 fusion.20
  12.6 0.8 fusion.18
  13.6 0.7 maximum_bitcast_fusion
  14.3 10.0 %all-to-all-start = ((bf16[16,32,512]{2,1,0:T(8,128)(2,1)}), bf16[16,32,512]{2,1,0:T(8,128)(2,1)S(1)}, u32[]{:S(2)}, u32[]{:S(2)}) async-start(bf16[16,32,512]{2,1,0:T(8,128)(2,1)} %bitcast), calls=%async_computation | async-start | bytes 1048576 | tf_op jit(solution)/shard_map/all_to_all | solution.py:148
  24.3 0.5 broadcast_in_dim.25.right
  24.9 1.1 broadcast_in_dim.47.left
  26.5 20.0 %all-to-all-done = bf16[16,32,512]{2,1,0:T(8,128)(2,1)S(1)} async-done(((bf16[16,32,512]{2,1,0:T(8,128)(2,1)}), bf16[16,32,512]{2,1,0:T(8,128)(2,1)S(1)}, u32[]{:S(2)}, u32[]{:S(2)}) %all-to-all-start) | async-done | bytes 524320 | tf_op jit(solution)/shard_map/all_to_all | solution.py:148
  46.5 2.7 %collective-permute-start.1 = (bf16[512,512]{1,0:T(8,128)(2,1)S(1)}, bf16[512,512]{1,0:T(8,128)(2,1)S(1)}, u32[]{:S(2)}, u32[]{:S(2)}) collective-permute-start(bf16[512,512]{1,0:T(8,128)(2,1)S(1)} %bitcast.10), channel_id=1, source_target_pairs={{0,12},{4,0},{8,4},{12,8},{1,13},{5,1},{9,5},{13,9},{2,14},{6,2},{... | collective-permute-start | bytes 1572872 | tf_op jit(solution)/shard_map/ppermute | solution.py:153
  49.3 11.1 %collective-permute-done.1.e2 = bf16[512,512]{1,0:T(8,128)(2,1)S(1)} collective-permute-done((bf16[512,512]{1,0:T(8,128)(2,1)S(1)}, bf16[512,512]{1,0:T(8,128)(2,1)S(1)}, u32[]{:S(2)}, u32[]{:S(2)}) %collective-permute-start.1) | collective-permute-done | bytes 524320 | tf_op jit(solution)/shard_map/ppermute | solution.py:153
  60.4 3.6 %collective-permute-start.3 = (bf16[256,512]{1,0:T(8,128)(2,1)S(1)}, bf16[256,512]{1,0:T(8,128)(2,1)S(1)}, u32[]{:S(2)}, u32[]{:S(2)}) collective-permute-start(bf16[256,512]{1,0:T(8,128)(2,1)S(1)} %slice.41), channel_id=1, source_target_pairs={{0,12},{4,0},{8,4},{12,8},{1,13},{5,1},{9,5},{13,9},{2,14},{6,2},{... | collective-permute-start | bytes 786440 | tf_op jit(solution)/shard_map/ppermute | solution.py:155
  64.1 2.4 %select_convert_fusion.spread = bf16[1024,1024]{1,0:T(8,128)(2,1)} fusion(s32[1024]{0:T(1024)S(1)} %get-tuple-element.16, bf16[128]{0:T(256)(128)(2,1)S(1)} %convert_multiply_fusion, s32[1024]{0:T(1024)S(1)} %get-tuple-element.15, s32[128]{0:T(128)S(1)} %get-tuple-element.18, s32[128]{0:T(128)S(1)} %get-tuple-element.17), kind=kOutput, calls=%fused_computation | convolution fusion | flops 271974400 | bytes 2106624 | tf_op jit(solution)/shard_map/dot_general | solution.py:27
  66.5 3.4 %collective-permute-done.3.e3b = bf16[256,512]{1,0:T(8,128)(2,1)S(1)} collective-permute-done((bf16[256,512]{1,0:T(8,128)(2,1)S(1)}, bf16[256,512]{1,0:T(8,128)(2,1)S(1)}, u32[]{:S(2)}, u32[]{:S(2)}) %collective-permute-start.3) | collective-permute-done | bytes 262176 | tf_op jit(solution)/shard_map/ppermute | solution.py:155
  69.9 3.1 %collective-permute-done.2.e3a = bf16[256,512]{1,0:T(8,128)(2,1)S(1)} collective-permute-done((bf16[256,512]{1,0:T(8,128)(2,1)S(1)}, bf16[256,512]{1,0:T(8,128)(2,1)S(1)}, u32[]{:S(2)}, u32[]{:S(2)}) %collective-permute-start.2) | collective-permute-done | bytes 262176 | tf_op jit(solution)/shard_map/ppermute | solution.py:154
  73.0 0.7 copy-done.4
  73.7 7.6 %first_stage.2 = bf16[16,128,256]{2,1,0:T(8,128)(2,1)} custom-call(s32[4]{0:T(128)} %and_select_fusion.yb, bf16[512,512]{1,0:T(8,128)(2,1)} %bitcast.12, bf16[512,512]{1,0:T(8,128)(2,1)} %copy-done.2, bf16[512,512]{1,0:T(8,128)(2,1)} %copy-done.1, bf16[256,512]{1,0:T(8,128)(2,1)} %copy-done.4, bf16[256,512]{1,0:T(8,128)(2,1)} %copy-done.3, ...), custom_call_target="tpu_custom_call" | custom-call | flops 2147483648 | bytes 8388608 | tf_op jit(solution)/shard_map/first_stage/pallas_call | solution.py:89
  81.3 4.8 %all-to-all-start.1 = ((bf16[16,128,256]{2,1,0:T(8,128)(2,1)}), bf16[16,128,256]{2,1,0:T(8,128)(2,1)S(1)}, u32[]{:S(2)}, u32[]{:S(2)}) async-start(bf16[16,128,256]{2,1,0:T(8,128)(2,1)} %first_stage.2), calls=%async_computation.1 | async-start | bytes 2097152 | tf_op jit(solution)/shard_map/all_to_all | solution.py:173
  86.1 0.5 broadcast_in_dim.45.left
  86.6 1.1 broadcast_in_dim.48.right
  87.8 7.7 %first_stage.3 = bf16[16,128,256]{2,1,0:T(8,128)(2,1)} custom-call(s32[4]{0:T(128)} %and_select_fusion.yb, bf16[512,512]{1,0:T(8,128)(2,1)} %bitcast.13, bf16[512,512]{1,0:T(8,128)(2,1)} %copy-done.2, bf16[512,512]{1,0:T(8,128)(2,1)} %copy-done.1, bf16[256,512]{1,0:T(8,128)(2,1)} %copy-done.4, bf16[256,512]{1,0:T(8,128)(2,1)} %copy-done.3, ...), custom_call_target="tpu_custom_call" | custom-call | flops 2147483648 | bytes 8388608 | tf_op jit(solution)/shard_map/first_stage/pallas_call | solution.py:89
  95.4 28.1 %all-to-all-done.1.got = bf16[16,128,256]{2,1,0:T(8,128)(2,1)S(1)} async-done(((bf16[16,128,256]{2,1,0:T(8,128)(2,1)}), bf16[16,128,256]{2,1,0:T(8,128)(2,1)S(1)}, u32[]{:S(2)}, u32[]{:S(2)}) %all-to-all-start.1) | async-done | bytes 1048608 | tf_op jit(solution)/shard_map/all_to_all | solution.py:173
  123.6 4.4 %all-to-all-start.2 = ((bf16[16,128,256]{2,1,0:T(8,128)(2,1)}), bf16[16,128,256]{2,1,0:T(8,128)(2,1)S(1)}, u32[]{:S(2)}, u32[]{:S(2)}) async-start(bf16[16,128,256]{2,1,0:T(8,128)(2,1)} %first_stage.3), calls=%async_computation.3 | async-start | bytes 2097152 | tf_op jit(solution)/shard_map/all_to_all | solution.py:173
  128.0 6.8 %second_stage.2 = bf16[2048,256]{1,0:T(8,128)(2,1)} custom-call(bf16[16,128,256]{2,1,0:T(8,128)(2,1)} %copy-done.5, bf16[16,2,128,512]{3,2,1,0:T(8,128)(2,1)} %bitcast.16, bf16[1,512]{1,0:T(2,128)(2,1)} %broadcast_in_dim.45.left, bf16[2048,1]{1,0:T(8,128)(2,1)} %broadcast_in_dim.48.right), custom_call_target="tpu_custom_call" | custom-call | flops 2147483648 | bytes 7340032 | tf_op jit(solution)/shard_map/second_stage/pallas_call | solution.py:116
  134.9 21.1 %all-to-all-done.2.got = bf16[16,128,256]{2,1,0:T(8,128)(2,1)S(1)} async-done(((bf16[16,128,256]{2,1,0:T(8,128)(2,1)}), bf16[16,128,256]{2,1,0:T(8,128)(2,1)S(1)}, u32[]{:S(2)}, u32[]{:S(2)}) %all-to-all-start.2) | async-done | bytes 1048608 | tf_op jit(solution)/shard_map/all_to_all | solution.py:173
  155.9 1.0 copy-done.6
  156.9 6.8 %second_stage.3 = bf16[2048,256]{1,0:T(8,128)(2,1)} custom-call(bf16[16,128,256]{2,1,0:T(8,128)(2,1)} %copy-done.6, bf16[16,2,128,512]{3,2,1,0:T(8,128)(2,1)} %bitcast.17, bf16[1,512]{1,0:T(2,128)(2,1)} %broadcast_in_dim.45.left, bf16[2048,1]{1,0:T(8,128)(2,1)} %broadcast_in_dim.48.right), custom_call_target="tpu_custom_call" | custom-call | flops 2147483648 | bytes 7340032 | tf_op jit(solution)/shard_map/second_stage/pallas_call | solution.py:116
  163.8 23.1 %reduce-scatter.5.cloned.1.call-done = bf16[512,256]{1,0:T(8,128)(2,1)} async-done(((bf16[2048,256]{1,0:T(8,128)(2,1)}), bf16[512,256]{1,0:T(8,128)(2,1)}) %reduce-scatter.5.cloned.1.call-update) | async-done | bytes 262160 | tf_op jit(solution)/shard_map/reduce_scatter | solution.py:175
  186.9 2.1 %maximum_convert_fusion = f32[1,512,512]{2,1,0:T(8,128)} fusion(bf16[1,512,256]{2,1,0:T(8,128)(2,1)} %bitcast.15, bf16[1,512,256]{2,1,0:T(8,128)(2,1)} %bitcast.14), kind=kLoop, calls=%fused_computation.1 | loop fusion | flops 1048576 | bytes 1572864 | tf_op jit(solution)/shard_map/convert_element_type | solution.py:176
  (55 shorter events, 1.6 us)
Async XLA Ops:
  6.5 19.5 %copy-start.14 = (s32[4]{0:T(128)S(1)}, s32[4]{0:T(128)}, u32[]{:S(2)}) copy-start(s32[4]{0:T(128)} %constant.95.clone) | copy-start | bytes 52
  6.5 17.8 %copy-start.7 = (s32[2048]{0:T(1024)S(1)}, s32[2048]{0:T(1024)}, u32[]{:S(2)}) copy-start(s32[2048]{0:T(1024)} %param.14) | copy-start | bytes 24580
  6.5 42.7 %copy-start.13 = (s32[128]{0:T(128)S(1)}, s32[128]{0:T(128)}, u32[]{:S(2)}) copy-start(s32[128]{0:T(128)} %param.20) | copy-start | bytes 1540
  6.5 42.7 %copy-start.10 = (s32[128]{0:T(128)S(1)}, s32[128]{0:T(128)}, u32[]{:S(2)}) copy-start(s32[128]{0:T(128)} %param.19) | copy-start | bytes 1540
  6.5 42.7 %copy-start.11 = (s32[128]{0:T(128)S(1)}, s32[128]{0:T(128)}, u32[]{:S(2)}) copy-start(s32[128]{0:T(128)} %param.18) | copy-start | bytes 1540
  6.5 42.7 %copy-start.12 = (s32[128]{0:T(128)S(1)}, s32[128]{0:T(128)}, u32[]{:S(2)}) copy-start(s32[128]{0:T(128)} %param.17) | copy-start | bytes 1540
  6.6 42.7 %copy-start.9 = (s32[128]{0:T(128)S(1)}, s32[128]{0:T(128)}, u32[]{:S(2)}) copy-start(s32[128]{0:T(128)} %param.16) | copy-start | bytes 1540
  6.6 66.4 %all-gather.5.cloned.1.call-start = ((), (), s32[]{:S(2)}) async-start(), calls=%async_computation.7 | async-start | bytes 4456448 | tf_op jit(solution)/shard_map/all_gather | solution.py:146
  10.2 117.8 %all-gather.7.cloned.1.call-start = ((), (), s32[]{:S(2)}) async-start(), calls=%async_computation.8 | async-start | bytes 4456448 | tf_op jit(solution)/shard_map/all_gather | solution.py:161
  14.3 32.2 %all-to-all-start = ((bf16[16,32,512]{2,1,0:T(8,128)(2,1)}), bf16[16,32,512]{2,1,0:T(8,128)(2,1)S(1)}, u32[]{:S(2)}, u32[]{:S(2)}) async-start(bf16[16,32,512]{2,1,0:T(8,128)(2,1)} %bitcast), calls=%async_computation | async-start | bytes 1048576 | tf_op jit(solution)/shard_map/all_to_all | solution.py:148
  46.5 26.5 %copy-start = (bf16[16,32,512]{2,1,0:T(8,128)(2,1)}, bf16[16,32,512]{2,1,0:T(8,128)(2,1)S(1)}, u32[]{:S(2)}) copy-start(bf16[16,32,512]{2,1,0:T(8,128)(2,1)S(1)} %all-to-all-done) | copy-start | bytes 1572868
  46.5 13.9 %collective-permute-start.1 = (bf16[512,512]{1,0:T(8,128)(2,1)S(1)}, bf16[512,512]{1,0:T(8,128)(2,1)S(1)}, u32[]{:S(2)}, u32[]{:S(2)}) collective-permute-start(bf16[512,512]{1,0:T(8,128)(2,1)S(1)} %bitcast.10), channel_id=1, source_target_pairs={{0,12},{4,0},{8,4},{12,8},{1,13},{5,1},{9,5},{13,9},{2,14},{6,2},{... | collective-permute-start | bytes 1572872 | tf_op jit(solution)/shard_map/ppermute | solution.py:153
  49.2 14.8 %collective-permute-start = (bf16[512,512]{1,0:T(8,128)(2,1)S(1)}, bf16[512,512]{1,0:T(8,128)(2,1)S(1)}, u32[]{:S(2)}, u32[]{:S(2)}) collective-permute-start(bf16[512,512]{1,0:T(8,128)(2,1)S(1)} %bitcast.11), channel_id=1, source_target_pairs={{0,4},{4,8},{8,12},{12,0},{1,5},{5,9},{9,13},{13,1},{2,6},{6,10},{... | collective-permute-start | bytes 1572872 | tf_op jit(solution)/shard_map/ppermute | solution.py:152
  60.4 12.6 %copy-start.1 = (bf16[512,512]{1,0:T(8,128)(2,1)}, bf16[512,512]{1,0:T(8,128)(2,1)S(1)}, u32[]{:S(2)}) copy-start(bf16[512,512]{1,0:T(8,128)(2,1)S(1)} %collective-permute-done.1.e2) | copy-start | bytes 1572868
  60.4 9.5 %collective-permute-start.3 = (bf16[256,512]{1,0:T(8,128)(2,1)S(1)}, bf16[256,512]{1,0:T(8,128)(2,1)S(1)}, u32[]{:S(2)}, u32[]{:S(2)}) collective-permute-start(bf16[256,512]{1,0:T(8,128)(2,1)S(1)} %slice.41), channel_id=1, source_target_pairs={{0,12},{4,0},{8,4},{12,8},{1,13},{5,1},{9,5},{13,9},{2,14},{6,2},{... | collective-permute-start | bytes 786440 | tf_op jit(solution)/shard_map/ppermute | solution.py:155
  64.0 9.0 %copy-start.2 = (bf16[512,512]{1,0:T(8,128)(2,1)}, bf16[512,512]{1,0:T(8,128)(2,1)S(1)}, u32[]{:S(2)}) copy-start(bf16[512,512]{1,0:T(8,128)(2,1)S(1)} %collective-permute-done.e1) | copy-start | bytes 1572868
  64.0 8.9 %collective-permute-start.2 = (bf16[256,512]{1,0:T(8,128)(2,1)S(1)}, bf16[256,512]{1,0:T(8,128)(2,1)S(1)}, u32[]{:S(2)}, u32[]{:S(2)}) collective-permute-start(bf16[256,512]{1,0:T(8,128)(2,1)S(1)} %slice.40), channel_id=1, source_target_pairs={{0,4},{4,8},{8,12},{12,0},{1,5},{5,9},{9,13},{13,1},{2,6},{6,10},{... | collective-permute-start | bytes 786440 | tf_op jit(solution)/shard_map/ppermute | solution.py:154
  69.9 3.1 %copy-start.3 = (bf16[256,512]{1,0:T(8,128)(2,1)}, bf16[256,512]{1,0:T(8,128)(2,1)S(1)}, u32[]{:S(2)}) copy-start(bf16[256,512]{1,0:T(8,128)(2,1)S(1)} %collective-permute-done.3.e3b) | copy-start | bytes 786436
  73.0 0.7 copy-start.4
  73.7 12.4 %copy-start.8 = (s32[2048]{0:T(1024)S(1)}, s32[2048]{0:T(1024)}, u32[]{:S(2)}) copy-start(s32[2048]{0:T(1024)} %param.15) | copy-start | bytes 24580
  81.3 42.3 %all-to-all-start.1 = ((bf16[16,128,256]{2,1,0:T(8,128)(2,1)}), bf16[16,128,256]{2,1,0:T(8,128)(2,1)S(1)}, u32[]{:S(2)}, u32[]{:S(2)}) async-start(bf16[16,128,256]{2,1,0:T(8,128)(2,1)} %first_stage.2), calls=%async_computation.1 | async-start | bytes 2097152 | tf_op jit(solution)/shard_map/all_to_all | solution.py:173
  123.6 4.5 %copy-start.5 = (bf16[16,128,256]{2,1,0:T(8,128)(2,1)}, bf16[16,128,256]{2,1,0:T(8,128)(2,1)S(1)}, u32[]{:S(2)}) copy-start(bf16[16,128,256]{2,1,0:T(8,128)(2,1)S(1)} %all-to-all-done.1.got) | copy-start | bytes 3145732
  123.6 32.4 %all-to-all-start.2 = ((bf16[16,128,256]{2,1,0:T(8,128)(2,1)}), bf16[16,128,256]{2,1,0:T(8,128)(2,1)S(1)}, u32[]{:S(2)}, u32[]{:S(2)}) async-start(bf16[16,128,256]{2,1,0:T(8,128)(2,1)} %first_stage.3), calls=%async_computation.3 | async-start | bytes 2097152 | tf_op jit(solution)/shard_map/all_to_all | solution.py:173
  127.9 35.8 %reduce-scatter.3.cloned.1.call-start = ((), (), s32[]{:S(2)}) async-start(), calls=%async_computation.5 | async-start | bytes 1310720 | tf_op jit(solution)/shard_map/reduce_scatter | solution.py:175
  134.8 52.0 %reduce-scatter.5.cloned.1.call-start = ((), (), s32[]{:S(2)}) async-start(), calls=%async_computation.6 | async-start | bytes 1310720 | tf_op jit(solution)/shard_map/reduce_scatter | solution.py:175
  155.9 1.0 copy-start.6
Sparse Core Ops, SparseCore 0:
  10.3 55.7 all-gather.4
  67.9 59.9 all-gather.6
  134.9 23.3 reduce-scatter.2
  163.8 22.9 reduce-scatter.4

commit v2 on v1

v2 whole, which is shorter than its diff:
```python
import functools

import jax
import jax.numpy as jnp
from jax import lax
from jax.experimental import pallas as pl
from jax.experimental.pallas import tpu as pltpu
from jax.sharding import PartitionSpec as P

BF16 = jnp.bfloat16
F32 = jnp.float32
PHYS = (0, 1, 1, 2)
PLANE = (0, 0, 1, 0)
WIDTH = 256


def spread_coupling(op_in, op_out, op_bra, op_ket, op_code):
    rows = jnp.arange(1024, dtype=jnp.int32)
    pick_out = (rows[:, None] // 16 == (op_out * 4 + op_bra)[None, :]).astype(BF16)
    weights = op_code.astype(F32) * 0.25
    hit = (op_ket * 16 + op_in)[:, None] == rows[None, :] // 16
    pick_in = jnp.where(hit, weights[:, None], 0.0).astype(BF16)
    table = jnp.dot(pick_out, pick_in, preferred_element_type=F32)
    same = rows[:, None] % 16 == rows[None, :] % 16
    return jnp.where(same, table, 0.0).astype(BF16)


def charge_row(charges, block):
    return charges[pl.ds(block, 1), :].astype(F32)


def charge_column(charges, block):
    return jnp.transpose(jnp.broadcast_to(charge_row(charges, block), (128, 128)))


def chosen(x, diff):
    diff = diff.astype(BF16)
    return jnp.where(diff == 0, x[0], jnp.where(diff == 1, x[1], x[3]))


def pack_kernel(ket, bra, left, right, out):
    chan, y, x = lax.axis_index("chan"), lax.axis_index("ket"), lax.axis_index("bra")
    rows = charge_column(left, chan)
    for r in range(4):
        cut = slice(r * 128, (r + 1) * 128)
        diff = charge_row(right, y * 4 + r) - rows
        out[0, :, cut] = chosen([ket[s, :, cut] for s in range(4)], diff)
    out[1] = ket[2]
    cols = charge_row(right, chan)
    for r in range(4):
        cut = slice(r * 128, (r + 1) * 128)
        diff = cols - charge_column(left, x * 4 + r)
        first = chosen([bra[t, cut, :] for t in range(4)], diff)
        out[2, :, cut] = jnp.transpose(first.astype(F32)).astype(BF16)
        out[3, :, cut] = jnp.transpose(bra[2, cut, :].astype(F32)).astype(BF16)


def masked_tiles(values, rows, cols, charge):
    tiles = []
    for r, col in enumerate(cols):
        part = values[:, r * 128 : (r + 1) * 128]
        tiles.append(jnp.where(rows + charge == col, part, jnp.zeros_like(part)))
    return jnp.concatenate(tiles, axis=1)


def first_kernel(
    start, left_s, right_s, e0, e1, e2, e3a, e3b, planes, left, right, spread, out, env, column, acc, parts
):
    y = lax.axis_index("ket")
    width = acc.shape[1]
    for i, e in enumerate((e0, e1, e2)):
        block = lax.rem(y + (0, 3, 1)[i], 4)
        for h in range(2):
            env[2 * block + h] = e[:, h * 256 : (h + 1) * 256]
    block = lax.rem(y + 2, 4)
    for h in range(2):
        env[2 * block + h, 0:256] = e3a[:, h * 256 : (h + 1) * 256]
        env[2 * block + h, 256:512] = e3b[:, h * 256 : (h + 1) * 256]
    for c in range(16):
        column[c * 128 : (c + 1) * 128, :] = charge_column(left, c).astype(BF16)
    at = y * 4 + start // 128
    cols = [charge_row(right, at + r).astype(BF16) for r in range(width // 128)]
    least, most = right_s[y * 512 + start], right_s[y * 512 + start + width - 1]
    for s in range(4):
        acc[...] = jnp.zeros_like(acc)
        low = sum((left_s[256 * i + 255] + PHYS[s] < least).astype(jnp.int32) for i in range(8))
        high = sum((left_s[256 * i] + PHYS[s] <= most).astype(jnp.int32) for i in range(8))

        def step(i, carry):
            tiles = []
            for r in range(2):
                rows = column[pl.ds(pl.multiple_of(i * 256 + r * 128, 128), 128), :]
                values = planes[2 * i + r, PLANE[s]]
                tiles.append(masked_tiles(values, rows, cols, PHYS[s]))
            block = jnp.concatenate(tiles, axis=0)
            acc[...] += jnp.dot(env[i], block, preferred_element_type=F32)
            return carry

        lax.fori_loop(low, high, step, 0)
        product = acc[...].astype(BF16).reshape(16, 2, 16, width)
        for h in range(2):
            parts[h, s * 256 : (s + 1) * 256, :] = product[:, h].reshape(256, width)
    for h in range(2):
        mixed = jnp.dot(spread[...], parts[h], preferred_element_type=F32)
        out[:, h * 64 : (h + 1) * 64, :] = mixed.astype(BF16).reshape(16, 64, width)


def second_kernel(left_s, right_s, got, planes, left, right, out, mixed, column, acc):
    x = lax.axis_index("bra")
    for j in range(16):
        for h in range(2):
            for t in range(4):
                at = (j % 8) * 32 + h * 16
                mixed[t * 2 + j // 8, at : at + 16, :] = got[j, h * 64 + t * 16 : h * 64 + (t + 1) * 16, :]
    for c in range(16):
        column[c * 128 : (c + 1) * 128, :] = charge_column(right, c).astype(BF16)
    cols = [charge_row(left, x * 4 + r).astype(BF16) for r in range(4)]

    def step(g, carry):
        acc[...] = jnp.zeros_like(acc)
        least, most = right_s[g * 512], right_s[g * 512 + 511]
        for t in range(4):
            for h in range(2):
                first = left_s[x * 512 + h * 256] + PHYS[t]
                last = left_s[x * 512 + h * 256 + 255] + PHYS[t]

                @pl.when((first <= most) & (last >= least))
                def _():
                    tiles = []
                    for r in range(4):
                        rows = column[pl.ds(pl.multiple_of(g * 512 + r * 128, 128), 128), :]
                        values = planes[g * 4 + r, PLANE[t], :, h * 256 : (h + 1) * 256]
                        tiles.append(masked_tiles(values, rows, cols[2 * h : 2 * h + 2], -PHYS[t]))
                    block = jnp.concatenate(tiles, axis=0)
                    acc[...] += jnp.dot(block, mixed[t * 2 + h], preferred_element_type=F32)

        out[pl.ds(pl.multiple_of(g * 512, 512), 512), :] = acc[...].astype(BF16)
        return carry

    lax.fori_loop(0, 4, step, 0)


def whole(x):
    return pl.BlockSpec(x.shape, lambda i: (0,) * len(x.shape))


SCALARS = pl.BlockSpec(memory_space=pltpu.SMEM)


def pack(ket_tensor, bra_tensor, left, right):
    return pl.pallas_call(
        pack_kernel,
        grid=(1,),
        out_shape=jax.ShapeDtypeStruct((4, 128, 512), BF16),
        in_specs=[whole(ket_tensor), whole(bra_tensor), whole(left), whole(right)],
        out_specs=pl.BlockSpec((4, 128, 512), lambda i: (0, 0, 0)),
        name="pack",
    )(ket_tensor, bra_tensor, left, right)


def first_stage(charge_left, charge_right, pieces, gathered, left, right, spread, start):
    column = start // WIDTH
    return pl.pallas_call(
        functools.partial(first_kernel, start),
        grid=(1,),
        out_shape=jax.ShapeDtypeStruct((16, 128, WIDTH), BF16),
        in_specs=[SCALARS, SCALARS]
        + [whole(p) for p in pieces]
        + [
            pl.BlockSpec((16, 2, 128, WIDTH), lambda i: (0, 0, 0, column)),
            whole(left),
            whole(right),
            whole(spread),
        ],
        out_specs=pl.BlockSpec((16, 128, WIDTH), lambda i: (0, 0, 0)),
        scratch_shapes=[
            pltpu.VMEM((8, 512, 256), BF16),
            pltpu.VMEM((2048, 128), BF16),
            pltpu.VMEM((512, WIDTH), F32),
            pltpu.VMEM((2, 1024, WIDTH), BF16),
        ],
        cost_estimate=pl.CostEstimate(
            flops=512 * 2048 * 4 * WIDTH, bytes_accessed=8 << 20, transcendentals=0
        ),
        name="first_stage",
    )(charge_left, charge_right, *pieces, gathered, left, right, spread)


def second_stage(charge_left, charge_right, got, gathered, left, right):
    return pl.pallas_call(
        second_kernel,
        grid=(1,),
        out_shape=jax.ShapeDtypeStruct((2048, WIDTH), BF16),
        in_specs=[
            SCALARS,
            SCALARS,
            whole(got),
            pl.BlockSpec((16, 2, 128, 512), lambda i: (0, 1, 0, 0)),
            whole(left),
            whole(right),
        ],
        out_specs=pl.BlockSpec((2048, WIDTH), lambda i: (0, 0)),
        scratch_shapes=[
            pltpu.VMEM((8, 256, WIDTH), BF16),
            pltpu.VMEM((2048, 128), BF16),
            pltpu.VMEM((512, WIDTH), F32),
        ],
        cost_estimate=pl.CostEstimate(
            flops=2048 * 2048 * WIDTH, bytes_accessed=7 << 20, transcendentals=0
        ),
        name="second_stage",
    )(charge_left, charge_right, got, gathered, left, right)


def local(
    environment,
    ket_tensor,
    bra_tensor,
    charge_left,
    charge_right,
    op_in,
    op_out,
    op_bra,
    op_ket,
    op_code,
):
    left, right = charge_left.reshape(16, 128), charge_right.reshape(16, 128)
    planes = pack(ket_tensor, bra_tensor, left, right)
    gathered = lax.all_gather(planes, "chan", axis=0)

    env = lax.all_to_all(environment.reshape(16, 32, 512), "chan", 0, 0, tiled=True)
    env = env.reshape(512, 512)
    up = [(i, (i + 1) % 4) for i in range(4)]
    down = [(i, (i + 3) % 4) for i in range(4)]
    env_below = lax.ppermute(env, "ket", up)
    env_above = lax.ppermute(env, "ket", down)
    far_a = lax.ppermute(env_below[:256], "ket", up)
    far_b = lax.ppermute(env_above[256:], "ket", down)
    pieces = (env, env_below, env_above, far_a, far_b)
    spread = spread_coupling(op_in, op_out, op_bra, op_ket, op_code)

    terms = []
    for start in (0, WIDTH):
        mixed = first_stage(charge_left, charge_right, pieces, gathered, left, right, spread, start)
        got = lax.all_to_all(mixed, "chan", 0, 0, tiled=True)
        terms.append(second_stage(charge_left, charge_right, got, gathered, left, right))
    one = lax.psum_scatter(terms[0], "bra", scatter_dimension=0, tiled=True).astype(F32)
    two = lax.all_to_all(terms[1].reshape(4, 512, WIDTH), "bra", 0, 0, tiled=True)
    two = jnp.sum(two.astype(F32), axis=0)
    return jnp.concatenate([one, two], axis=1)[None]


def solution(mesh):
    placed = (
        P("chan", "bra", "ket"),
        P(None, "chan", "ket"),
        P(None, "bra", "chan"),
        P(),
        P(),
        P(),
        P(),
        P(),
        P(),
        P(),
    )
    return jax.shard_map(
        local, mesh=mesh, in_specs=placed, out_specs=P("chan", "bra", "ket"), check_vma=False
    )
```

time: 197 us -> 186 us (0.944)
  blocking collectives: 0 us -> 47.9 us
  waiting for transfers between devices: 110 us -> 66 us
  starting transfers between devices: 25.7 us -> 15 us
  local copies, waits for them, and re-layouts: 8.23 us -> 1.03 us
  Pallas kernels: 28.8 us -> 34.2 us
  other arithmetic: 7.06 us -> 3.62 us
    all_to_all x0 -> x2, blocking collectives: none -> 47.9 us  [the longest x1 30 us: local(): lax.all_to_all(environment.reshape(16, 32, 512), 'chan', 0, 0, tiled=True)]
    reduce_scatter x2 -> x1, waiting for transfers between devices: 23.1 us -> 0.02 us  [local(): lax.psum_scatter(terms[0], 'bra', scatter_dimension=0, tiled=True)]
    all_to_all x1 -> x0, waiting for transfers between devices: 20 us -> none  [local(): lax.all_to_all(environment.reshape(16, 32, 512), 'chan', 0, 0, tiled=True)]
    all_gather x2 -> x1, waiting for transfers between devices: 0.02 us -> 10.3 us  [local(): gathered = lax.all_gather(planes, 'chan', axis=0)]
    all_to_all x1 -> x0, starting transfers between devices: 9.98 us -> none  [local(): lax.all_to_all(environment.reshape(16, 32, 512), 'chan', 0, 0, tiled=True)]
    all_to_all x2, waiting for transfers between devices: 49.2 us -> 39.9 us  [local(): got = lax.all_to_all(mixed, 'chan', 0, 0, tiled=True)]
    broadcast_in_dim x4 -> x0, local copies, waits for them, and re-layouts: 3.33 us -> none  [the longest x1 1.13 us: local(): right_column = charge_right.astype(BF16)[:, None]]
    pallas_call x2, Pallas kernels: 13.6 us -> 16.7 us  [second_stage(): pl.pallas_call(second_kernel, grid=(1,), out_shape=jax.ShapeDtypeStruct((...]
  transfers between devices with their start and end apart: 11 -> 8, of which waited for: 7 -> 7; matrix products, arithmetic and copies ran while one was open for 5% -> 2% of each run, Pallas kernels for 15% -> 13%
where the time goes in v2:
time: 186 us; the launch traced here: 184 us
  waiting for transfers between devices  66 us (35%)
  blocking collectives  47.9 us (26%)
  Pallas kernels  34.2 us (18%)
  starting transfers between devices  15 us (8%)
  between operations  13.5 us (7%)
  other arithmetic  3.62 us (2%)
  matrix products  2.35 us (1%)
    all_to_all x2, waiting for transfers between devices, local(): got = lax.all_to_all(mixed, 'chan', 0, 0, tiled=True)  39.9 us
    all_to_all x1, blocking collectives, local(): lax.all_to_all(environment.reshape(16, 32, 512), 'chan', 0, 0, tiled=True)  30 us
    all_to_all x1, blocking collectives, local(): lax.all_to_all(terms[1].reshape(4, 512, WIDTH), 'bra', 0, 0, tiled=True)  17.9 us
    pallas_call x2, Pallas kernels, second_stage(): pl.pallas_call(second_kernel, grid=(1,), out_shape=jax.ShapeDtypeStruct((...  16.7 us
    pallas_call x2, Pallas kernels, first_stage(): pl.pallas_call(functools.partial(first_kernel, start), grid=(1,), out_sha...  15.2 us
    all_gather x1, waiting for transfers between devices, local(): gathered = lax.all_gather(planes, 'chan', axis=0)  10.3 us
    ppermute x1, waiting for transfers between devices, local(): env_above = lax.ppermute(env, 'ket', down)  8.81 us
    all_to_all x2, starting transfers between devices, local(): got = lax.all_to_all(mixed, 'chan', 0, 0, tiled=True)  8.37 us
  transfers between devices with their start and end apart: 8, of which 7 were waited for; matrix products, arithmetic and copies ran while one was open for 2% of the time, Pallas kernels for 13%

profile of v2, /device:TPU:1, one launch (start us, length us, event | category | flops | bytes accessed | tf_op | source)
XLA Modules:
  0.0 183.5 jit_solution(5574753430467579016)
XLA Ops:
  6.5 0.0 all-gather.3.cloned.1.call-start
  6.5 2.3 %pack.1 = bf16[4,128,512]{2,1,0:T(8,128)(2,1)} custom-call(bf16[4,128,512]{2,1,0:T(8,128)(2,1)} %ket.1, bf16[4,512,128]{2,1,0:T(8,128)(2,1)} %bra.1, s32[16,128]{1,0:T(8,128)} %bitcast.17, s32[16,128]{1,0:T(8,128)} %bitcast.22), custom_call_target="tpu_custom_call" | custom-call | tf_op jit(solution)/shard_map/pack/pallas_call | solution.py:151
  8.8 0.0 all-gather.3.cloned.1.call-update
  8.8 30.0 %all_to_all.20 = bf16[16,32,512]{2,1,0:T(8,128)(2,1)S(1)} all-to-all(bf16[16,32,512]{2,1,0:T(8,128)(2,1)} %bitcast.27), channel_id=1, replica_groups=mesh['chan'=16,'ket'=4,'bra'=4] {'chan'}, dimensions={0} | all-to-all | bytes 1048576 | tf_op jit(solution)/shard_map/all_to_all | solution.py:231
  38.9 2.9 %collective-permute-start.1 = (bf16[512,512]{1,0:T(8,128)(2,1)S(1)}, bf16[512,512]{1,0:T(8,128)(2,1)S(1)}, u32[]{:S(2)}, u32[]{:S(2)}) collective-permute-start(bf16[512,512]{1,0:T(8,128)(2,1)S(1)} %bitcast.12), channel_id=1, source_target_pairs={{0,12},{4,0},{8,4},{12,8},{1,13},{5,1},{9,5},{13,9},{2,14},{6,2},{... | collective-permute-start | bytes 1572872 | tf_op jit(solution)/shard_map/ppermute | solution.py:236
  41.7 0.0 collective-permute-start
  41.7 0.7 convert_multiply_fusion
  42.4 0.7 multiply_add_fusion
  43.1 8.8 %collective-permute-done.1.e2 = bf16[512,512]{1,0:T(8,128)(2,1)S(1)} collective-permute-done((bf16[512,512]{1,0:T(8,128)(2,1)S(1)}, bf16[512,512]{1,0:T(8,128)(2,1)S(1)}, u32[]{:S(2)}, u32[]{:S(2)}) %collective-permute-start.1) | collective-permute-done | bytes 524320 | tf_op jit(solution)/shard_map/ppermute | solution.py:236
  51.9 3.6 %collective-permute-start.3 = (bf16[256,512]{1,0:T(8,128)(2,1)S(1)}, bf16[256,512]{1,0:T(8,128)(2,1)S(1)}, u32[]{:S(2)}, u32[]{:S(2)}) collective-permute-start(bf16[256,512]{1,0:T(8,128)(2,1)S(1)} %slice.9), channel_id=1, source_target_pairs={{0,12},{4,0},{8,4},{12,8},{1,13},{5,1},{9,5},{13,9},{2,14},{6,2},{... | collective-permute-start | bytes 786440 | tf_op jit(solution)/shard_map/ppermute | solution.py:238
  55.5 0.2 collective-permute-done.e1
  55.7 0.1 collective-permute-start.2
  55.8 2.4 %select_convert_fusion.spread = bf16[1024,1024]{1,0:T(8,128)(2,1)} fusion(s32[1024]{0:T(1024)S(1)} %get-tuple-element.6, bf16[128]{0:T(256)(128)(2,1)S(1)} %convert_multiply_fusion, s32[1024]{0:T(1024)S(1)} %get-tuple-element.5, s32[128]{0:T(128)S(1)} %get-tuple-element.8, s32[128]{0:T(128)S(1)} %get-tuple-element.7), kind=kOutput, calls=%fused_computation | convolution fusion | flops 271974400 | bytes 2106624 | tf_op jit(solution)/shard_map/dot_general | solution.py:23
  58.2 2.7 %collective-permute-done.3.e3b = bf16[256,512]{1,0:T(8,128)(2,1)S(1)} collective-permute-done((bf16[256,512]{1,0:T(8,128)(2,1)S(1)}, bf16[256,512]{1,0:T(8,128)(2,1)S(1)}, u32[]{:S(2)}, u32[]{:S(2)}) %collective-permute-start.3) | collective-permute-done | bytes 262176 | tf_op jit(solution)/shard_map/ppermute | solution.py:238
  60.9 4.1 %collective-permute-done.2.e3a = bf16[256,512]{1,0:T(8,128)(2,1)S(1)} collective-permute-done((bf16[256,512]{1,0:T(8,128)(2,1)S(1)}, bf16[256,512]{1,0:T(8,128)(2,1)S(1)}, u32[]{:S(2)}, u32[]{:S(2)}) %collective-permute-start.2) | collective-permute-done | bytes 262176 | tf_op jit(solution)/shard_map/ppermute | solution.py:237
  64.9 10.3 %all-gather.3.cloned.1.call-done = bf16[64,128,512]{2,1,0:T(8,128)(2,1)} async-done(((bf16[4,128,512]{2,1,0:T(8,128)(2,1)}), bf16[64,128,512]{2,1,0:T(8,128)(2,1)}) %all-gather.3.cloned.1.call-update) | async-done | bytes 8388624 | tf_op jit(solution)/shard_map/all_gather | solution.py:229
  75.2 7.7 %first_stage.2 = bf16[16,128,256]{2,1,0:T(8,128)(2,1)} custom-call(s32[2048]{0:T(1024)} %left_s.7, s32[2048]{0:T(1024)} %right_s.7, bf16[512,512]{1,0:T(8,128)(2,1)} %bitcast.14, bf16[512,512]{1,0:T(8,128)(2,1)} %copy-done.4, bf16[512,512]{1,0:T(8,128)(2,1)} %copy-done.3, bf16[256,512]{1,0:T(8,128)(2,1)} %copy-done.6, bf16[256,512]{1,0:T(8,128)(2,1)} %copy-done.5, ...), custom_call_target="tpu_custom_call" | custom-call | flops 1073741824 | bytes 8388608 | tf_op jit(solution)/shard_map/first_stage/pallas_call | solution.py:163
  82.9 4.8 %all-to-all-start.1 = ((bf16[16,128,256]{2,1,0:T(8,128)(2,1)}), bf16[16,128,256]{2,1,0:T(8,128)(2,1)S(1)}, u32[]{:S(2)}, u32[]{:S(2)}) async-start(bf16[16,128,256]{2,1,0:T(8,128)(2,1)} %first_stage.2), calls=%async_computation.1 | async-start | bytes 2097152 | tf_op jit(solution)/shard_map/all_to_all | solution.py:245
  87.8 7.5 %first_stage.3 = bf16[16,128,256]{2,1,0:T(8,128)(2,1)} custom-call(s32[2048]{0:T(1024)} %left_s.7, s32[2048]{0:T(1024)} %right_s.7, bf16[512,512]{1,0:T(8,128)(2,1)} %bitcast.15, bf16[512,512]{1,0:T(8,128)(2,1)} %copy-done.4, bf16[512,512]{1,0:T(8,128)(2,1)} %copy-done.3, bf16[256,512]{1,0:T(8,128)(2,1)} %copy-done.6, bf16[256,512]{1,0:T(8,128)(2,1)} %copy-done.5, ...), custom_call_target="tpu_custom_call" | custom-call | flops 1073741824 | bytes 8388608 | tf_op jit(solution)/shard_map/first_stage/pallas_call | solution.py:163
  95.2 20.5 %all-to-all-done.1.got = bf16[16,128,256]{2,1,0:T(8,128)(2,1)S(1)} async-done(((bf16[16,128,256]{2,1,0:T(8,128)(2,1)}), bf16[16,128,256]{2,1,0:T(8,128)(2,1)S(1)}, u32[]{:S(2)}, u32[]{:S(2)}) %all-to-all-start.1) | async-done | bytes 1048608 | tf_op jit(solution)/shard_map/all_to_all | solution.py:245
  115.8 3.6 %all-to-all-start.2 = ((bf16[16,128,256]{2,1,0:T(8,128)(2,1)}), bf16[16,128,256]{2,1,0:T(8,128)(2,1)S(1)}, u32[]{:S(2)}, u32[]{:S(2)}) async-start(bf16[16,128,256]{2,1,0:T(8,128)(2,1)} %first_stage.3), calls=%async_computation.3 | async-start | bytes 2097152 | tf_op jit(solution)/shard_map/all_to_all | solution.py:245
  119.3 0.0 reduce-scatter.2.cloned.1.call-start
  119.4 8.4 %second_stage.2 = bf16[2048,256]{1,0:T(8,128)(2,1)} custom-call(s32[2048]{0:T(1024)} %left_s.7, s32[2048]{0:T(1024)} %right_s.7, bf16[16,128,256]{2,1,0:T(8,128)(2,1)} %copy-done.1, bf16[16,4,128,512]{3,2,1,0:T(8,128)(2,1)} %bitcast.10, s32[16,128]{1,0:T(8,128)} %bitcast.20, s32[16,128]{1,0:T(8,128)} %bitcast.25), custom_call_target="tpu_custom_call" | custom-call | flops 1073741824 | bytes 7340032 | tf_op jit(solution)/shard_map/second_stage/pallas_call | solution.py:190
  127.8 0.0 reduce-scatter.2.cloned.1.call-update
  127.8 19.4 %all-to-all-done.2.got = bf16[16,128,256]{2,1,0:T(8,128)(2,1)S(1)} async-done(((bf16[16,128,256]{2,1,0:T(8,128)(2,1)}), bf16[16,128,256]{2,1,0:T(8,128)(2,1)S(1)}, u32[]{:S(2)}, u32[]{:S(2)}) %all-to-all-start.2) | async-done | bytes 1048608 | tf_op jit(solution)/shard_map/all_to_all | solution.py:245
  147.2 1.0 copy-done.2
  148.2 8.4 %second_stage.3 = bf16[2048,256]{1,0:T(8,128)(2,1)} custom-call(s32[2048]{0:T(1024)} %left_s.7, s32[2048]{0:T(1024)} %right_s.7, bf16[16,128,256]{2,1,0:T(8,128)(2,1)} %copy-done.2, bf16[16,4,128,512]{3,2,1,0:T(8,128)(2,1)} %bitcast.11, s32[16,128]{1,0:T(8,128)} %bitcast.21, s32[16,128]{1,0:T(8,128)} %bitcast.26), custom_call_target="tpu_custom_call" | custom-call | flops 1073741824 | bytes 7340032 | tf_op jit(solution)/shard_map/second_stage/pallas_call | solution.py:190
  156.5 17.9 %all_to_all.21 = bf16[4,512,256]{2,1,0:T(8,128)(2,1)S(1)} all-to-all(bf16[4,512,256]{2,1,0:T(8,128)(2,1)} %bitcast.16), channel_id=1, replica_groups=mesh['chan'=16,'ket'=4,'bra'=4] {'bra'}, dimensions={0} | all-to-all | bytes 2097152 | tf_op jit(solution)/shard_map/all_to_all | solution.py:248
  174.4 0.1 convert_reduce_fusion
  174.5 0.0 reduce-scatter.2.cloned.1.call-done
  174.6 1.0 convert_element_type.19
  175.6 1.1 maximum_bitcast_fusion
  (16 shorter events, 0.1 us)
Async XLA Ops:
  6.5 68.7 %all-gather.3.cloned.1.call-start = ((), (), s32[]{:S(2)}) async-start(), calls=%async_computation.6 | async-start | bytes 8912896 | tf_op jit(solution)/shard_map/all_gather | solution.py:229
  38.9 36.3 %copy-start = (bf16[16,32,512]{2,1,0:T(8,128)(2,1)}, bf16[16,32,512]{2,1,0:T(8,128)(2,1)S(1)}, u32[]{:S(2)}) copy-start(bf16[16,32,512]{2,1,0:T(8,128)(2,1)S(1)} %all_to_all.20) | copy-start | bytes 1572868
  38.9 13.0 %collective-permute-start.1 = (bf16[512,512]{1,0:T(8,128)(2,1)S(1)}, bf16[512,512]{1,0:T(8,128)(2,1)S(1)}, u32[]{:S(2)}, u32[]{:S(2)}) collective-permute-start(bf16[512,512]{1,0:T(8,128)(2,1)S(1)} %bitcast.12), channel_id=1, source_target_pairs={{0,12},{4,0},{8,4},{12,8},{1,13},{5,1},{9,5},{13,9},{2,14},{6,2},{... | collective-permute-start | bytes 1572872 | tf_op jit(solution)/shard_map/ppermute | solution.py:236
  41.7 14.0 %collective-permute-start = (bf16[512,512]{1,0:T(8,128)(2,1)S(1)}, bf16[512,512]{1,0:T(8,128)(2,1)S(1)}, u32[]{:S(2)}, u32[]{:S(2)}) collective-permute-start(bf16[512,512]{1,0:T(8,128)(2,1)S(1)} %bitcast.13), channel_id=1, source_target_pairs={{0,4},{4,8},{8,12},{12,0},{1,5},{5,9},{9,13},{13,1},{2,6},{6,10},{... | collective-permute-start | bytes 1572872 | tf_op jit(solution)/shard_map/ppermute | solution.py:235
  51.9 23.3 %copy-start.3 = (bf16[512,512]{1,0:T(8,128)(2,1)}, bf16[512,512]{1,0:T(8,128)(2,1)S(1)}, u32[]{:S(2)}) copy-start(bf16[512,512]{1,0:T(8,128)(2,1)S(1)} %collective-permute-done.1.e2) | copy-start | bytes 1572868
  51.9 8.9 %collective-permute-start.3 = (bf16[256,512]{1,0:T(8,128)(2,1)S(1)}, bf16[256,512]{1,0:T(8,128)(2,1)S(1)}, u32[]{:S(2)}, u32[]{:S(2)}) collective-permute-start(bf16[256,512]{1,0:T(8,128)(2,1)S(1)} %slice.9), channel_id=1, source_target_pairs={{0,12},{4,0},{8,4},{12,8},{1,13},{5,1},{9,5},{13,9},{2,14},{6,2},{... | collective-permute-start | bytes 786440 | tf_op jit(solution)/shard_map/ppermute | solution.py:238
  55.7 19.5 %copy-start.4 = (bf16[512,512]{1,0:T(8,128)(2,1)}, bf16[512,512]{1,0:T(8,128)(2,1)S(1)}, u32[]{:S(2)}) copy-start(bf16[512,512]{1,0:T(8,128)(2,1)S(1)} %collective-permute-done.e1) | copy-start | bytes 1572868
  55.7 9.2 %collective-permute-start.2 = (bf16[256,512]{1,0:T(8,128)(2,1)S(1)}, bf16[256,512]{1,0:T(8,128)(2,1)S(1)}, u32[]{:S(2)}, u32[]{:S(2)}) collective-permute-start(bf16[256,512]{1,0:T(8,128)(2,1)S(1)} %slice.8), channel_id=1, source_target_pairs={{0,4},{4,8},{8,12},{12,0},{1,5},{5,9},{9,13},{13,1},{2,6},{6,10},{... | collective-permute-start | bytes 786440 | tf_op jit(solution)/shard_map/ppermute | solution.py:237
  60.9 14.4 %copy-start.5 = (bf16[256,512]{1,0:T(8,128)(2,1)}, bf16[256,512]{1,0:T(8,128)(2,1)S(1)}, u32[]{:S(2)}) copy-start(bf16[256,512]{1,0:T(8,128)(2,1)S(1)} %collective-permute-done.3.e3b) | copy-start | bytes 786436
  64.9 10.3 %copy-start.6 = (bf16[256,512]{1,0:T(8,128)(2,1)}, bf16[256,512]{1,0:T(8,128)(2,1)S(1)}, u32[]{:S(2)}) copy-start(bf16[256,512]{1,0:T(8,128)(2,1)S(1)} %collective-permute-done.2.e3a) | copy-start | bytes 786436
  82.9 32.8 %all-to-all-start.1 = ((bf16[16,128,256]{2,1,0:T(8,128)(2,1)}), bf16[16,128,256]{2,1,0:T(8,128)(2,1)S(1)}, u32[]{:S(2)}, u32[]{:S(2)}) async-start(bf16[16,128,256]{2,1,0:T(8,128)(2,1)} %first_stage.2), calls=%async_computation.1 | async-start | bytes 2097152 | tf_op jit(solution)/shard_map/all_to_all | solution.py:245
  115.8 3.6 %copy-start.1 = (bf16[16,128,256]{2,1,0:T(8,128)(2,1)}, bf16[16,128,256]{2,1,0:T(8,128)(2,1)S(1)}, u32[]{:S(2)}) copy-start(bf16[16,128,256]{2,1,0:T(8,128)(2,1)S(1)} %all-to-all-done.1.got) | copy-start | bytes 3145732
  115.8 31.4 %all-to-all-start.2 = ((bf16[16,128,256]{2,1,0:T(8,128)(2,1)}), bf16[16,128,256]{2,1,0:T(8,128)(2,1)S(1)}, u32[]{:S(2)}, u32[]{:S(2)}) async-start(bf16[16,128,256]{2,1,0:T(8,128)(2,1)} %first_stage.3), calls=%async_computation.3 | async-start | bytes 2097152 | tf_op jit(solution)/shard_map/all_to_all | solution.py:245
  119.3 55.3 %reduce-scatter.2.cloned.1.call-start = ((), (), s32[]{:S(2)}) async-start(), calls=%async_computation.5 | async-start | bytes 1310720 | tf_op jit(solution)/shard_map/reduce_scatter | solution.py:247
  147.2 1.0 copy-start.2
Sparse Core Ops, SparseCore 0:
  9.2 65.9 all-gather.2
  127.9 27.4 reduce-scatter.1

commit v3 on v2

v3 whole, which is shorter than its diff:
```python
import functools

import jax
import jax.numpy as jnp
from jax import lax
from jax.experimental import pallas as pl
from jax.experimental.pallas import tpu as pltpu
from jax.sharding import PartitionSpec as P

BF16 = jnp.bfloat16
F32 = jnp.float32
PHYS = (0, 1, 1, 2)
PLANE = (0, 0, 1, 0)
WIDTH = 256


def spread_coupling(op_in, op_out, op_bra, op_ket, op_code):
    rows = jnp.arange(1024, dtype=jnp.int32)
    pick_out = (rows[:, None] // 16 == (op_out * 4 + op_bra)[None, :]).astype(BF16)
    weights = op_code.astype(F32) * 0.25
    hit = (op_ket * 16 + op_in)[:, None] == rows[None, :] // 16
    pick_in = jnp.where(hit, weights[:, None], 0.0).astype(BF16)
    table = jnp.dot(pick_out, pick_in, preferred_element_type=F32)
    same = rows[:, None] % 16 == rows[None, :] % 16
    return jnp.where(same, table, 0.0).astype(BF16)


def charge_row(charges, block):
    return charges[pl.ds(block, 1), :].astype(F32)


def charge_column(charges, block):
    return jnp.transpose(jnp.broadcast_to(charge_row(charges, block), (128, 128)))


def chosen(x, diff):
    diff = diff.astype(BF16)
    return jnp.where(diff == 0, x[0], jnp.where(diff == 1, x[1], x[3]))


def pack_kernel(ket, bra, left, right, out):
    chan, y, x = lax.axis_index("chan"), lax.axis_index("ket"), lax.axis_index("bra")
    rows = charge_column(left, chan)
    for r in range(4):
        cut = slice(r * 128, (r + 1) * 128)
        diff = charge_row(right, y * 4 + r) - rows
        out[r, 0] = chosen([ket[s, :, cut] for s in range(4)], diff)
        out[r, 1] = ket[2, :, cut]
    own = pl.ds(pl.multiple_of(y * 128, 128), 128)
    diff = charge_row(right, chan) - charge_column(left, x * 4 + y)
    first = chosen([bra[t, own, :] for t in range(4)], diff)
    out[4, 0] = jnp.transpose(first.astype(F32)).astype(BF16)
    out[4, 1] = jnp.transpose(bra[2, own, :].astype(F32)).astype(BF16)


def masked_tiles(parts, rows, cols, charge):
    tiles = []
    for part, col in zip(parts, cols):
        tiles.append(jnp.where(rows + charge == col, part, jnp.zeros_like(part)))
    return jnp.concatenate(tiles, axis=1)


def begin(copies, sems):
    made = [pltpu.make_async_copy(src, dst, sems.at[n]) for n, (src, dst) in enumerate(copies)]
    for copy in made:
        copy.start()
    return made


def first_kernel(
    start, left_s, right_s, e0, e1, e2, e3a, e3b, gathered, left, right, spread,
    out, env, planes, table, column, acc, parts, results, sems, out_sems,
):
    y = lax.axis_index("ket")
    width = acc.shape[1]
    tiles = width // 128
    blocks = [lax.rem(y + n, 4) for n in (0, 3, 1, 2)]
    copies = [(gathered.at[:, pl.ds(start // 128, tiles)], planes)]
    for h in range(2):
        cut = pl.ds(h * 256, 256)
        copies += [(e.at[:, cut], env.at[2 * blocks[i] + h]) for i, e in enumerate((e0, e1, e2))]
        copies += [
            (e.at[:, cut], env.at[2 * blocks[3] + h, pl.ds(n * 256, 256)])
            for n, e in enumerate((e3a, e3b))
        ]
    copies.append((spread, table))
    copies = begin(copies, sems)
    for c in range(16):
        column[c * 128 : (c + 1) * 128, :] = charge_column(left, c).astype(BF16)
    at = y * 4 + start // 128
    cols = [charge_row(right, at + r).astype(BF16) for r in range(tiles)]
    least, most = right_s[y * 512 + start], right_s[y * 512 + start + width - 1]
    for copy in copies[:-1]:
        copy.wait()
    for s in range(4):
        acc[...] = jnp.zeros_like(acc)
        low = sum((left_s[256 * i + 255] + PHYS[s] < least).astype(jnp.int32) for i in range(8))
        high = sum((left_s[256 * i] + PHYS[s] <= most).astype(jnp.int32) for i in range(8))

        def step(i, carry):
            pair = []
            for r in range(2):
                rows = column[pl.ds(pl.multiple_of(i * 256 + r * 128, 128), 128), :]
                values = [planes[2 * i + r, q, PLANE[s]] for q in range(tiles)]
                pair.append(masked_tiles(values, rows, cols, PHYS[s]))
            block = jnp.concatenate(pair, axis=0)
            acc[...] += jnp.dot(env[i], block, preferred_element_type=F32)
            return carry

        lax.fori_loop(low, high, step, 0)
        product = acc[...].astype(BF16).reshape(16, 2, 16, width)
        for h in range(2):
            parts[h, s * 256 : (s + 1) * 256, :] = product[:, h].reshape(256, width)
    copies[-1].wait()
    sent = []
    for h in range(2):
        mixed = jnp.dot(table[...], parts[h], preferred_element_type=F32)
        results[h] = mixed.astype(BF16).reshape(16, 64, width)
        copy = pltpu.make_async_copy(results.at[h], out.at[:, pl.ds(h * 64, 64)], out_sems.at[h])
        copy.start()
        sent.append(copy)
    for copy in sent:
        copy.wait()


def second_kernel(
    left_s, right_s, got, gathered, left, right,
    out, mixed, planes, column, acc, results, sems, plane_sems, out_sems,
):
    x = lax.axis_index("bra")
    copies = []
    for t in range(4):
        for half in range(2):
            for h in range(2):
                source = got.at[pl.ds(8 * half, 8), pl.ds(h * 64 + t * 16, 16)]
                copies.append((source, mixed.at[t * 2 + half, :, pl.ds(h * 16, 16)]))
    loads = begin([(gathered.at[:, pl.ds(0, 4)], planes.at[0])], plane_sems)
    copies = begin(copies, sems)
    for g in range(1, 4):
        copy = pltpu.make_async_copy(
            gathered.at[:, pl.ds(g * 4, 4)], planes.at[g], plane_sems.at[g]
        )
        copy.start()
        loads.append(copy)
    for c in range(16):
        column[c * 128 : (c + 1) * 128, :] = charge_column(right, c).astype(BF16)
    cols = [charge_row(left, x * 4 + r).astype(BF16) for r in range(4)]
    for copy in copies:
        copy.wait()
    sent = []
    for g in range(4):
        loads[g].wait()
        acc[...] = jnp.zeros_like(acc)
        least, most = right_s[g * 512], right_s[g * 512 + 511]
        for t in range(4):
            for h in range(2):
                first = left_s[x * 512 + h * 256] + PHYS[t]
                last = left_s[x * 512 + h * 256 + 255] + PHYS[t]

                @pl.when((first <= most) & (last >= least))
                def _():
                    stack = []
                    for r in range(4):
                        rows = column[g * 512 + r * 128 : g * 512 + (r + 1) * 128, :]
                        values = [planes[g, 2 * h + q, r, PLANE[t]] for q in range(2)]
                        stack.append(masked_tiles(values, rows, cols[2 * h : 2 * h + 2], -PHYS[t]))
                    block = jnp.concatenate(stack, axis=0)
                    other = mixed[t * 2 + h].reshape(256, acc.shape[1])
                    acc[...] += jnp.dot(block, other, preferred_element_type=F32)

        results[g] = acc[...].astype(BF16)
        copy = pltpu.make_async_copy(results.at[g], out.at[pl.ds(g * 512, 512)], out_sems.at[g])
        copy.start()
        sent.append(copy)
    for copy in sent:
        copy.wait()


SCALARS = pl.BlockSpec(memory_space=pltpu.SMEM)
FAST = pl.BlockSpec(memory_space=pltpu.VMEM)
PLACE = pl.BlockSpec(memory_space=pl.ANY)


def pack(ket_tensor, bra_tensor, left, right):
    return pl.pallas_call(
        pack_kernel,
        out_shape=jax.ShapeDtypeStruct((5, 2, 128, 128), BF16),
        in_specs=[FAST] * 4,
        out_specs=FAST,
        name="pack",
    )(ket_tensor, bra_tensor, left, right)


def first_stage(charge_left, charge_right, pieces, gathered, left, right, spread, start):
    return pl.pallas_call(
        functools.partial(first_kernel, start),
        out_shape=jax.ShapeDtypeStruct((16, 128, WIDTH), BF16),
        in_specs=[SCALARS, SCALARS] + [PLACE] * (len(pieces) + 1) + [FAST, FAST, PLACE],
        out_specs=PLACE,
        scratch_shapes=[
            pltpu.VMEM((8, 512, 256), BF16),
            pltpu.VMEM((16, WIDTH // 128, 2, 128, 128), BF16),
            pltpu.VMEM((1024, 1024), BF16),
            pltpu.VMEM((2048, 128), BF16),
            pltpu.VMEM((512, WIDTH), F32),
            pltpu.VMEM((2, 1024, WIDTH), BF16),
            pltpu.VMEM((2, 16, 64, WIDTH), BF16),
            pltpu.SemaphoreType.DMA((12,)),
            pltpu.SemaphoreType.DMA((2,)),
        ],
        cost_estimate=pl.CostEstimate(
            flops=512 * 2048 * 4 * WIDTH, bytes_accessed=8 << 20, transcendentals=0
        ),
        name="first_stage",
    )(charge_left, charge_right, *pieces, gathered, left, right, spread)


def second_stage(charge_left, charge_right, got, gathered, left, right):
    return pl.pallas_call(
        second_kernel,
        out_shape=jax.ShapeDtypeStruct((2048, WIDTH), BF16),
        in_specs=[SCALARS, SCALARS, PLACE, PLACE, FAST, FAST],
        out_specs=PLACE,
        scratch_shapes=[
            pltpu.VMEM((8, 8, 32, WIDTH), BF16),
            pltpu.VMEM((4, 4, 4, 2, 128, 128), BF16),
            pltpu.VMEM((2048, 128), BF16),
            pltpu.VMEM((512, WIDTH), F32),
            pltpu.VMEM((4, 512, WIDTH), BF16),
            pltpu.SemaphoreType.DMA((16,)),
            pltpu.SemaphoreType.DMA((4,)),
            pltpu.SemaphoreType.DMA((4,)),
        ],
        cost_estimate=pl.CostEstimate(
            flops=2048 * 2048 * WIDTH, bytes_accessed=7 << 20, transcendentals=0
        ),
        name="second_stage",
    )(charge_left, charge_right, got, gathered, left, right)


def local(
    environment,
    ket_tensor,
    bra_tensor,
    charge_left,
    charge_right,
    op_in,
    op_out,
    op_bra,
    op_ket,
    op_code,
):
    left, right = charge_left.reshape(16, 128), charge_right.reshape(16, 128)
    planes = pack(ket_tensor, bra_tensor, left, right)
    gathered = lax.all_gather(planes, "chan", axis=0)

    env = lax.all_to_all(environment.reshape(16, 32, 512), "chan", 0, 0, tiled=True)
    env = env.reshape(512, 512)
    up = [(i, (i + 1) % 4) for i in range(4)]
    down = [(i, (i + 3) % 4) for i in range(4)]
    env_below = lax.ppermute(env, "ket", up)
    env_above = lax.ppermute(env, "ket", down)
    far_a = lax.ppermute(env_below[:256], "ket", up)
    far_b = lax.ppermute(env_above[256:], "ket", down)
    spread = spread_coupling(op_in, op_out, op_bra, op_ket, op_code)
    pieces = (env, env_below, env_above, far_a, far_b)
    gathered, spread, pieces = lax.optimization_barrier((gathered, spread, pieces))
    bra_gathered = lax.all_gather(gathered[:, 4], "ket", axis=0)

    terms = []
    for start in (0, WIDTH):
        mixed = first_stage(charge_left, charge_right, pieces, gathered, left, right, spread, start)
        got = lax.all_to_all(mixed, "chan", 0, 0, tiled=True)
        terms.append(second_stage(charge_left, charge_right, got, bra_gathered, left, right))
    one = lax.psum_scatter(terms[0], "bra", scatter_dimension=0, tiled=True).astype(F32)
    two = lax.all_to_all(terms[1].reshape(4, 512, WIDTH), "bra", 0, 0, tiled=True)
    two = jnp.sum(two.astype(F32), axis=0)
    return jnp.concatenate([one, two], axis=1)[None]


def solution(mesh):
    placed = (
        P("chan", "bra", "ket"),
        P(None, "chan", "ket"),
        P(None, "bra", "chan"),
        P(),
        P(),
        P(),
        P(),
        P(),
        P(),
        P(),
    )
    return jax.shard_map(
        local, mesh=mesh, in_specs=placed, out_specs=P("chan", "bra", "ket"), check_vma=False
    )
```

time: 186 us -> 177 us (0.952)
  waiting for transfers between devices: 66 us -> 54.6 us
  local copies, waits for them, and re-layouts: 1.03 us -> 3.47 us
    all_gather x1, waiting for transfers between devices: 10.3 us -> 0.01 us  [local(): gathered = lax.all_gather(planes, 'chan', axis=0)]
    all_to_all x2, waiting for transfers between devices: 39.9 us -> 35.6 us  [local(): got = lax.all_to_all(mixed, 'chan', 0, 0, tiled=True)]
    all_gather x0 -> x1, waiting for transfers between devices: none -> 3.65 us  [local(): bra_gathered = lax.all_gather(gathered[:, 4], 'ket', axis=0)]
    slice x0 -> x1, local copies, waits for them, and re-layouts: none -> 2.44 us  [local(): bra_gathered = lax.all_gather(gathered[:, 4], 'ket', axis=0)]
  transfers between devices with their start and end apart: 8 -> 9, of which waited for: 7 -> 7; matrix products, arithmetic and copies ran while one was open for 2% -> 2% of each run, Pallas kernels for 13% -> 18%
where the time goes in v3:
time: 177 us; the launch traced here: 175 us
  waiting for transfers between devices  54.6 us (31%)
  blocking collectives  47.9 us (27%)
  Pallas kernels  33.9 us (19%)
  starting transfers between devices  16.2 us (9%)
  between operations  13.2 us (7%)
  other arithmetic  3.63 us (2%)
  local copies, waits for them, and re-layouts  3.47 us (2%)
  matrix products  2.36 us (1%)
    all_to_all x2, waiting for transfers between devices, local(): got = lax.all_to_all(mixed, 'chan', 0, 0, tiled=True)  35.6 us
    all_to_all x1, blocking collectives, local(): lax.all_to_all(environment.reshape(16, 32, 512), 'chan', 0, 0, tiled=True)  30 us
    all_to_all x1, blocking collectives, local(): lax.all_to_all(terms[1].reshape(4, 512, WIDTH), 'bra', 0, 0, tiled=True)  17.9 us
    pallas_call x2, Pallas kernels, second_stage(): pl.pallas_call(second_kernel, out_shape=jax.ShapeDtypeStruct((2048, WIDTH...  17.4 us
    pallas_call x2, Pallas kernels, first_stage(): pl.pallas_call(functools.partial(first_kernel, start), out_shape=jax.Shap...  14.4 us
    all_to_all x2, starting transfers between devices, local(): got = lax.all_to_all(mixed, 'chan', 0, 0, tiled=True)  9.52 us
    ppermute x1, waiting for transfers between devices, local(): env_above = lax.ppermute(env, 'ket', down)  8.79 us
    ppermute x1, waiting for transfers between devices, local(): far_a = lax.ppermute(env_below[:256], 'ket', up)  3.67 us
  transfers between devices with their start and end apart: 9, of which 7 were waited for; matrix products, arithmetic and copies ran while one was open for 2% of the time, Pallas kernels for 18%

profile of v3, /device:TPU:1, one launch (start us, length us, event | category | flops | bytes accessed | tf_op | source)
XLA Modules:
  0.0 175.2 jit_solution(3733698085336927855)
XLA Ops:
  6.5 2.1 %pack.1 = bf16[5,2,128,128]{3,2,1,0:T(8,128)(2,1)} custom-call(bf16[4,128,512]{2,1,0:T(8,128)(2,1)} %ket.1, bf16[4,512,128]{2,1,0:T(8,128)(2,1)} %bra.1, s32[16,128]{1,0:T(8,128)} %bitcast.19, s32[16,128]{1,0:T(8,128)} %bitcast.24), custom_call_target="tpu_custom_call" | custom-call | tf_op jit(solution)/shard_map/pack/pallas_call | solution.py:185
  8.6 0.0 all-gather.5.cloned.1.call-update
  8.7 0.0 all-gather.7.cloned.1.call-start
  8.7 30.0 %all_to_all.20 = bf16[16,32,512]{2,1,0:T(8,128)(2,1)S(1)} all-to-all(bf16[16,32,512]{2,1,0:T(8,128)(2,1)} %bitcast.29), channel_id=1, replica_groups=mesh['chan'=16,'ket'=4,'bra'=4] {'chan'}, dimensions={0} | all-to-all | bytes 1048576 | tf_op jit(solution)/shard_map/all_to_all | solution.py:257
  38.7 2.9 %collective-permute-start.1 = (bf16[512,512]{1,0:T(8,128)(2,1)S(1)}, bf16[512,512]{1,0:T(8,128)(2,1)S(1)}, u32[]{:S(2)}, u32[]{:S(2)}) collective-permute-start(bf16[512,512]{1,0:T(8,128)(2,1)S(1)} %bitcast.14), channel_id=1, source_target_pairs={{0,12},{4,0},{8,4},{12,8},{1,13},{5,1},{9,5},{13,9},{2,14},{6,2},{... | collective-permute-start | bytes 1572872 | tf_op jit(solution)/shard_map/ppermute | solution.py:262
  41.6 0.7 convert_multiply_fusion
  42.2 0.7 multiply_add_fusion
  42.9 8.8 %collective-permute-done.1.e2 = bf16[512,512]{1,0:T(8,128)(2,1)S(1)} collective-permute-done((bf16[512,512]{1,0:T(8,128)(2,1)S(1)}, bf16[512,512]{1,0:T(8,128)(2,1)S(1)}, u32[]{:S(2)}, u32[]{:S(2)}) %collective-permute-start.1) | collective-permute-done | bytes 524320 | tf_op jit(solution)/shard_map/ppermute | solution.py:262
  51.8 3.6 %collective-permute-start.3 = (bf16[256,512]{1,0:T(8,128)(2,1)S(1)}, bf16[256,512]{1,0:T(8,128)(2,1)S(1)}, u32[]{:S(2)}, u32[]{:S(2)}) collective-permute-start(bf16[256,512]{1,0:T(8,128)(2,1)S(1)} %slice.13), channel_id=1, source_target_pairs={{0,12},{4,0},{8,4},{12,8},{1,13},{5,1},{9,5},{13,9},{2,14},{6,2},{... | collective-permute-start | bytes 786440 | tf_op jit(solution)/shard_map/ppermute | solution.py:264
  55.3 0.2 collective-permute-done.e1
  55.6 0.1 collective-permute-start.2
  55.6 2.4 %select_convert_fusion.spread = bf16[1024,1024]{1,0:T(8,128)(2,1)} fusion(s32[1024]{0:T(1024)S(1)} %get-tuple-element.20, bf16[128]{0:T(256)(128)(2,1)S(1)} %convert_multiply_fusion, s32[1024]{0:T(1024)S(1)} %get-tuple-element.19, s32[128]{0:T(128)S(1)} %get-tuple-element.22, s32[128]{0:T(128)S(1)} %get-tuple-element.21), kind=kOutput, calls=%fused_computation | convolution fusion | flops 271974400 | bytes 2106624 | tf_op jit(solution)/shard_map/dot_general | solution.py:23
  58.0 2.6 %collective-permute-done.3.e3b = bf16[256,512]{1,0:T(8,128)(2,1)S(1)} collective-permute-done((bf16[256,512]{1,0:T(8,128)(2,1)S(1)}, bf16[256,512]{1,0:T(8,128)(2,1)S(1)}, u32[]{:S(2)}, u32[]{:S(2)}) %collective-permute-start.3) | collective-permute-done | bytes 262176 | tf_op jit(solution)/shard_map/ppermute | solution.py:264
  60.7 3.7 %collective-permute-done.2.e3a = bf16[256,512]{1,0:T(8,128)(2,1)S(1)} collective-permute-done((bf16[256,512]{1,0:T(8,128)(2,1)S(1)}, bf16[256,512]{1,0:T(8,128)(2,1)S(1)}, u32[]{:S(2)}, u32[]{:S(2)}) %collective-permute-start.2) | collective-permute-done | bytes 262176 | tf_op jit(solution)/shard_map/ppermute | solution.py:263
  64.3 2.4 %slice.11 = bf16[16,1,2,128,128]{4,3,2,1,0:T(8,128)(2,1)} slice(bf16[16,5,2,128,128]{4,3,2,1,0:T(8,128)(2,1)} %bitcast.9), slice={[0:16], [4:5], [0:2], [0:128], [0:128]} | slice | bytes 2097152 | tf_op jit(solution)/shard_map/slice | solution.py:268
  66.8 6.6 %first_stage.2 = bf16[16,128,256]{2,1,0:T(8,128)(2,1)} custom-call(s32[2048]{0:T(1024)} %left_s.7, s32[2048]{0:T(1024)} %right_s.7, bf16[512,512]{1,0:T(8,128)(2,1)} %bitcast.16, bf16[512,512]{1,0:T(8,128)(2,1)} %copy-done.4, bf16[512,512]{1,0:T(8,128)(2,1)} %copy-done.3, bf16[256,512]{1,0:T(8,128)(2,1)} %copy-done.6, bf16[256,512]{1,0:T(8,128)(2,1)} %copy-done.5, ...), custom_call_target="tpu_custom_call" | custom-call | flops 1073741824 | bytes 8388608 | tf_op jit(solution)/shard_map/first_stage/pallas_call | solution.py:195
  73.5 6.0 %all-to-all-start.1 = ((bf16[16,128,256]{2,1,0:T(8,128)(2,1)}), bf16[16,128,256]{2,1,0:T(8,128)(2,1)S(1)}, u32[]{:S(2)}, u32[]{:S(2)}) async-start(bf16[16,128,256]{2,1,0:T(8,128)(2,1)} %first_stage.2), calls=%async_computation.1 | async-start | bytes 2097152 | tf_op jit(solution)/shard_map/all_to_all | solution.py:273
  79.5 7.7 %first_stage.3 = bf16[16,128,256]{2,1,0:T(8,128)(2,1)} custom-call(s32[2048]{0:T(1024)} %left_s.7, s32[2048]{0:T(1024)} %right_s.7, bf16[512,512]{1,0:T(8,128)(2,1)} %bitcast.17, bf16[512,512]{1,0:T(8,128)(2,1)} %copy-done.4, bf16[512,512]{1,0:T(8,128)(2,1)} %copy-done.3, bf16[256,512]{1,0:T(8,128)(2,1)} %copy-done.6, bf16[256,512]{1,0:T(8,128)(2,1)} %copy-done.5, ...), custom_call_target="tpu_custom_call" | custom-call | flops 1073741824 | bytes 8388608 | tf_op jit(solution)/shard_map/first_stage/pallas_call | solution.py:195
  87.2 20.3 %all-to-all-done.1.got = bf16[16,128,256]{2,1,0:T(8,128)(2,1)S(1)} async-done(((bf16[16,128,256]{2,1,0:T(8,128)(2,1)}), bf16[16,128,256]{2,1,0:T(8,128)(2,1)S(1)}, u32[]{:S(2)}, u32[]{:S(2)}) %all-to-all-start.1) | async-done | bytes 1048608 | tf_op jit(solution)/shard_map/all_to_all | solution.py:273
  107.5 3.6 %all-to-all-start.2 = ((bf16[16,128,256]{2,1,0:T(8,128)(2,1)}), bf16[16,128,256]{2,1,0:T(8,128)(2,1)S(1)}, u32[]{:S(2)}, u32[]{:S(2)}) async-start(bf16[16,128,256]{2,1,0:T(8,128)(2,1)} %first_stage.3), calls=%async_computation.3 | async-start | bytes 2097152 | tf_op jit(solution)/shard_map/all_to_all | solution.py:273
  111.0 0.0 reduce-scatter.2.cloned.1.call-start
  111.1 3.6 %all-gather.7.cloned.1.call-done = bf16[64,1,2,128,128]{4,3,2,1,0:T(8,128)(2,1)} async-done(((bf16[16,1,2,128,128]{4,3,2,1,0:T(8,128)(2,1)}), bf16[64,1,2,128,128]{4,3,2,1,0:T(8,128)(2,1)}) %all-gather.7.cloned.1.call-update) | async-done | bytes 4194320 | tf_op jit(solution)/shard_map/all_gather | solution.py:268
  114.7 8.8 %second_stage.2 = bf16[2048,256]{1,0:T(8,128)(2,1)} custom-call(s32[2048]{0:T(1024)} %left_s.7, s32[2048]{0:T(1024)} %right_s.7, bf16[16,128,256]{2,1,0:T(8,128)(2,1)} %copy-done.1, bf16[4,16,2,128,128]{4,3,2,1,0:T(8,128)(2,1)} %bitcast.12, s32[16,128]{1,0:T(8,128)} %bitcast.22, s32[16,128]{1,0:T(8,128)} %bitcast.27), custom_call_target="tpu_custom_call" | custom-call | flops 1073741824 | bytes 7340032 | tf_op jit(solution)/shard_map/second_stage/pallas_call | solution.py:219
  123.5 0.0 reduce-scatter.2.cloned.1.call-update
  123.5 15.4 %all-to-all-done.2.got = bf16[16,128,256]{2,1,0:T(8,128)(2,1)S(1)} async-done(((bf16[16,128,256]{2,1,0:T(8,128)(2,1)}), bf16[16,128,256]{2,1,0:T(8,128)(2,1)S(1)}, u32[]{:S(2)}, u32[]{:S(2)}) %all-to-all-start.2) | async-done | bytes 1048608 | tf_op jit(solution)/shard_map/all_to_all | solution.py:273
  138.9 1.0 copy-done.2
  139.8 8.7 %second_stage.3 = bf16[2048,256]{1,0:T(8,128)(2,1)} custom-call(s32[2048]{0:T(1024)} %left_s.7, s32[2048]{0:T(1024)} %right_s.7, bf16[16,128,256]{2,1,0:T(8,128)(2,1)} %copy-done.2, bf16[4,16,2,128,128]{4,3,2,1,0:T(8,128)(2,1)} %bitcast.13, s32[16,128]{1,0:T(8,128)} %bitcast.23, s32[16,128]{1,0:T(8,128)} %bitcast.28), custom_call_target="tpu_custom_call" | custom-call | flops 1073741824 | bytes 7340032 | tf_op jit(solution)/shard_map/second_stage/pallas_call | solution.py:219
  148.5 17.9 %all_to_all.21 = bf16[4,512,256]{2,1,0:T(8,128)(2,1)S(1)} all-to-all(bf16[4,512,256]{2,1,0:T(8,128)(2,1)} %bitcast.18), channel_id=1, replica_groups=mesh['chan'=16,'ket'=4,'bra'=4] {'bra'}, dimensions={0} | all-to-all | bytes 2097152 | tf_op jit(solution)/shard_map/all_to_all | solution.py:276
  166.4 0.1 convert_reduce_fusion
  166.6 0.0 reduce-scatter.2.cloned.1.call-done
  166.6 1.0 convert_element_type.19
  167.6 1.1 maximum_bitcast_fusion
  (20 shorter events, 0.1 us)
Async XLA Ops:
  6.5 57.8 %all-gather.5.cloned.1.call-start = ((), (), s32[]{:S(2)}) async-start(), calls=%async_computation.6 | async-start | bytes 5570560 | tf_op jit(solution)/shard_map/all_gather | solution.py:255
  8.7 106.0 %all-gather.7.cloned.1.call-start = ((), (), s32[]{:S(2)}) async-start(), calls=%async_computation.7 | async-start | bytes 5242880 | tf_op jit(solution)/shard_map/all_gather | solution.py:268
  38.7 28.1 %copy-start = (bf16[16,32,512]{2,1,0:T(8,128)(2,1)}, bf16[16,32,512]{2,1,0:T(8,128)(2,1)S(1)}, u32[]{:S(2)}) copy-start(bf16[16,32,512]{2,1,0:T(8,128)(2,1)S(1)} %all_to_all.20) | copy-start | bytes 1572868
  38.7 13.1 %collective-permute-start.1 = (bf16[512,512]{1,0:T(8,128)(2,1)S(1)}, bf16[512,512]{1,0:T(8,128)(2,1)S(1)}, u32[]{:S(2)}, u32[]{:S(2)}) collective-permute-start(bf16[512,512]{1,0:T(8,128)(2,1)S(1)} %bitcast.14), channel_id=1, source_target_pairs={{0,12},{4,0},{8,4},{12,8},{1,13},{5,1},{9,5},{13,9},{2,14},{6,2},{... | collective-permute-start | bytes 1572872 | tf_op jit(solution)/shard_map/ppermute | solution.py:262
  41.6 14.0 %collective-permute-start = (bf16[512,512]{1,0:T(8,128)(2,1)S(1)}, bf16[512,512]{1,0:T(8,128)(2,1)S(1)}, u32[]{:S(2)}, u32[]{:S(2)}) collective-permute-start(bf16[512,512]{1,0:T(8,128)(2,1)S(1)} %bitcast.15), channel_id=1, source_target_pairs={{0,4},{4,8},{8,12},{12,0},{1,5},{5,9},{9,13},{13,1},{2,6},{6,10},{... | collective-permute-start | bytes 1572872 | tf_op jit(solution)/shard_map/ppermute | solution.py:261
  51.7 15.1 %copy-start.3 = (bf16[512,512]{1,0:T(8,128)(2,1)}, bf16[512,512]{1,0:T(8,128)(2,1)S(1)}, u32[]{:S(2)}) copy-start(bf16[512,512]{1,0:T(8,128)(2,1)S(1)} %collective-permute-done.1.e2) | copy-start | bytes 1572868
  51.8 8.9 %collective-permute-start.3 = (bf16[256,512]{1,0:T(8,128)(2,1)S(1)}, bf16[256,512]{1,0:T(8,128)(2,1)S(1)}, u32[]{:S(2)}, u32[]{:S(2)}) collective-permute-start(bf16[256,512]{1,0:T(8,128)(2,1)S(1)} %slice.13), channel_id=1, source_target_pairs={{0,12},{4,0},{8,4},{12,8},{1,13},{5,1},{9,5},{13,9},{2,14},{6,2},{... | collective-permute-start | bytes 786440 | tf_op jit(solution)/shard_map/ppermute | solution.py:264
  55.5 11.3 %copy-start.4 = (bf16[512,512]{1,0:T(8,128)(2,1)}, bf16[512,512]{1,0:T(8,128)(2,1)S(1)}, u32[]{:S(2)}) copy-start(bf16[512,512]{1,0:T(8,128)(2,1)S(1)} %collective-permute-done.e1) | copy-start | bytes 1572868
  55.6 8.8 %collective-permute-start.2 = (bf16[256,512]{1,0:T(8,128)(2,1)S(1)}, bf16[256,512]{1,0:T(8,128)(2,1)S(1)}, u32[]{:S(2)}, u32[]{:S(2)}) collective-permute-start(bf16[256,512]{1,0:T(8,128)(2,1)S(1)} %slice.12), channel_id=1, source_target_pairs={{0,4},{4,8},{8,12},{12,0},{1,5},{5,9},{9,13},{13,1},{2,6},{6,10},{... | collective-permute-start | bytes 786440 | tf_op jit(solution)/shard_map/ppermute | solution.py:263
  60.6 6.2 %copy-start.5 = (bf16[256,512]{1,0:T(8,128)(2,1)}, bf16[256,512]{1,0:T(8,128)(2,1)S(1)}, u32[]{:S(2)}) copy-start(bf16[256,512]{1,0:T(8,128)(2,1)S(1)} %collective-permute-done.3.e3b) | copy-start | bytes 786436
  64.3 2.5 %copy-start.6 = (bf16[256,512]{1,0:T(8,128)(2,1)}, bf16[256,512]{1,0:T(8,128)(2,1)S(1)}, u32[]{:S(2)}) copy-start(bf16[256,512]{1,0:T(8,128)(2,1)S(1)} %collective-permute-done.2.e3a) | copy-start | bytes 786436
  73.5 34.0 %all-to-all-start.1 = ((bf16[16,128,256]{2,1,0:T(8,128)(2,1)}), bf16[16,128,256]{2,1,0:T(8,128)(2,1)S(1)}, u32[]{:S(2)}, u32[]{:S(2)}) async-start(bf16[16,128,256]{2,1,0:T(8,128)(2,1)} %first_stage.2), calls=%async_computation.1 | async-start | bytes 2097152 | tf_op jit(solution)/shard_map/all_to_all | solution.py:273
  107.4 7.3 %copy-start.1 = (bf16[16,128,256]{2,1,0:T(8,128)(2,1)}, bf16[16,128,256]{2,1,0:T(8,128)(2,1)S(1)}, u32[]{:S(2)}) copy-start(bf16[16,128,256]{2,1,0:T(8,128)(2,1)S(1)} %all-to-all-done.1.got) | copy-start | bytes 3145732
  107.5 31.4 %all-to-all-start.2 = ((bf16[16,128,256]{2,1,0:T(8,128)(2,1)}), bf16[16,128,256]{2,1,0:T(8,128)(2,1)S(1)}, u32[]{:S(2)}, u32[]{:S(2)}) async-start(bf16[16,128,256]{2,1,0:T(8,128)(2,1)} %first_stage.3), calls=%async_computation.3 | async-start | bytes 2097152 | tf_op jit(solution)/shard_map/all_to_all | solution.py:273
  111.0 55.6 %reduce-scatter.2.cloned.1.call-start = ((), (), s32[]{:S(2)}) async-start(), calls=%async_computation.5 | async-start | bytes 1310720 | tf_op jit(solution)/shard_map/reduce_scatter | solution.py:275
  138.9 1.0 copy-start.2
Sparse Core Ops, SparseCore 0:
  9.2 52.9 all-gather.4
  66.9 47.7 all-gather.6
  123.6 24.3 reduce-scatter.1

commit v4 on v3

v4 whole, which is shorter than its diff:
```python
import functools

import jax
import jax.numpy as jnp
from jax import lax
from jax.experimental import pallas as pl
from jax.experimental.pallas import tpu as pltpu
from jax.sharding import PartitionSpec as P

BF16 = jnp.bfloat16
F32 = jnp.float32
PHYS = (0, 1, 1, 2)
PLANE = (0, 0, 1, 0)
WIDTH = 256


def spread_coupling(op_in, op_out, op_bra, op_ket, op_code):
    rows = jnp.arange(1024, dtype=jnp.int32)
    pick_out = (rows[:, None] // 16 == (op_out * 4 + op_bra)[None, :]).astype(BF16)
    weights = op_code.astype(F32) * 0.25
    hit = (op_ket * 16 + op_in)[:, None] == rows[None, :] // 16
    pick_in = jnp.where(hit, weights[:, None], 0.0).astype(BF16)
    table = jnp.dot(pick_out, pick_in, preferred_element_type=F32)
    same = rows[:, None] % 16 == rows[None, :] % 16
    return jnp.where(same, table, 0.0).astype(BF16)


def charge_row(charges, block):
    return charges[pl.ds(block, 1), :].astype(F32)


def charge_column(charges, block):
    return jnp.transpose(jnp.broadcast_to(charge_row(charges, block), (128, 128)))


def chosen(x, diff):
    diff = diff.astype(BF16)
    return jnp.where(diff == 0, x[0], jnp.where(diff == 1, x[1], x[3]))


def pack_kernel(ket, bra, left, right, out):
    chan, y, x = lax.axis_index("chan"), lax.axis_index("ket"), lax.axis_index("bra")
    rows = charge_column(left, chan)
    for r in range(4):
        cut = slice(r * 128, (r + 1) * 128)
        diff = charge_row(right, y * 4 + r) - rows
        out[r, 0] = chosen([ket[s, :, cut] for s in range(4)], diff)
        out[r, 1] = ket[2, :, cut]
    own = pl.ds(pl.multiple_of(y * 128, 128), 128)
    diff = charge_row(right, chan) - charge_column(left, x * 4 + y)
    first = chosen([bra[t, own, :] for t in range(4)], diff)
    out[4, 0] = jnp.transpose(first.astype(F32)).astype(BF16)
    out[4, 1] = jnp.transpose(bra[2, own, :].astype(F32)).astype(BF16)


def masked_tiles(parts, rows, cols, charge):
    tiles = []
    for part, col in zip(parts, cols):
        tiles.append(jnp.where(rows + charge == col, part, jnp.zeros_like(part)))
    return jnp.concatenate(tiles, axis=1)


def begin(copies, sems):
    made = [pltpu.make_async_copy(src, dst, sems.at[n]) for n, (src, dst) in enumerate(copies)]
    for copy in made:
        copy.start()
    return made


def first_kernel(
    start, left_s, right_s, e0, e1, e2, e3a, e3b, gathered, left, right, spread,
    out, bra_out, env, planes, bra_planes, column, acc, parts, results, sems, out_sems,
):
    y = lax.axis_index("ket")
    width = acc.shape[1]
    tiles = width // 128
    blocks = [lax.rem(y + n, 4) for n in (0, 3, 1, 2)]
    loads = [(gathered.at[:, pl.ds(start // 128, tiles)], planes)]
    if start == 0:
        loads.append((gathered.at[:, 4], bra_planes))
    loads = begin(loads, sems)
    for h in range(2):
        cut = slice(h * 256, (h + 1) * 256)
        for i, e in enumerate((e0, e1, e2)):
            env[2 * blocks[i] + h] = e[:, cut]
        for n, e in enumerate((e3a, e3b)):
            env[2 * blocks[3] + h, n * 256 : (n + 1) * 256] = e[:, cut]
    for c in range(16):
        column[c * 128 : (c + 1) * 128, :] = charge_column(left, c).astype(BF16)
    at = y * 4 + start // 128
    cols = [charge_row(right, at + r).astype(BF16) for r in range(tiles)]
    least, most = right_s[y * 512 + start], right_s[y * 512 + start + width - 1]
    loads[0].wait()
    for s in range(4):
        acc[...] = jnp.zeros_like(acc)
        low = sum((left_s[256 * i + 255] + PHYS[s] < least).astype(jnp.int32) for i in range(8))
        high = sum((left_s[256 * i] + PHYS[s] <= most).astype(jnp.int32) for i in range(8))

        def step(i, carry):
            pair = []
            for r in range(2):
                rows = column[pl.ds(pl.multiple_of(i * 256 + r * 128, 128), 128), :]
                values = [planes[2 * i + r, q, PLANE[s]] for q in range(tiles)]
                pair.append(masked_tiles(values, rows, cols, PHYS[s]))
            block = jnp.concatenate(pair, axis=0)
            acc[...] += jnp.dot(env[i], block, preferred_element_type=F32)
            return carry

        lax.fori_loop(low, high, step, 0)
        product = acc[...].astype(BF16).reshape(16, 2, 16, width)
        for h in range(2):
            parts[h, s * 256 : (s + 1) * 256, :] = product[:, h].reshape(256, width)
    sent = []
    if start == 0:
        loads[1].wait()
        sent = begin([(bra_planes, bra_out)], out_sems.at[pl.ds(2, 1)])
    for h in range(2):
        mixed = jnp.dot(spread[...], parts[h], preferred_element_type=F32)
        results[h] = mixed.astype(BF16).reshape(16, 64, width)
        copy = pltpu.make_async_copy(results.at[h], out.at[:, pl.ds(h * 64, 64)], out_sems.at[h])
        copy.start()
        sent.append(copy)
    for copy in sent:
        copy.wait()


def active(left_s, right_s, x, g, t, h):
    least, most = right_s[g * 512], right_s[g * 512 + 511]
    first = left_s[x * 512 + h * 256] + PHYS[t]
    last = left_s[x * 512 + h * 256 + 255] + PHYS[t]
    return (first <= most) & (last >= least)


def each_active(left_s, right_s, x, act):
    for g in range(4):
        for t in range(4):
            for h in range(2):

                @pl.when(active(left_s, right_s, x, g, t, h))
                def _():
                    act(g, t * 2 + h)


def tile_copy(source, target, sems, g, n):
    return pltpu.make_async_copy(source.at[g, n], target.at[g, n], sems.at[g * 8 + n])


def mask_kernel(
    left_s, right_s, gathered, left, right, out, planes, tiles, column, sems, out_sems
):
    x = lax.axis_index("bra")
    loads = begin([(gathered.at[:, pl.ds(g * 4, 4)], planes.at[g]) for g in range(4)], sems)
    for c in range(16):
        column[c * 128 : (c + 1) * 128, :] = charge_column(right, c).astype(BF16)
    cols = [charge_row(left, x * 4 + r).astype(BF16) for r in range(4)]
    for g in range(4):
        loads[g].wait()
        for t in range(4):
            for h in range(2):

                @pl.when(active(left_s, right_s, x, g, t, h))
                def _():
                    for r in range(4):
                        rows = column[g * 512 + r * 128 : g * 512 + (r + 1) * 128, :]
                        values = [planes[g, 2 * h + q, r, PLANE[t]] for q in range(2)]
                        tile = masked_tiles(values, rows, cols[2 * h : 2 * h + 2], -PHYS[t])
                        tiles[g, t * 2 + h, r * 128 : (r + 1) * 128, :] = tile
                    tile_copy(tiles, out, out_sems, g, t * 2 + h).start()

    each_active(
        left_s, right_s, x, lambda g, n: tile_copy(tiles, out, out_sems, g, n).wait()
    )


def second_kernel(left_s, right_s, got, masked, out, mixed, acc, tiles, sems):
    x = lax.axis_index("bra")
    each_active(
        left_s, right_s, x, lambda g, n: tile_copy(masked, tiles, sems, g, n).start()
    )
    for j in range(16):
        for h in range(2):
            for t in range(4):
                at = (j % 8) * 32 + h * 16
                mixed[t * 2 + j // 8, at : at + 16, :] = got[j, h * 64 + t * 16 : h * 64 + (t + 1) * 16, :]
    for g in range(4):
        acc[...] = jnp.zeros_like(acc)
        for t in range(4):
            for h in range(2):

                @pl.when(active(left_s, right_s, x, g, t, h))
                def _():
                    n = t * 2 + h
                    tile_copy(masked, tiles, sems, g, n).wait()
                    acc[...] += jnp.dot(tiles[g, n], mixed[n], preferred_element_type=F32)

        out[g * 512 : (g + 1) * 512, :] = acc[...].astype(BF16)


def last_kernel(one, two, out):
    out[0, :, 0:WIDTH] = one[...].astype(F32)
    total = two[0].astype(F32) + two[1].astype(F32)
    out[0, :, WIDTH : 2 * WIDTH] = total + two[2].astype(F32) + two[3].astype(F32)


SCALARS = pl.BlockSpec(memory_space=pltpu.SMEM)
FAST = pl.BlockSpec(memory_space=pltpu.VMEM)
PLACE = pl.BlockSpec(memory_space=pltpu.HBM)
PARAMS = pltpu.CompilerParams(vmem_limit_bytes=24 << 20)


def held(x):
    return pltpu.with_memory_space_constraint(x, pltpu.HBM)


def pack(ket_tensor, bra_tensor, left, right):
    return pl.pallas_call(
        pack_kernel,
        out_shape=jax.ShapeDtypeStruct((5, 2, 128, 128), BF16),
        in_specs=[FAST] * 4,
        out_specs=FAST,
        name="pack",
    )(ket_tensor, bra_tensor, left, right)


def first_stage(charge_left, charge_right, pieces, gathered, left, right, spread, start):
    bra_shape = (16, 2, 128, 128) if start == 0 else (1, 2, 128, 128)
    return pl.pallas_call(
        functools.partial(first_kernel, start),
        out_shape=[
            pltpu.HBM((16, 128, WIDTH), BF16),
            pltpu.HBM(bra_shape, BF16),
        ],
        in_specs=[SCALARS, SCALARS] + [FAST] * len(pieces) + [PLACE] + [FAST] * 3,
        out_specs=[PLACE, PLACE],
        scratch_shapes=[
            pltpu.VMEM((8, 512, 256), BF16),
            pltpu.VMEM((16, WIDTH // 128, 2, 128, 128), BF16),
            pltpu.VMEM(bra_shape, BF16),
            pltpu.VMEM((2048, 128), BF16),
            pltpu.VMEM((512, WIDTH), F32),
            pltpu.VMEM((2, 1024, WIDTH), BF16),
            pltpu.VMEM((2, 16, 64, WIDTH), BF16),
            pltpu.SemaphoreType.DMA((2,)),
            pltpu.SemaphoreType.DMA((3,)),
        ],
        compiler_params=PARAMS,
        cost_estimate=pl.CostEstimate(
            flops=512 * 2048 * 4 * WIDTH, bytes_accessed=8 << 20, transcendentals=0
        ),
        name="first_stage",
    )(charge_left, charge_right, *pieces, held(gathered), left, right, spread)


def mask_bra(charge_left, charge_right, gathered, left, right):
    return pl.pallas_call(
        mask_kernel,
        out_shape=pltpu.HBM((4, 8, 512, 256), BF16),
        in_specs=[SCALARS, SCALARS, PLACE, FAST, FAST],
        out_specs=PLACE,
        scratch_shapes=[
            pltpu.VMEM((4, 4, 4, 2, 128, 128), BF16),
            pltpu.VMEM((4, 8, 512, 256), BF16),
            pltpu.VMEM((2048, 128), BF16),
            pltpu.SemaphoreType.DMA((4,)),
            pltpu.SemaphoreType.DMA((32,)),
        ],
        compiler_params=PARAMS,
        name="mask_bra",
    )(charge_left, charge_right, held(gathered), left, right)


def second_stage(charge_left, charge_right, got, masked):
    return pl.pallas_call(
        second_kernel,
        out_shape=jax.ShapeDtypeStruct((2048, WIDTH), BF16),
        in_specs=[SCALARS, SCALARS, FAST, PLACE],
        out_specs=FAST,
        scratch_shapes=[
            pltpu.VMEM((8, 256, WIDTH), BF16),
            pltpu.VMEM((512, WIDTH), F32),
            pltpu.VMEM((4, 8, 512, 256), BF16),
            pltpu.SemaphoreType.DMA((32,)),
        ],
        compiler_params=PARAMS,
        cost_estimate=pl.CostEstimate(
            flops=2048 * 2048 * WIDTH, bytes_accessed=2 << 20, transcendentals=0
        ),
        name="second_stage",
    )(charge_left, charge_right, got, held(masked))


def last_stage(one, two):
    return pl.pallas_call(
        last_kernel,
        grid=(4,),
        out_shape=jax.ShapeDtypeStruct((1, 512, 2 * WIDTH), F32),
        in_specs=[
            pl.BlockSpec((128, WIDTH), lambda i: (i, 0)),
            pl.BlockSpec((4, 128, WIDTH), lambda i: (0, i, 0)),
        ],
        out_specs=pl.BlockSpec((1, 128, 2 * WIDTH), lambda i: (0, i, 0)),
        name="last_stage",
    )(one, two)


def local(
    environment,
    ket_tensor,
    bra_tensor,
    charge_left,
    charge_right,
    op_in,
    op_out,
    op_bra,
    op_ket,
    op_code,
):
    left, right = charge_left.reshape(16, 128), charge_right.reshape(16, 128)
    planes = pack(ket_tensor, bra_tensor, left, right)
    gathered = lax.all_gather(planes, "chan", axis=0)

    env = lax.all_to_all(environment.reshape(16, 32, 512), "chan", 0, 0, tiled=True)
    env = env.reshape(512, 512)
    up = [(i, (i + 1) % 4) for i in range(4)]
    down = [(i, (i + 3) % 4) for i in range(4)]
    env_below = lax.ppermute(env, "ket", up)
    env_above = lax.ppermute(env, "ket", down)
    far_a = lax.ppermute(env_below[:256], "ket", up)
    far_b = lax.ppermute(env_above[256:], "ket", down)
    spread = spread_coupling(op_in, op_out, op_bra, op_ket, op_code)
    gathered, spread = lax.optimization_barrier((gathered, spread))
    pieces = (env, env_below, env_above, far_a, far_b)
    mixed, bra_quarter = zip(
        *(
            first_stage(charge_left, charge_right, pieces, gathered, left, right, spread, start)
            for start in (0, WIDTH)
        )
    )
    bra_gathered = lax.all_gather(bra_quarter[0], "ket", axis=0)
    masked = mask_bra(charge_left, charge_right, bra_gathered, left, right)
    terms = []
    for part in mixed:
        got = lax.all_to_all(part, "chan", 0, 0, tiled=True)
        terms.append(second_stage(charge_left, charge_right, got, masked))
    one = lax.psum_scatter(terms[0], "bra", scatter_dimension=0, tiled=True)
    two = lax.all_to_all(terms[1].reshape(4, 512, WIDTH), "bra", 0, 0, tiled=True)
    return last_stage(one, two)


def solution(mesh):
    placed = (
        P("chan", "bra", "ket"),
        P(None, "chan", "ket"),
        P(None, "bra", "chan"),
        P(),
        P(),
        P(),
        P(),
        P(),
        P(),
        P(),
    )
    return jax.shard_map(
        local, mesh=mesh, in_specs=placed, out_specs=P("chan", "bra", "ket"), check_vma=False
    )
```

time: 177 us -> 180 us (1.017)
  blocking collectives: 47.9 us -> 54.3 us
  Pallas kernels: 33.9 us -> 37.5 us
  waiting for transfers between devices: 54.6 us -> 52.3 us
  other arithmetic: 3.63 us -> 1.38 us
    all_to_all x2, waiting for transfers between devices: 35.6 us -> 25.5 us  [local(): got = lax.all_to_all(part, 'chan', 0, 0, tiled=True)]
    pallas_call x2 -> x4, Pallas kernels: 14.4 us -> 22.1 us  [the longest x2 14.4 us: first_stage(): pl.pallas_call(functools.partial(first_kernel, start), out_shape=[pltpu.H...]
    all_gather x1, waiting for transfers between devices: 3.65 us -> 10.4 us  [local(): bra_gathered = lax.all_gather(bra_quarter[0], 'ket', axis=0)]
    all_to_all x1, blocking collectives: 17.9 us -> 24.3 us  [local(): lax.all_to_all(terms[1].reshape(4, 512, WIDTH), 'bra', 0, 0, tiled=True)]
    pallas_call x2, Pallas kernels: 17.4 us -> 13.3 us  [second_stage(): pl.pallas_call(second_kernel, out_shape=jax.ShapeDtypeStruct((2048, WIDTH...]
    all_gather x1, waiting for transfers between devices: 0.01 us -> 3.91 us  [local(): gathered = lax.all_gather(planes, 'chan', axis=0)]
    ppermute x1, waiting for transfers between devices: 2.65 us -> 0.01 us  [local(): far_b = lax.ppermute(env_above[256:], 'ket', down)]
    slice x1 -> x0, local copies, waits for them, and re-layouts: 2.44 us -> none  [local(): bra_gathered = lax.all_gather(gathered[:, 4], 'ket', axis=0)]
  transfers between devices with their start and end apart: 9 -> 9, of which waited for: 7 -> 6; matrix products, arithmetic and copies ran while one was open for 2% -> 2% of each run, Pallas kernels for 18% -> 14%
where the time goes in v4:
time: 180 us
  blocking collectives  54.3 us (30%)
  waiting for transfers between devices  52.3 us (29%)
  Pallas kernels  37.5 us (21%)
  starting transfers between devices  16 us (9%)
  between operations  13.2 us (7%)
  local copies, waits for them, and re-layouts  3.69 us (2%)
    all_to_all x1, blocking collectives, local(): lax.all_to_all(environment.reshape(16, 32, 512), 'chan', 0, 0, tiled=True)  30 us
    all_to_all x2, waiting for transfers between devices, local(): got = lax.all_to_all(part, 'chan', 0, 0, tiled=True)  25.5 us
    all_to_all x1, blocking collectives, local(): lax.all_to_all(terms[1].reshape(4, 512, WIDTH), 'bra', 0, 0, tiled=True)  24.3 us
    pallas_call x2, Pallas kernels, first_stage(): pl.pallas_call(functools.partial(first_kernel, start), out_shape=[pltpu.H...  14.4 us
    pallas_call x2, Pallas kernels, second_stage(): pl.pallas_call(second_kernel, out_shape=jax.ShapeDtypeStruct((2048, WIDTH...  13.3 us
    all_gather x1, waiting for transfers between devices, local(): bra_gathered = lax.all_gather(bra_quarter[0], 'ket', axis=0)  10.4 us
    all_to_all x2, starting transfers between devices, local(): got = lax.all_to_all(part, 'chan', 0, 0, tiled=True)  9.49 us
    ppermute x1, waiting for transfers between devices, local(): env_above = lax.ppermute(env, 'ket', down)  8.8 us
  transfers between devices with their start and end apart: 9, of which 6 were waited for; matrix products, arithmetic and copies ran while one was open for 2% of the time, Pallas kernels for 14%

profile of v4, /device:TPU:1, one launch (start us, length us, event | category | flops | bytes accessed | tf_op | source)
XLA Modules:
  0.0 179.7 jit_solution(13269463917313928397)
XLA Ops:
  6.5 2.1 %pack.1 = bf16[5,2,128,128]{3,2,1,0:T(8,128)(2,1)} custom-call(bf16[4,128,512]{2,1,0:T(8,128)(2,1)} %ket.1, bf16[4,512,128]{2,1,0:T(8,128)(2,1)} %bra.1, s32[16,128]{1,0:T(8,128)} %bitcast.12, s32[16,128]{1,0:T(8,128)} %bitcast.16), custom_call_target="tpu_custom_call" | custom-call | tf_op jit(solution)/shard_map/pack/pallas_call | solution.py:216
  8.7 0.0 all-gather.5.cloned.1.call-update
  8.7 0.0 all-gather.7.cloned.1.call-start
  8.7 30.0 %all_to_all.20 = bf16[16,32,512]{2,1,0:T(8,128)(2,1)S(1)} all-to-all(bf16[16,32,512]{2,1,0:T(8,128)(2,1)} %bitcast.23), channel_id=1, replica_groups=mesh['chan'=16,'ket'=4,'bra'=4] {'chan'}, dimensions={0} | all-to-all | bytes 1048576 | tf_op jit(solution)/shard_map/all_to_all | solution.py:322
  38.7 2.9 %collective-permute-start.1 = (bf16[512,512]{1,0:T(8,128)(2,1)S(1)}, bf16[512,512]{1,0:T(8,128)(2,1)S(1)}, u32[]{:S(2)}, u32[]{:S(2)}) collective-permute-start(bf16[512,512]{1,0:T(8,128)(2,1)S(1)} %bitcast.7), channel_id=1, source_target_pairs={{0,12},{4,0},{8,4},{12,8},{1,13},{5,1},{9,5},{13,9},{2,14},{6,2},{... | collective-permute-start | bytes 1572872 | tf_op jit(solution)/shard_map/ppermute | solution.py:327
  41.6 0.7 convert_multiply_fusion
  42.3 0.7 multiply_add_fusion
  43.0 8.8 %collective-permute-done.1.e2 = bf16[512,512]{1,0:T(8,128)(2,1)S(1)} collective-permute-done((bf16[512,512]{1,0:T(8,128)(2,1)S(1)}, bf16[512,512]{1,0:T(8,128)(2,1)S(1)}, u32[]{:S(2)}, u32[]{:S(2)}) %collective-permute-start.1) | collective-permute-done | bytes 524320 | tf_op jit(solution)/shard_map/ppermute | solution.py:327
  51.8 0.7 slice.9
  52.5 3.5 %collective-permute-start.3 = (bf16[256,512]{1,0:T(8,128)(2,1)}, bf16[256,512]{1,0:T(8,128)(2,1)S(1)}, u32[]{:S(2)}, u32[]{:S(2)}) collective-permute-start(bf16[256,512]{1,0:T(8,128)(2,1)} %slice.9), channel_id=1, source_target_pairs={{0,12},{4,0},{8,4},{12,8},{1,13},{5,1},{9,5},{13,9},{2,14},{6,2},{... | collective-permute-start | bytes 786440 | tf_op jit(solution)/shard_map/ppermute | solution.py:329
  56.0 0.8 slice.8
  56.8 0.1 copy-done
  56.9 1.4 select_convert_fusion.spread
  58.3 3.9 %all-gather.5.cloned.1.call-done = bf16[80,2,128,128]{3,2,1,0:T(8,128)(2,1)} async-done(((bf16[5,2,128,128]{3,2,1,0:T(8,128)(2,1)}), bf16[80,2,128,128]{3,2,1,0:T(8,128)(2,1)}) %all-gather.5.cloned.1.call-update) | async-done | bytes 5242896 | tf_op jit(solution)/shard_map/all_gather | solution.py:320
  62.2 3.6 %collective-permute-done.2.e3a = bf16[256,512]{1,0:T(8,128)(2,1)} collective-permute-done((bf16[256,512]{1,0:T(8,128)(2,1)}, bf16[256,512]{1,0:T(8,128)(2,1)}, u32[]{:S(2)}, u32[]{:S(2)}) %collective-permute-start.2) | collective-permute-done | bytes 262176 | tf_op jit(solution)/shard_map/ppermute | solution.py:328
  65.8 1.0 copy-done.1
  66.9 7.2 %first_stage.2 = (bf16[16,128,256]{2,1,0:T(8,128)(2,1)}, bf16[16,2,128,128]{3,2,1,0:T(8,128)(2,1)}) custom-call(s32[2048]{0:T(1024)S(1)} %copy-done.3, s32[2048]{0:T(1024)S(1)} %copy-done.4, bf16[512,512]{1,0:T(8,128)(2,1)S(1)} %bitcast.9, bf16[512,512]{1,0:T(8,128)(2,1)S(1)} %copy-done.1, bf16[512,512]{1,0:T(8,128)(2,1)S(1)} %collective-permute-done.1.e2, ...), custom_call_target="tpu_custom_call" | custom-call | flops 1073741824 | bytes 8388608 | tf_op jit(solution)/shard_map/first_stage/pallas_call | solution.py:227
  74.1 0.0 all-gather.7.cloned.1.call-update
  74.1 5.9 %all-to-all-start.1 = ((bf16[16,128,256]{2,1,0:T(8,128)(2,1)}), bf16[16,128,256]{2,1,0:T(8,128)(2,1)}, u32[]{:S(2)}, u32[]{:S(2)}) async-start(bf16[16,128,256]{2,1,0:T(8,128)(2,1)} %get-tuple-element.12), calls=%async_computation.1 | async-start | bytes 2097152 | tf_op jit(solution)/shard_map/all_to_all | solution.py:343
  80.0 1.0 copy-done.2
  81.1 7.2 %first_stage.3 = (bf16[16,128,256]{2,1,0:T(8,128)(2,1)}, bf16[1,2,128,128]{3,2,1,0:T(8,128)(2,1)}) custom-call(s32[2048]{0:T(1024)S(1)} %copy-done.3, s32[2048]{0:T(1024)S(1)} %copy-done.4, bf16[512,512]{1,0:T(8,128)(2,1)S(1)} %bitcast.10, bf16[512,512]{1,0:T(8,128)(2,1)S(1)} %copy-done.2, bf16[512,512]{1,0:T(8,128)(2,1)S(1)} %collective-permute-done.1.e2, ...), custom_call_target="tpu_custom_call" | custom-call | flops 1073741824 | bytes 8388608 | tf_op jit(solution)/shard_map/first_stage/pallas_call | solution.py:227
  88.3 19.9 %all-to-all-done.1.got = bf16[16,128,256]{2,1,0:T(8,128)(2,1)} async-done(((bf16[16,128,256]{2,1,0:T(8,128)(2,1)}), bf16[16,128,256]{2,1,0:T(8,128)(2,1)}, u32[]{:S(2)}, u32[]{:S(2)}) %all-to-all-start.1) | async-done | bytes 1048608 | tf_op jit(solution)/shard_map/all_to_all | solution.py:343
  108.1 3.6 %all-to-all-start.2 = ((bf16[16,128,256]{2,1,0:T(8,128)(2,1)}), bf16[16,128,256]{2,1,0:T(8,128)(2,1)S(1)}, u32[]{:S(2)}, u32[]{:S(2)}) async-start(bf16[16,128,256]{2,1,0:T(8,128)(2,1)} %get-tuple-element.14), calls=%async_computation.3 | async-start | bytes 2097152 | tf_op jit(solution)/shard_map/all_to_all | solution.py:343
  111.7 0.0 reduce-scatter.2.cloned.1.call-start
  111.7 10.4 %all-gather.7.cloned.1.call-done = bf16[64,2,128,128]{3,2,1,0:T(8,128)(2,1)} async-done(((bf16[16,2,128,128]{3,2,1,0:T(8,128)(2,1)}), bf16[64,2,128,128]{3,2,1,0:T(8,128)(2,1)}) %all-gather.7.cloned.1.call-update) | async-done | bytes 4194320 | tf_op jit(solution)/shard_map/all_gather | solution.py:339
  122.1 4.3 %mask_bra.1.masked = bf16[4,8,512,256]{3,2,1,0:T(8,128)(2,1)} custom-call(s32[2048]{0:T(1024)S(1)} %copy-done.3, s32[2048]{0:T(1024)S(1)} %copy-done.4, bf16[4,16,2,128,128]{4,3,2,1,0:T(8,128)(2,1)} %bitcast.22, s32[16,128]{1,0:T(8,128)S(1)} %bitcast.15, s32[16,128]{1,0:T(8,128)S(1)} %bitcast.19), custom_call_target="tpu_custom_call" | custom-call | tf_op jit(solution)/shard_map/mask_bra/pallas_call | solution.py:255
  126.4 7.5 %second_stage.2 = bf16[2048,256]{1,0:T(8,128)(2,1)} custom-call(s32[2048]{0:T(1024)S(1)} %copy-done.3, s32[2048]{0:T(1024)S(1)} %copy-done.4, bf16[16,128,256]{2,1,0:T(8,128)(2,1)} %all-to-all-done.1.got, bf16[4,8,512,256]{3,2,1,0:T(8,128)(2,1)} %mask_bra.1.masked), custom_call_target="tpu_custom_call" | custom-call | flops 1073741824 | bytes 2097152 | tf_op jit(solution)/shard_map/second_stage/pallas_call | solution.py:273
  133.9 0.0 reduce-scatter.2.cloned.1.call-update
  133.9 5.6 %all-to-all-done.2.got = bf16[16,128,256]{2,1,0:T(8,128)(2,1)S(1)} async-done(((bf16[16,128,256]{2,1,0:T(8,128)(2,1)}), bf16[16,128,256]{2,1,0:T(8,128)(2,1)S(1)}, u32[]{:S(2)}, u32[]{:S(2)}) %all-to-all-start.2) | async-done | bytes 1048608 | tf_op jit(solution)/shard_map/all_to_all | solution.py:343
  139.6 5.8 %second_stage.3 = bf16[2048,256]{1,0:T(8,128)(2,1)S(1)} custom-call(s32[2048]{0:T(1024)S(1)} %copy-done.3, s32[2048]{0:T(1024)S(1)} %copy-done.4, bf16[16,128,256]{2,1,0:T(8,128)(2,1)S(1)} %all-to-all-done.2.got, bf16[4,8,512,256]{3,2,1,0:T(8,128)(2,1)} %mask_bra.1.masked), custom_call_target="tpu_custom_call" | custom-call | flops 1073741824 | bytes 2097152 | tf_op jit(solution)/shard_map/second_stage/pallas_call | solution.py:273
  145.4 24.3 %all_to_all.21.two = bf16[4,512,256]{2,1,0:T(8,128)(2,1)} all-to-all(bf16[4,512,256]{2,1,0:T(8,128)(2,1)S(1)} %bitcast.11), channel_id=1, replica_groups=mesh['chan'=16,'ket'=4,'bra'=4] {'bra'}, dimensions={0} | all-to-all | bytes 2097152 | tf_op jit(solution)/shard_map/all_to_all | solution.py:346
  169.7 3.5 %last_stage.1 = f32[1,512,512]{2,1,0:T(8,128)} custom-call(bf16[512,256]{1,0:T(8,128)(2,1)} %reduce-scatter.2.cloned.1.call-done.one, bf16[4,512,256]{2,1,0:T(8,128)(2,1)} %all_to_all.21.two), custom_call_target="tpu_custom_call" | custom-call | tf_op jit(solution)/shard_map/last_stage/pallas_call | solution.py:293
  (14 shorter events, 0.0 us)
Async XLA Ops:
  6.5 59.3 %copy-start.3 = (s32[2048]{0:T(1024)S(1)}, s32[2048]{0:T(1024)}, u32[]{:S(2)}) copy-start(s32[2048]{0:T(1024)} %left_s.9) | copy-start | bytes 24580
  6.5 59.3 %copy-start.4 = (s32[2048]{0:T(1024)S(1)}, s32[2048]{0:T(1024)}, u32[]{:S(2)}) copy-start(s32[2048]{0:T(1024)} %right_s.9) | copy-start | bytes 24580
  6.5 55.7 %all-gather.5.cloned.1.call-start = ((), (), s32[]{:S(2)}) async-start(), calls=%async_computation.6 | async-start | bytes 5570560 | tf_op jit(solution)/shard_map/all_gather | solution.py:320
  8.7 113.4 %all-gather.7.cloned.1.call-start = ((), (), s32[]{:S(2)}) async-start(), calls=%async_computation.7 | async-start | bytes 5242880 | tf_op jit(solution)/shard_map/all_gather | solution.py:339
  38.7 13.1 %collective-permute-start.1 = (bf16[512,512]{1,0:T(8,128)(2,1)S(1)}, bf16[512,512]{1,0:T(8,128)(2,1)S(1)}, u32[]{:S(2)}, u32[]{:S(2)}) collective-permute-start(bf16[512,512]{1,0:T(8,128)(2,1)S(1)} %bitcast.7), channel_id=1, source_target_pairs={{0,12},{4,0},{8,4},{12,8},{1,13},{5,1},{9,5},{13,9},{2,14},{6,2},{... | collective-permute-start | bytes 1572872 | tf_op jit(solution)/shard_map/ppermute | solution.py:327
  41.6 14.4 %collective-permute-start = (bf16[512,512]{1,0:T(8,128)(2,1)S(1)}, bf16[512,512]{1,0:T(8,128)(2,1)S(1)}, u32[]{:S(2)}, u32[]{:S(2)}) collective-permute-start(bf16[512,512]{1,0:T(8,128)(2,1)S(1)} %bitcast.8), channel_id=1, source_target_pairs={{0,4},{4,8},{8,12},{12,0},{1,5},{5,9},{9,13},{13,1},{2,6},{6,10},{... | collective-permute-start | bytes 1572872 | tf_op jit(solution)/shard_map/ppermute | solution.py:326
  52.5 9.7 %collective-permute-start.3 = (bf16[256,512]{1,0:T(8,128)(2,1)}, bf16[256,512]{1,0:T(8,128)(2,1)S(1)}, u32[]{:S(2)}, u32[]{:S(2)}) collective-permute-start(bf16[256,512]{1,0:T(8,128)(2,1)} %slice.9), channel_id=1, source_target_pairs={{0,12},{4,0},{8,4},{12,8},{1,13},{5,1},{9,5},{13,9},{2,14},{6,2},{... | collective-permute-start | bytes 786440 | tf_op jit(solution)/shard_map/ppermute | solution.py:329
  56.0 0.9 copy-start
  56.8 9.0 %collective-permute-start.2 = (bf16[256,512]{1,0:T(8,128)(2,1)}, bf16[256,512]{1,0:T(8,128)(2,1)}, u32[]{:S(2)}, u32[]{:S(2)}) collective-permute-start(bf16[256,512]{1,0:T(8,128)(2,1)} %slice.8), channel_id=1, source_target_pairs={{0,4},{4,8},{8,12},{12,0},{1,5},{5,9},{9,13},{13,1},{2,6},{6,10},{... | collective-permute-start | bytes 786440 | tf_op jit(solution)/shard_map/ppermute | solution.py:328
  65.8 1.0 copy-start.1
  74.1 34.0 %all-to-all-start.1 = ((bf16[16,128,256]{2,1,0:T(8,128)(2,1)}), bf16[16,128,256]{2,1,0:T(8,128)(2,1)}, u32[]{:S(2)}, u32[]{:S(2)}) async-start(bf16[16,128,256]{2,1,0:T(8,128)(2,1)} %get-tuple-element.12), calls=%async_computation.1 | async-start | bytes 2097152 | tf_op jit(solution)/shard_map/all_to_all | solution.py:343
  80.0 1.0 copy-start.2
  108.1 31.4 %all-to-all-start.2 = ((bf16[16,128,256]{2,1,0:T(8,128)(2,1)}), bf16[16,128,256]{2,1,0:T(8,128)(2,1)S(1)}, u32[]{:S(2)}, u32[]{:S(2)}) async-start(bf16[16,128,256]{2,1,0:T(8,128)(2,1)} %get-tuple-element.14), calls=%async_computation.3 | async-start | bytes 2097152 | tf_op jit(solution)/shard_map/all_to_all | solution.py:343
  111.7 58.0 %reduce-scatter.2.cloned.1.call-start = ((), (), s32[]{:S(2)}) async-start(), calls=%async_computation.5 | async-start | bytes 1310720 | tf_op jit(solution)/shard_map/reduce_scatter | solution.py:345
Sparse Core Ops, SparseCore 0:
  9.2 52.9 all-gather.4
  74.2 47.8 all-gather.6
  134.0 31.8 reduce-scatter.1

commit v5 on v4

--- a/solution.py
+++ b/solution.py
@@ -15,13 +15,13 @@
 
 
 def spread_coupling(op_in, op_out, op_bra, op_ket, op_code):
-    rows = jnp.arange(1024, dtype=jnp.int32)
-    pick_out = (rows[:, None] // 16 == (op_out * 4 + op_bra)[None, :]).astype(BF16)
+    rows = jnp.arange(512, dtype=jnp.int32)
+    pick_out = (rows[:, None] // 8 == (op_out * 4 + op_bra)[None, :]).astype(BF16)
     weights = op_code.astype(F32) * 0.25
-    hit = (op_ket * 16 + op_in)[:, None] == rows[None, :] // 16
+    hit = (op_ket * 16 + op_in)[:, None] == rows[None, :] // 8
     pick_in = jnp.where(hit, weights[:, None], 0.0).astype(BF16)
     table = jnp.dot(pick_out, pick_in, preferred_element_type=F32)
-    same = rows[:, None] % 16 == rows[None, :] % 16
+    same = rows[:, None] % 8 == rows[None, :] % 8
     return jnp.where(same, table, 0.0).astype(BF16)
 
 
@@ -69,28 +69,29 @@
 
 def first_kernel(
     start, left_s, right_s, e0, e1, e2, e3a, e3b, gathered, left, right, spread,
-    out, bra_out, env, planes, bra_planes, column, acc, parts, results, sems, out_sems,
+    out, env, planes, table, column, acc, parts, results, sems, out_sems,
 ):
     y = lax.axis_index("ket")
     width = acc.shape[1]
     tiles = width // 128
     blocks = [lax.rem(y + n, 4) for n in (0, 3, 1, 2)]
-    loads = [(gathered.at[:, pl.ds(start // 128, tiles)], planes)]
-    if start == 0:
-        loads.append((gathered.at[:, 4], bra_planes))
-    loads = begin(loads, sems)
+    copies = [(gathered.at[:, pl.ds(start // 128, tiles)], planes)]
     for h in range(2):
-        cut = slice(h * 256, (h + 1) * 256)
-        for i, e in enumerate((e0, e1, e2)):
-            env[2 * blocks[i] + h] = e[:, cut]
-        for n, e in enumerate((e3a, e3b)):
-            env[2 * blocks[3] + h, n * 256 : (n + 1) * 256] = e[:, cut]
+        cut = pl.ds(h * 256, 256)
+        copies += [(e.at[:, cut], env.at[2 * blocks[i] + h]) for i, e in enumerate((e0, e1, e2))]
+        copies += [
+            (e.at[:, cut], env.at[2 * blocks[3] + h, pl.ds(n * 256, 256)])
+            for n, e in enumerate((e3a, e3b))
+        ]
+    copies.append((spread, table))
+    copies = begin(copies, sems)
     for c in range(16):
         column[c * 128 : (c + 1) * 128, :] = charge_column(left, c).astype(BF16)
     at = y * 4 + start // 128
     cols = [charge_row(right, at + r).astype(BF16) for r in range(tiles)]
     least, most = right_s[y * 512 + start], right_s[y * 512 + start + width - 1]
-    loads[0].wait()
+    for copy in copies[:-1]:
+        copy.wait()
     for s in range(4):
         acc[...] = jnp.zeros_like(acc)
         low = sum((left_s[256 * i + 255] + PHYS[s] < least).astype(jnp.int32) for i in range(8))
@@ -107,17 +108,31 @@
             return carry
 
         lax.fori_loop(low, high, step, 0)
-        product = acc[...].astype(BF16).reshape(16, 2, 16, width)
-        for h in range(2):
-            parts[h, s * 256 : (s + 1) * 256, :] = product[:, h].reshape(256, width)
+        product = acc[...].reshape(16, 4, 8, width)
+        for g in range(4):
+            parts[g, s * 128 : (s + 1) * 128, :] = product[:, g].reshape(128, width).astype(BF16)
+    copies[-1].wait()
     sent = []
-    if start == 0:
-        loads[1].wait()
-        sent = begin([(bra_planes, bra_out)], out_sems.at[pl.ds(2, 1)])
     for h in range(2):
-        mixed = jnp.dot(spread[...], parts[h], preferred_element_type=F32)
-        results[h] = mixed.astype(BF16).reshape(16, 64, width)
+        pair = [
+            jnp.dot(table[...], parts[g], preferred_element_type=F32).reshape(16, 4, 8, width)
+            for g in (2 * h, 2 * h + 1)
+        ]
+        results[h] = jnp.stack(pair, axis=2).reshape(16, 64, width).astype(BF16)
         copy = pltpu.make_async_copy(results.at[h], out.at[:, pl.ds(h * 64, 64)], out_sems.at[h])
+        copy.start()
+        sent.append(copy)
+    for copy in sent:
+        copy.wait()
+
+
+def cut_kernel(gathered, out, held, sems, out_sems):
+    parts = [pl.ds(n * 4, 4) for n in range(4)]
+    loads = begin([(gathered.at[p, 4], held.at[p]) for p in parts], sems)
+    sent = []
+    for n, load in enumerate(loads):
+        load.wait()
+        copy = pltpu.make_async_copy(held.at[parts[n]], out.at[parts[n]], out_sems.at[n])
         copy.start()
         sent.append(copy)
     for copy in sent:
@@ -196,15 +211,9 @@
         out[g * 512 : (g + 1) * 512, :] = acc[...].astype(BF16)
 
 
-def last_kernel(one, two, out):
-    out[0, :, 0:WIDTH] = one[...].astype(F32)
-    total = two[0].astype(F32) + two[1].astype(F32)
-    out[0, :, WIDTH : 2 * WIDTH] = total + two[2].astype(F32) + two[3].astype(F32)
-
-
 SCALARS = pl.BlockSpec(memory_space=pltpu.SMEM)
 FAST = pl.BlockSpec(memory_space=pltpu.VMEM)
-PLACE = pl.BlockSpec(memory_space=pltpu.HBM)
+PLACE = pl.BlockSpec(memory_space=pl.ANY)
 PARAMS = pltpu.CompilerParams(vmem_limit_bytes=24 << 20)
 
 
@@ -223,32 +232,42 @@
 
 
 def first_stage(charge_left, charge_right, pieces, gathered, left, right, spread, start):
-    bra_shape = (16, 2, 128, 128) if start == 0 else (1, 2, 128, 128)
     return pl.pallas_call(
         functools.partial(first_kernel, start),
-        out_shape=[
-            pltpu.HBM((16, 128, WIDTH), BF16),
-            pltpu.HBM(bra_shape, BF16),
-        ],
-        in_specs=[SCALARS, SCALARS] + [FAST] * len(pieces) + [PLACE] + [FAST] * 3,
-        out_specs=[PLACE, PLACE],
+        out_shape=jax.ShapeDtypeStruct((16, 128, WIDTH), BF16),
+        in_specs=[SCALARS, SCALARS] + [PLACE] * (len(pieces) + 1) + [FAST, FAST, PLACE],
+        out_specs=PLACE,
         scratch_shapes=[
             pltpu.VMEM((8, 512, 256), BF16),
             pltpu.VMEM((16, WIDTH // 128, 2, 128, 128), BF16),
-            pltpu.VMEM(bra_shape, BF16),
+            pltpu.VMEM((512, 512), BF16),
             pltpu.VMEM((2048, 128), BF16),
             pltpu.VMEM((512, WIDTH), F32),
-            pltpu.VMEM((2, 1024, WIDTH), BF16),
+            pltpu.VMEM((4, 512, WIDTH), BF16),
             pltpu.VMEM((2, 16, 64, WIDTH), BF16),
+            pltpu.SemaphoreType.DMA((12,)),
             pltpu.SemaphoreType.DMA((2,)),
-            pltpu.SemaphoreType.DMA((3,)),
         ],
-        compiler_params=PARAMS,
         cost_estimate=pl.CostEstimate(
             flops=512 * 2048 * 4 * WIDTH, bytes_accessed=8 << 20, transcendentals=0
         ),
         name="first_stage",
-    )(charge_left, charge_right, *pieces, held(gathered), left, right, spread)
+    )(charge_left, charge_right, *pieces, gathered, left, right, spread)
+
+
+def cut_bra(gathered):
+    return pl.pallas_call(
+        cut_kernel,
+        out_shape=jax.ShapeDtypeStruct((16, 2, 128, 128), BF16),
+        in_specs=[PLACE],
+        out_specs=PLACE,
+        scratch_shapes=[
+            pltpu.VMEM((16, 2, 128, 128), BF16),
+            pltpu.SemaphoreType.DMA((4,)),
+            pltpu.SemaphoreType.DMA((4,)),
+        ],
+        name="cut_bra",
+    )(gathered)
 
 
 def mask_bra(charge_left, charge_right, gathered, left, right):
@@ -264,7 +283,6 @@
             pltpu.SemaphoreType.DMA((4,)),
             pltpu.SemaphoreType.DMA((32,)),
         ],
-        compiler_params=PARAMS,
         name="mask_bra",
     )(charge_left, charge_right, held(gathered), left, right)
 
@@ -289,20 +307,6 @@
     )(charge_left, charge_right, got, held(masked))
 
 
-def last_stage(one, two):
-    return pl.pallas_call(
-        last_kernel,
-        grid=(4,),
-        out_shape=jax.ShapeDtypeStruct((1, 512, 2 * WIDTH), F32),
-        in_specs=[
-            pl.BlockSpec((128, WIDTH), lambda i: (i, 0)),
-            pl.BlockSpec((4, 128, WIDTH), lambda i: (0, i, 0)),
-        ],
-        out_specs=pl.BlockSpec((1, 128, 2 * WIDTH), lambda i: (0, i, 0)),
-        name="last_stage",
-    )(one, two)
-
-
 def local(
     environment,
     ket_tensor,
@@ -328,23 +332,19 @@
     far_a = lax.ppermute(env_below[:256], "ket", up)
     far_b = lax.ppermute(env_above[256:], "ket", down)
     spread = spread_coupling(op_in, op_out, op_bra, op_ket, op_code)
-    gathered, spread = lax.optimization_barrier((gathered, spread))
     pieces = (env, env_below, env_above, far_a, far_b)
-    mixed, bra_quarter = zip(
-        *(
-            first_stage(charge_left, charge_right, pieces, gathered, left, right, spread, start)
-            for start in (0, WIDTH)
-        )
-    )
-    bra_gathered = lax.all_gather(bra_quarter[0], "ket", axis=0)
+    gathered, spread, pieces = lax.optimization_barrier((gathered, spread, pieces))
+    bra_gathered = lax.all_gather(cut_bra(gathered), "ket", axis=0)
     masked = mask_bra(charge_left, charge_right, bra_gathered, left, right)
     terms = []
-    for part in mixed:
-        got = lax.all_to_all(part, "chan", 0, 0, tiled=True)
+    for start in (0, WIDTH):
+        mixed = first_stage(charge_left, charge_right, pieces, gathered, left, right, spread, start)
+        got = lax.all_to_all(mixed, "chan", 0, 0, tiled=True)
         terms.append(second_stage(charge_left, charge_right, got, masked))
-    one = lax.psum_scatter(terms[0], "bra", scatter_dimension=0, tiled=True)
+    one = lax.psum_scatter(terms[0], "bra", scatter_dimension=0, tiled=True).astype(F32)
     two = lax.all_to_all(terms[1].reshape(4, 512, WIDTH), "bra", 0, 0, tiled=True)
-    return last_stage(one, two)
+    two = jnp.sum(two.astype(F32), axis=0)
+    return jnp.concatenate([one, two], axis=1)[None]
 
 
 def solution(mesh):

time: 180 us -> 173 us (0.961)
  blocking collectives: 54.3 us -> 48.8 us
  local copies, waits for them, and re-layouts: 3.69 us -> 0.06 us
  other arithmetic: 1.38 us -> 3.63 us
  Pallas kernels: 37.5 us -> 35.6 us
    all_to_all x2, waiting for transfers between devices: 25.5 us -> 34.1 us  [local(): got = lax.all_to_all(mixed, 'chan', 0, 0, tiled=True)]
    all_gather x1, waiting for transfers between devices: 10.4 us -> 3.19 us  [local(): bra_gathered = lax.all_gather(cut_bra(gathered), 'ket', axis=0)]
    all_to_all x1, blocking collectives: 24.3 us -> 18.8 us  [local(): lax.all_to_all(terms[1].reshape(4, 512, WIDTH), 'bra', 0, 0, tiled=True)]
    all_gather x1, waiting for transfers between devices: 3.91 us -> 0.01 us  [local(): gathered = lax.all_gather(planes, 'chan', axis=0)]
    ppermute x1, waiting for transfers between devices: 0.01 us -> 3.79 us  [local(): far_b = lax.ppermute(env_above[256:], 'ket', down)]
    unnamed x10 -> x14, local copies, waits for them, and re-layouts: 2.21 us -> 0.03 us
    pallas_call x3, Pallas kernels: 17.9 us -> 16 us  [the longest x2 13.9 us: first_stage(): pl.pallas_call(functools.partial(first_kernel, start), out_shape=jax.Shap...]
  transfers between devices with their start and end apart: 9 -> 9, of which waited for: 6 -> 7; matrix products, arithmetic and copies ran while one was open for 2% -> 2% of each run, Pallas kernels for 14% -> 18%
where the time goes in v5:
time: 173 us
  waiting for transfers between devices  53.8 us (31%)
  blocking collectives  48.8 us (28%)
  Pallas kernels  35.6 us (21%)
  starting transfers between devices  16.2 us (9%)
  between operations  13.3 us (8%)
  other arithmetic  3.63 us (2%)
    all_to_all x2, waiting for transfers between devices, local(): got = lax.all_to_all(mixed, 'chan', 0, 0, tiled=True)  34.1 us
    all_to_all x1, blocking collectives, local(): lax.all_to_all(environment.reshape(16, 32, 512), 'chan', 0, 0, tiled=True)  30 us
    all_to_all x1, blocking collectives, local(): lax.all_to_all(terms[1].reshape(4, 512, WIDTH), 'bra', 0, 0, tiled=True)  18.8 us
    pallas_call x2, Pallas kernels, first_stage(): pl.pallas_call(functools.partial(first_kernel, start), out_shape=jax.Shap...  13.9 us
    pallas_call x2, Pallas kernels, second_stage(): pl.pallas_call(second_kernel, out_shape=jax.ShapeDtypeStruct((2048, WIDTH...  13 us
    all_to_all x2, starting transfers between devices, local(): got = lax.all_to_all(mixed, 'chan', 0, 0, tiled=True)  9.52 us
    ppermute x1, waiting for transfers between devices, local(): env_above = lax.ppermute(env, 'ket', down)  8.79 us
    pallas_call x1, Pallas kernels, mask_bra(): pl.pallas_call(mask_kernel, out_shape=pltpu.HBM((4, 8, 512, 256), BF16),...  4.54 us
  transfers between devices with their start and end apart: 9, of which 7 were waited for; matrix products, arithmetic and copies ran while one was open for 2% of the time, Pallas kernels for 18%

profile of v5, /device:TPU:1, one launch (start us, length us, event | category | flops | bytes accessed | tf_op | source)
XLA Modules:
  0.0 172.5 jit_solution(9373780383041297145)
XLA Ops:
  6.5 2.1 %pack.1 = bf16[5,2,128,128]{3,2,1,0:T(8,128)(2,1)} custom-call(bf16[4,128,512]{2,1,0:T(8,128)(2,1)} %ket.1, bf16[4,512,128]{2,1,0:T(8,128)(2,1)} %bra.1, s32[16,128]{1,0:T(8,128)} %bitcast.10, s32[16,128]{1,0:T(8,128)} %bitcast.14), custom_call_target="tpu_custom_call" | custom-call | tf_op jit(solution)/shard_map/pack/pallas_call | solution.py:225
  8.7 0.0 all-gather.7.cloned.1.call-start
  8.7 30.0 %all_to_all.20 = bf16[16,32,512]{2,1,0:T(8,128)(2,1)S(1)} all-to-all(bf16[16,32,512]{2,1,0:T(8,128)(2,1)} %bitcast.26), channel_id=1, replica_groups=mesh['chan'=16,'ket'=4,'bra'=4] {'chan'}, dimensions={0} | all-to-all | bytes 1048576 | tf_op jit(solution)/shard_map/all_to_all | solution.py:326
  38.7 2.9 %collective-permute-start.1 = (bf16[512,512]{1,0:T(8,128)(2,1)S(1)}, bf16[512,512]{1,0:T(8,128)(2,1)S(1)}, u32[]{:S(2)}, u32[]{:S(2)}) collective-permute-start(bf16[512,512]{1,0:T(8,128)(2,1)S(1)} %bitcast.21), channel_id=1, source_target_pairs={{0,12},{4,0},{8,4},{12,8},{1,13},{5,1},{9,5},{13,9},{2,14},{6,2},{... | collective-permute-start | bytes 1572872 | tf_op jit(solution)/shard_map/ppermute | solution.py:331
  41.6 0.7 convert_multiply_fusion
  42.2 0.7 multiply_add_fusion
  42.9 8.8 %collective-permute-done.1.e2 = bf16[512,512]{1,0:T(8,128)(2,1)S(1)} collective-permute-done((bf16[512,512]{1,0:T(8,128)(2,1)S(1)}, bf16[512,512]{1,0:T(8,128)(2,1)S(1)}, u32[]{:S(2)}, u32[]{:S(2)}) %collective-permute-start.1) | collective-permute-done | bytes 524320 | tf_op jit(solution)/shard_map/ppermute | solution.py:331
  51.8 3.6 %collective-permute-start.3 = (bf16[256,512]{1,0:T(8,128)(2,1)S(1)}, bf16[256,512]{1,0:T(8,128)(2,1)S(1)}, u32[]{:S(2)}, u32[]{:S(2)}) collective-permute-start(bf16[256,512]{1,0:T(8,128)(2,1)S(1)} %slice.9), channel_id=1, source_target_pairs={{0,12},{4,0},{8,4},{12,8},{1,13},{5,1},{9,5},{13,9},{2,14},{6,2},{... | collective-permute-start | bytes 786440 | tf_op jit(solution)/shard_map/ppermute | solution.py:333
  55.3 0.2 collective-permute-done.e1
  55.6 0.1 collective-permute-start.2
  55.7 1.2 fusion.spread
  56.9 3.8 %collective-permute-done.3.e3b = bf16[256,512]{1,0:T(8,128)(2,1)S(1)} collective-permute-done((bf16[256,512]{1,0:T(8,128)(2,1)S(1)}, bf16[256,512]{1,0:T(8,128)(2,1)S(1)}, u32[]{:S(2)}, u32[]{:S(2)}) %collective-permute-start.3) | collective-permute-done | bytes 262176 | tf_op jit(solution)/shard_map/ppermute | solution.py:333
  60.7 3.7 %collective-permute-done.2.e3a = bf16[256,512]{1,0:T(8,128)(2,1)S(1)} collective-permute-done((bf16[256,512]{1,0:T(8,128)(2,1)S(1)}, bf16[256,512]{1,0:T(8,128)(2,1)S(1)}, u32[]{:S(2)}, u32[]{:S(2)}) %collective-permute-start.2) | collective-permute-done | bytes 262176 | tf_op jit(solution)/shard_map/ppermute | solution.py:332
  64.3 2.1 %cut_bra.1 = bf16[16,2,128,128]{3,2,1,0:T(8,128)(2,1)} custom-call(bf16[16,5,2,128,128]{4,3,2,1,0:T(8,128)(2,1)} %bitcast.18), custom_call_target="tpu_custom_call" | custom-call | tf_op jit(solution)/shard_map/cut_bra/pallas_call | solution.py:259
  66.5 0.0 all-gather.7.cloned.1.call-update
  66.5 7.1 %first_stage.2 = bf16[16,128,256]{2,1,0:T(8,128)(2,1)} custom-call(s32[2048]{0:T(1024)} %left_s.9, s32[2048]{0:T(1024)} %right_s.9, bf16[512,512]{1,0:T(8,128)(2,1)} %bitcast.23, bf16[512,512]{1,0:T(8,128)(2,1)} %copy-done.4, bf16[512,512]{1,0:T(8,128)(2,1)} %copy-done.3, bf16[256,512]{1,0:T(8,128)(2,1)} %copy-done.6, bf16[256,512]{1,0:T(8,128)(2,1)} %copy-done.5, ...), custom_call_target="tpu_custom_call" | custom-call | flops 1073741824 | bytes 8388608 | tf_op jit(solution)/shard_map/first_stage/pallas_call | solution.py:235
  73.6 6.0 %all-to-all-start.1 = ((bf16[16,128,256]{2,1,0:T(8,128)(2,1)}), bf16[16,128,256]{2,1,0:T(8,128)(2,1)S(1)}, u32[]{:S(2)}, u32[]{:S(2)}) async-start(bf16[16,128,256]{2,1,0:T(8,128)(2,1)} %first_stage.2), calls=%async_computation.1 | async-start | bytes 2097152 | tf_op jit(solution)/shard_map/all_to_all | solution.py:342
  79.6 6.8 %first_stage.3 = bf16[16,128,256]{2,1,0:T(8,128)(2,1)} custom-call(s32[2048]{0:T(1024)} %left_s.9, s32[2048]{0:T(1024)} %right_s.9, bf16[512,512]{1,0:T(8,128)(2,1)} %bitcast.24, bf16[512,512]{1,0:T(8,128)(2,1)} %copy-done.4, bf16[512,512]{1,0:T(8,128)(2,1)} %copy-done.3, bf16[256,512]{1,0:T(8,128)(2,1)} %copy-done.6, bf16[256,512]{1,0:T(8,128)(2,1)} %copy-done.5, ...), custom_call_target="tpu_custom_call" | custom-call | flops 1073741824 | bytes 8388608 | tf_op jit(solution)/shard_map/first_stage/pallas_call | solution.py:235
  86.4 21.2 %all-to-all-done.1.got = bf16[16,128,256]{2,1,0:T(8,128)(2,1)S(1)} async-done(((bf16[16,128,256]{2,1,0:T(8,128)(2,1)}), bf16[16,128,256]{2,1,0:T(8,128)(2,1)S(1)}, u32[]{:S(2)}, u32[]{:S(2)}) %all-to-all-start.1) | async-done | bytes 1048608 | tf_op jit(solution)/shard_map/all_to_all | solution.py:342
  107.6 3.6 %all-to-all-start.2 = ((bf16[16,128,256]{2,1,0:T(8,128)(2,1)}), bf16[16,128,256]{2,1,0:T(8,128)(2,1)S(1)}, u32[]{:S(2)}, u32[]{:S(2)}) async-start(bf16[16,128,256]{2,1,0:T(8,128)(2,1)} %first_stage.3), calls=%async_computation.3 | async-start | bytes 2097152 | tf_op jit(solution)/shard_map/all_to_all | solution.py:342
  111.2 0.0 reduce-scatter.2.cloned.1.call-start
  111.2 3.2 %all-gather.7.cloned.1.call-done = bf16[64,2,128,128]{3,2,1,0:T(8,128)(2,1)} async-done(((bf16[16,2,128,128]{3,2,1,0:T(8,128)(2,1)}), bf16[64,2,128,128]{3,2,1,0:T(8,128)(2,1)}) %all-gather.7.cloned.1.call-update) | async-done | bytes 4194320 | tf_op jit(solution)/shard_map/all_gather | solution.py:337
  114.4 4.5 %mask_bra.1.masked = bf16[4,8,512,256]{3,2,1,0:T(8,128)(2,1)} custom-call(s32[2048]{0:T(1024)} %left_s.9, s32[2048]{0:T(1024)} %right_s.9, bf16[4,16,2,128,128]{4,3,2,1,0:T(8,128)(2,1)} %bitcast.25, s32[16,128]{1,0:T(8,128)} %bitcast.13, s32[16,128]{1,0:T(8,128)} %bitcast.17), custom_call_target="tpu_custom_call" | custom-call | tf_op jit(solution)/shard_map/mask_bra/pallas_call | solution.py:274
  119.0 7.1 %second_stage.2 = bf16[2048,256]{1,0:T(8,128)(2,1)} custom-call(s32[2048]{0:T(1024)S(1)} %copy-done, s32[2048]{0:T(1024)S(1)} %copy-done.1, bf16[16,128,256]{2,1,0:T(8,128)(2,1)S(1)} %all-to-all-done.1.got, bf16[4,8,512,256]{3,2,1,0:T(8,128)(2,1)} %mask_bra.1.masked), custom_call_target="tpu_custom_call" | custom-call | flops 1073741824 | bytes 2097152 | tf_op jit(solution)/shard_map/second_stage/pallas_call | solution.py:291
  126.1 0.0 reduce-scatter.2.cloned.1.call-update
  126.1 12.9 %all-to-all-done.2.got = bf16[16,128,256]{2,1,0:T(8,128)(2,1)S(1)} async-done(((bf16[16,128,256]{2,1,0:T(8,128)(2,1)}), bf16[16,128,256]{2,1,0:T(8,128)(2,1)S(1)}, u32[]{:S(2)}, u32[]{:S(2)}) %all-to-all-start.2) | async-done | bytes 1048608 | tf_op jit(solution)/shard_map/all_to_all | solution.py:342
  139.0 5.9 %second_stage.3 = bf16[2048,256]{1,0:T(8,128)(2,1)S(1)} custom-call(s32[2048]{0:T(1024)S(1)} %copy-done, s32[2048]{0:T(1024)S(1)} %copy-done.1, bf16[16,128,256]{2,1,0:T(8,128)(2,1)S(1)} %all-to-all-done.2.got, bf16[4,8,512,256]{3,2,1,0:T(8,128)(2,1)} %mask_bra.1.masked), custom_call_target="tpu_custom_call" | custom-call | flops 1073741824 | bytes 2097152 | tf_op jit(solution)/shard_map/second_stage/pallas_call | solution.py:291
  144.9 18.8 %all_to_all.21 = bf16[4,512,256]{2,1,0:T(8,128)(2,1)S(1)} all-to-all(bf16[4,512,256]{2,1,0:T(8,128)(2,1)S(1)} %bitcast.9), channel_id=1, replica_groups=mesh['chan'=16,'ket'=4,'bra'=4] {'bra'}, dimensions={0} | all-to-all | bytes 2097152 | tf_op jit(solution)/shard_map/all_to_all | solution.py:345
  163.7 0.1 convert_reduce_fusion
  163.9 0.0 reduce-scatter.2.cloned.1.call-done
  163.9 1.0 convert_element_type.19
  164.9 1.1 maximum_bitcast_fusion
  (21 shorter events, 0.1 us)
Async XLA Ops:
  6.5 57.8 %all-gather.5.cloned.1.call-start = ((), (), s32[]{:S(2)}) async-start(), calls=%async_computation.6 | async-start | bytes 5570560 | tf_op jit(solution)/shard_map/all_gather | solution.py:324
  8.7 105.7 %all-gather.7.cloned.1.call-start = ((), (), s32[]{:S(2)}) async-start(), calls=%async_computation.7 | async-start | bytes 5242880 | tf_op jit(solution)/shard_map/all_gather | solution.py:337
  38.7 27.8 %copy-start.2 = (bf16[16,32,512]{2,1,0:T(8,128)(2,1)}, bf16[16,32,512]{2,1,0:T(8,128)(2,1)S(1)}, u32[]{:S(2)}) copy-start(bf16[16,32,512]{2,1,0:T(8,128)(2,1)S(1)} %all_to_all.20) | copy-start | bytes 1572868
  38.7 13.1 %collective-permute-start.1 = (bf16[512,512]{1,0:T(8,128)(2,1)S(1)}, bf16[512,512]{1,0:T(8,128)(2,1)S(1)}, u32[]{:S(2)}, u32[]{:S(2)}) collective-permute-start(bf16[512,512]{1,0:T(8,128)(2,1)S(1)} %bitcast.21), channel_id=1, source_target_pairs={{0,12},{4,0},{8,4},{12,8},{1,13},{5,1},{9,5},{13,9},{2,14},{6,2},{... | collective-permute-start | bytes 1572872 | tf_op jit(solution)/shard_map/ppermute | solution.py:331
  41.6 14.0 %collective-permute-start = (bf16[512,512]{1,0:T(8,128)(2,1)S(1)}, bf16[512,512]{1,0:T(8,128)(2,1)S(1)}, u32[]{:S(2)}, u32[]{:S(2)}) collective-permute-start(bf16[512,512]{1,0:T(8,128)(2,1)S(1)} %bitcast.22), channel_id=1, source_target_pairs={{0,4},{4,8},{8,12},{12,0},{1,5},{5,9},{9,13},{13,1},{2,6},{6,10},{... | collective-permute-start | bytes 1572872 | tf_op jit(solution)/shard_map/ppermute | solution.py:330
  51.7 14.8 %copy-start.3 = (bf16[512,512]{1,0:T(8,128)(2,1)}, bf16[512,512]{1,0:T(8,128)(2,1)S(1)}, u32[]{:S(2)}) copy-start(bf16[512,512]{1,0:T(8,128)(2,1)S(1)} %collective-permute-done.1.e2) | copy-start | bytes 1572868
  51.8 8.9 %collective-permute-start.3 = (bf16[256,512]{1,0:T(8,128)(2,1)S(1)}, bf16[256,512]{1,0:T(8,128)(2,1)S(1)}, u32[]{:S(2)}, u32[]{:S(2)}) collective-permute-start(bf16[256,512]{1,0:T(8,128)(2,1)S(1)} %slice.9), channel_id=1, source_target_pairs={{0,12},{4,0},{8,4},{12,8},{1,13},{5,1},{9,5},{13,9},{2,14},{6,2},{... | collective-permute-start | bytes 786440 | tf_op jit(solution)/shard_map/ppermute | solution.py:333
  55.5 11.0 %copy-start.4 = (bf16[512,512]{1,0:T(8,128)(2,1)}, bf16[512,512]{1,0:T(8,128)(2,1)S(1)}, u32[]{:S(2)}) copy-start(bf16[512,512]{1,0:T(8,128)(2,1)S(1)} %collective-permute-done.e1) | copy-start | bytes 1572868
  55.6 8.8 %collective-permute-start.2 = (bf16[256,512]{1,0:T(8,128)(2,1)S(1)}, bf16[256,512]{1,0:T(8,128)(2,1)S(1)}, u32[]{:S(2)}, u32[]{:S(2)}) collective-permute-start(bf16[256,512]{1,0:T(8,128)(2,1)S(1)} %slice.8), channel_id=1, source_target_pairs={{0,4},{4,8},{8,12},{12,0},{1,5},{5,9},{9,13},{13,1},{2,6},{6,10},{... | collective-permute-start | bytes 786440 | tf_op jit(solution)/shard_map/ppermute | solution.py:332
  60.6 5.9 %copy-start.5 = (bf16[256,512]{1,0:T(8,128)(2,1)}, bf16[256,512]{1,0:T(8,128)(2,1)S(1)}, u32[]{:S(2)}) copy-start(bf16[256,512]{1,0:T(8,128)(2,1)S(1)} %collective-permute-done.3.e3b) | copy-start | bytes 786436
  64.3 2.2 %copy-start.6 = (bf16[256,512]{1,0:T(8,128)(2,1)}, bf16[256,512]{1,0:T(8,128)(2,1)S(1)}, u32[]{:S(2)}) copy-start(bf16[256,512]{1,0:T(8,128)(2,1)S(1)} %collective-permute-done.2.e3a) | copy-start | bytes 786436
  73.6 34.0 %all-to-all-start.1 = ((bf16[16,128,256]{2,1,0:T(8,128)(2,1)}), bf16[16,128,256]{2,1,0:T(8,128)(2,1)S(1)}, u32[]{:S(2)}, u32[]{:S(2)}) async-start(bf16[16,128,256]{2,1,0:T(8,128)(2,1)} %first_stage.2), calls=%async_computation.1 | async-start | bytes 2097152 | tf_op jit(solution)/shard_map/all_to_all | solution.py:342
  107.6 31.4 %all-to-all-start.2 = ((bf16[16,128,256]{2,1,0:T(8,128)(2,1)}), bf16[16,128,256]{2,1,0:T(8,128)(2,1)S(1)}, u32[]{:S(2)}, u32[]{:S(2)}) async-start(bf16[16,128,256]{2,1,0:T(8,128)(2,1)} %first_stage.3), calls=%async_computation.3 | async-start | bytes 2097152 | tf_op jit(solution)/shard_map/all_to_all | solution.py:342
  111.2 52.7 %reduce-scatter.2.cloned.1.call-start = ((), (), s32[]{:S(2)}) async-start(), calls=%async_computation.5 | async-start | bytes 1310720 | tf_op jit(solution)/shard_map/reduce_scatter | solution.py:344
  114.4 4.6 %copy-start = (s32[2048]{0:T(1024)S(1)}, s32[2048]{0:T(1024)}, u32[]{:S(2)}) copy-start(s32[2048]{0:T(1024)} %left_s.9) | copy-start | bytes 24580
  114.4 4.6 %copy-start.1 = (s32[2048]{0:T(1024)S(1)}, s32[2048]{0:T(1024)}, u32[]{:S(2)}) copy-start(s32[2048]{0:T(1024)} %right_s.9) | copy-start | bytes 24580
Sparse Core Ops, SparseCore 0:
  9.2 52.9 all-gather.4
  66.6 47.7 all-gather.6
  126.2 26.0 reduce-scatter.1

commit v6 on v5

--- a/solution.py
+++ b/solution.py
@@ -97,17 +97,25 @@
         low = sum((left_s[256 * i + 255] + PHYS[s] < least).astype(jnp.int32) for i in range(8))
         high = sum((left_s[256 * i] + PHYS[s] <= most).astype(jnp.int32) for i in range(8))
 
-        def step(i, carry):
-            pair = []
-            for r in range(2):
-                rows = column[pl.ds(pl.multiple_of(i * 256 + r * 128, 128), 128), :]
-                values = [planes[2 * i + r, q, PLANE[s]] for q in range(tiles)]
-                pair.append(masked_tiles(values, rows, cols, PHYS[s]))
-            block = jnp.concatenate(pair, axis=0)
-            acc[...] += jnp.dot(env[i], block, preferred_element_type=F32)
+        count = (high - low + 1) // 2
+        low = low - jnp.where(2 * count > high - low, jnp.minimum(low, 1), 0)
+
+        def step(n, carry):
+            i = low + 2 * n
+            total = None
+            for k in (i, i + 1):
+                pair = []
+                for r in range(2):
+                    rows = column[pl.ds(pl.multiple_of(k * 256 + r * 128, 128), 128), :]
+                    values = [planes[2 * k + r, q, PLANE[s]] for q in range(tiles)]
+                    pair.append(masked_tiles(values, rows, cols, PHYS[s]))
+                block = jnp.concatenate(pair, axis=0)
+                product = jnp.dot(env[k], block, preferred_element_type=F32)
+                total = product if total is None else total + product
+            acc[...] += total
             return carry
 
-        lax.fori_loop(low, high, step, 0)
+        lax.fori_loop(0, count, step, 0)
         product = acc[...].reshape(16, 4, 8, width)
         for g in range(4):
             parts[g, s * 128 : (s + 1) * 128, :] = product[:, g].reshape(128, width).astype(BF16)

time: 173 us -> 173 us (level)
  no operation moved by 1% of the time
where the time goes in v6:
time: 173 us; the launch traced here: 172 us
  waiting for transfers between devices  54.1 us (31%)
  blocking collectives  49.1 us (28%)
  Pallas kernels  34.8 us (20%)
  starting transfers between devices  16.2 us (9%)
  between operations  13.3 us (8%)
  other arithmetic  3.63 us (2%)
    all_to_all x2, waiting for transfers between devices, local(): got = lax.all_to_all(mixed, 'chan', 0, 0, tiled=True)  33.9 us
    all_to_all x1, blocking collectives, local(): lax.all_to_all(environment.reshape(16, 32, 512), 'chan', 0, 0, tiled=True)  30 us
    all_to_all x1, blocking collectives, local(): lax.all_to_all(terms[1].reshape(4, 512, WIDTH), 'bra', 0, 0, tiled=True)  19.1 us
    pallas_call x2, Pallas kernels, first_stage(): pl.pallas_call(functools.partial(first_kernel, start), out_shape=jax.Shap...  13.2 us
    pallas_call x2, Pallas kernels, second_stage(): pl.pallas_call(second_kernel, out_shape=jax.ShapeDtypeStruct((2048, WIDTH...  12.8 us
    all_to_all x2, starting transfers between devices, local(): got = lax.all_to_all(mixed, 'chan', 0, 0, tiled=True)  9.52 us
    ppermute x1, waiting for transfers between devices, local(): env_above = lax.ppermute(env, 'ket', down)  8.79 us
    pallas_call x1, Pallas kernels, mask_bra(): pl.pallas_call(mask_kernel, out_shape=pltpu.HBM((4, 8, 512, 256), BF16),...  4.54 us
  transfers between devices with their start and end apart: 9, of which 7 were waited for; matrix products, arithmetic and copies ran while one was open for 2% of the time, Pallas kernels for 18%

profile of v6, /device:TPU:1, one launch (start us, length us, event | category | flops | bytes accessed | tf_op | source)
XLA Modules:
  0.0 172.3 jit_solution(11710552830795661947)
XLA Ops:
  6.5 2.1 %pack.1 = bf16[5,2,128,128]{3,2,1,0:T(8,128)(2,1)} custom-call(bf16[4,128,512]{2,1,0:T(8,128)(2,1)} %ket.1, bf16[4,512,128]{2,1,0:T(8,128)(2,1)} %bra.1, s32[16,128]{1,0:T(8,128)} %bitcast.10, s32[16,128]{1,0:T(8,128)} %bitcast.14), custom_call_target="tpu_custom_call" | custom-call | tf_op jit(solution)/shard_map/pack/pallas_call | solution.py:233
  8.7 0.0 all-gather.7.cloned.1.call-start
  8.7 30.0 %all_to_all.20 = bf16[16,32,512]{2,1,0:T(8,128)(2,1)S(1)} all-to-all(bf16[16,32,512]{2,1,0:T(8,128)(2,1)} %bitcast.26), channel_id=1, replica_groups=mesh['chan'=16,'ket'=4,'bra'=4] {'chan'}, dimensions={0} | all-to-all | bytes 1048576 | tf_op jit(solution)/shard_map/all_to_all | solution.py:334
  38.7 2.9 %collective-permute-start.1 = (bf16[512,512]{1,0:T(8,128)(2,1)S(1)}, bf16[512,512]{1,0:T(8,128)(2,1)S(1)}, u32[]{:S(2)}, u32[]{:S(2)}) collective-permute-start(bf16[512,512]{1,0:T(8,128)(2,1)S(1)} %bitcast.21), channel_id=1, source_target_pairs={{0,12},{4,0},{8,4},{12,8},{1,13},{5,1},{9,5},{13,9},{2,14},{6,2},{... | collective-permute-start | bytes 1572872 | tf_op jit(solution)/shard_map/ppermute | solution.py:339
  41.6 0.7 convert_multiply_fusion
  42.2 0.7 multiply_add_fusion
  42.9 8.8 %collective-permute-done.1.e2 = bf16[512,512]{1,0:T(8,128)(2,1)S(1)} collective-permute-done((bf16[512,512]{1,0:T(8,128)(2,1)S(1)}, bf16[512,512]{1,0:T(8,128)(2,1)S(1)}, u32[]{:S(2)}, u32[]{:S(2)}) %collective-permute-start.1) | collective-permute-done | bytes 524320 | tf_op jit(solution)/shard_map/ppermute | solution.py:339
  51.8 3.6 %collective-permute-start.3 = (bf16[256,512]{1,0:T(8,128)(2,1)S(1)}, bf16[256,512]{1,0:T(8,128)(2,1)S(1)}, u32[]{:S(2)}, u32[]{:S(2)}) collective-permute-start(bf16[256,512]{1,0:T(8,128)(2,1)S(1)} %slice.9), channel_id=1, source_target_pairs={{0,12},{4,0},{8,4},{12,8},{1,13},{5,1},{9,5},{13,9},{2,14},{6,2},{... | collective-permute-start | bytes 786440 | tf_op jit(solution)/shard_map/ppermute | solution.py:341
  55.3 0.2 collective-permute-done.e1
  55.6 0.1 collective-permute-start.2
  55.7 1.2 fusion.spread
  56.9 3.8 %collective-permute-done.3.e3b = bf16[256,512]{1,0:T(8,128)(2,1)S(1)} collective-permute-done((bf16[256,512]{1,0:T(8,128)(2,1)S(1)}, bf16[256,512]{1,0:T(8,128)(2,1)S(1)}, u32[]{:S(2)}, u32[]{:S(2)}) %collective-permute-start.3) | collective-permute-done | bytes 262176 | tf_op jit(solution)/shard_map/ppermute | solution.py:341
  60.7 3.7 %collective-permute-done.2.e3a = bf16[256,512]{1,0:T(8,128)(2,1)S(1)} collective-permute-done((bf16[256,512]{1,0:T(8,128)(2,1)S(1)}, bf16[256,512]{1,0:T(8,128)(2,1)S(1)}, u32[]{:S(2)}, u32[]{:S(2)}) %collective-permute-start.2) | collective-permute-done | bytes 262176 | tf_op jit(solution)/shard_map/ppermute | solution.py:340
  64.3 2.1 %cut_bra.1 = bf16[16,2,128,128]{3,2,1,0:T(8,128)(2,1)} custom-call(bf16[16,5,2,128,128]{4,3,2,1,0:T(8,128)(2,1)} %bitcast.18), custom_call_target="tpu_custom_call" | custom-call | tf_op jit(solution)/shard_map/cut_bra/pallas_call | solution.py:267
  66.5 0.0 all-gather.7.cloned.1.call-update
  66.5 6.7 %first_stage.2 = bf16[16,128,256]{2,1,0:T(8,128)(2,1)} custom-call(s32[2048]{0:T(1024)} %left_s.9, s32[2048]{0:T(1024)} %right_s.9, bf16[512,512]{1,0:T(8,128)(2,1)} %bitcast.23, bf16[512,512]{1,0:T(8,128)(2,1)} %copy-done.4, bf16[512,512]{1,0:T(8,128)(2,1)} %copy-done.3, bf16[256,512]{1,0:T(8,128)(2,1)} %copy-done.6, bf16[256,512]{1,0:T(8,128)(2,1)} %copy-done.5, ...), custom_call_target="tpu_custom_call" | custom-call | flops 1073741824 | bytes 8388608 | tf_op jit(solution)/shard_map/first_stage/pallas_call | solution.py:243
  73.2 6.0 %all-to-all-start.1 = ((bf16[16,128,256]{2,1,0:T(8,128)(2,1)}), bf16[16,128,256]{2,1,0:T(8,128)(2,1)S(1)}, u32[]{:S(2)}, u32[]{:S(2)}) async-start(bf16[16,128,256]{2,1,0:T(8,128)(2,1)} %first_stage.2), calls=%async_computation.1 | async-start | bytes 2097152 | tf_op jit(solution)/shard_map/all_to_all | solution.py:350
  79.2 6.6 %first_stage.3 = bf16[16,128,256]{2,1,0:T(8,128)(2,1)} custom-call(s32[2048]{0:T(1024)} %left_s.9, s32[2048]{0:T(1024)} %right_s.9, bf16[512,512]{1,0:T(8,128)(2,1)} %bitcast.24, bf16[512,512]{1,0:T(8,128)(2,1)} %copy-done.4, bf16[512,512]{1,0:T(8,128)(2,1)} %copy-done.3, bf16[256,512]{1,0:T(8,128)(2,1)} %copy-done.6, bf16[256,512]{1,0:T(8,128)(2,1)} %copy-done.5, ...), custom_call_target="tpu_custom_call" | custom-call | flops 1073741824 | bytes 8388608 | tf_op jit(solution)/shard_map/first_stage/pallas_call | solution.py:243
  85.7 21.4 %all-to-all-done.1.got = bf16[16,128,256]{2,1,0:T(8,128)(2,1)S(1)} async-done(((bf16[16,128,256]{2,1,0:T(8,128)(2,1)}), bf16[16,128,256]{2,1,0:T(8,128)(2,1)S(1)}, u32[]{:S(2)}, u32[]{:S(2)}) %all-to-all-start.1) | async-done | bytes 1048608 | tf_op jit(solution)/shard_map/all_to_all | solution.py:350
  107.2 3.6 %all-to-all-start.2 = ((bf16[16,128,256]{2,1,0:T(8,128)(2,1)}), bf16[16,128,256]{2,1,0:T(8,128)(2,1)S(1)}, u32[]{:S(2)}, u32[]{:S(2)}) async-start(bf16[16,128,256]{2,1,0:T(8,128)(2,1)} %first_stage.3), calls=%async_computation.3 | async-start | bytes 2097152 | tf_op jit(solution)/shard_map/all_to_all | solution.py:350
  110.7 0.0 reduce-scatter.2.cloned.1.call-start
  110.8 3.6 %all-gather.7.cloned.1.call-done = bf16[64,2,128,128]{3,2,1,0:T(8,128)(2,1)} async-done(((bf16[16,2,128,128]{3,2,1,0:T(8,128)(2,1)}), bf16[64,2,128,128]{3,2,1,0:T(8,128)(2,1)}) %all-gather.7.cloned.1.call-update) | async-done | bytes 4194320 | tf_op jit(solution)/shard_map/all_gather | solution.py:345
  114.4 4.5 %mask_bra.1.masked = bf16[4,8,512,256]{3,2,1,0:T(8,128)(2,1)} custom-call(s32[2048]{0:T(1024)} %left_s.9, s32[2048]{0:T(1024)} %right_s.9, bf16[4,16,2,128,128]{4,3,2,1,0:T(8,128)(2,1)} %bitcast.25, s32[16,128]{1,0:T(8,128)} %bitcast.13, s32[16,128]{1,0:T(8,128)} %bitcast.17), custom_call_target="tpu_custom_call" | custom-call | tf_op jit(solution)/shard_map/mask_bra/pallas_call | solution.py:282
  119.0 7.0 %second_stage.2 = bf16[2048,256]{1,0:T(8,128)(2,1)} custom-call(s32[2048]{0:T(1024)S(1)} %copy-done, s32[2048]{0:T(1024)S(1)} %copy-done.1, bf16[16,128,256]{2,1,0:T(8,128)(2,1)S(1)} %all-to-all-done.1.got, bf16[4,8,512,256]{3,2,1,0:T(8,128)(2,1)} %mask_bra.1.masked), custom_call_target="tpu_custom_call" | custom-call | flops 1073741824 | bytes 2097152 | tf_op jit(solution)/shard_map/second_stage/pallas_call | solution.py:299
  126.0 0.0 reduce-scatter.2.cloned.1.call-update
  126.0 12.5 %all-to-all-done.2.got = bf16[16,128,256]{2,1,0:T(8,128)(2,1)S(1)} async-done(((bf16[16,128,256]{2,1,0:T(8,128)(2,1)}), bf16[16,128,256]{2,1,0:T(8,128)(2,1)S(1)}, u32[]{:S(2)}, u32[]{:S(2)}) %all-to-all-start.2) | async-done | bytes 1048608 | tf_op jit(solution)/shard_map/all_to_all | solution.py:350
  138.6 5.8 %second_stage.3 = bf16[2048,256]{1,0:T(8,128)(2,1)S(1)} custom-call(s32[2048]{0:T(1024)S(1)} %copy-done, s32[2048]{0:T(1024)S(1)} %copy-done.1, bf16[16,128,256]{2,1,0:T(8,128)(2,1)S(1)} %all-to-all-done.2.got, bf16[4,8,512,256]{3,2,1,0:T(8,128)(2,1)} %mask_bra.1.masked), custom_call_target="tpu_custom_call" | custom-call | flops 1073741824 | bytes 2097152 | tf_op jit(solution)/shard_map/second_stage/pallas_call | solution.py:299
  144.4 19.1 %all_to_all.21 = bf16[4,512,256]{2,1,0:T(8,128)(2,1)S(1)} all-to-all(bf16[4,512,256]{2,1,0:T(8,128)(2,1)S(1)} %bitcast.9), channel_id=1, replica_groups=mesh['chan'=16,'ket'=4,'bra'=4] {'bra'}, dimensions={0} | all-to-all | bytes 2097152 | tf_op jit(solution)/shard_map/all_to_all | solution.py:353
  163.5 0.1 convert_reduce_fusion
  163.6 0.0 reduce-scatter.2.cloned.1.call-done
  163.7 1.0 convert_element_type.19
  164.6 1.1 maximum_bitcast_fusion
  (21 shorter events, 0.1 us)
Async XLA Ops:
  6.5 57.8 %all-gather.5.cloned.1.call-start = ((), (), s32[]{:S(2)}) async-start(), calls=%async_computation.6 | async-start | bytes 5570560 | tf_op jit(solution)/shard_map/all_gather | solution.py:332
  8.7 105.7 %all-gather.7.cloned.1.call-start = ((), (), s32[]{:S(2)}) async-start(), calls=%async_computation.7 | async-start | bytes 5242880 | tf_op jit(solution)/shard_map/all_gather | solution.py:345
  38.7 27.8 %copy-start.2 = (bf16[16,32,512]{2,1,0:T(8,128)(2,1)}, bf16[16,32,512]{2,1,0:T(8,128)(2,1)S(1)}, u32[]{:S(2)}) copy-start(bf16[16,32,512]{2,1,0:T(8,128)(2,1)S(1)} %all_to_all.20) | copy-start | bytes 1572868
  38.7 13.1 %collective-permute-start.1 = (bf16[512,512]{1,0:T(8,128)(2,1)S(1)}, bf16[512,512]{1,0:T(8,128)(2,1)S(1)}, u32[]{:S(2)}, u32[]{:S(2)}) collective-permute-start(bf16[512,512]{1,0:T(8,128)(2,1)S(1)} %bitcast.21), channel_id=1, source_target_pairs={{0,12},{4,0},{8,4},{12,8},{1,13},{5,1},{9,5},{13,9},{2,14},{6,2},{... | collective-permute-start | bytes 1572872 | tf_op jit(solution)/shard_map/ppermute | solution.py:339
  41.6 14.0 %collective-permute-start = (bf16[512,512]{1,0:T(8,128)(2,1)S(1)}, bf16[512,512]{1,0:T(8,128)(2,1)S(1)}, u32[]{:S(2)}, u32[]{:S(2)}) collective-permute-start(bf16[512,512]{1,0:T(8,128)(2,1)S(1)} %bitcast.22), channel_id=1, source_target_pairs={{0,4},{4,8},{8,12},{12,0},{1,5},{5,9},{9,13},{13,1},{2,6},{6,10},{... | collective-permute-start | bytes 1572872 | tf_op jit(solution)/shard_map/ppermute | solution.py:338
  51.7 14.8 %copy-start.3 = (bf16[512,512]{1,0:T(8,128)(2,1)}, bf16[512,512]{1,0:T(8,128)(2,1)S(1)}, u32[]{:S(2)}) copy-start(bf16[512,512]{1,0:T(8,128)(2,1)S(1)} %collective-permute-done.1.e2) | copy-start | bytes 1572868
  51.8 8.9 %collective-permute-start.3 = (bf16[256,512]{1,0:T(8,128)(2,1)S(1)}, bf16[256,512]{1,0:T(8,128)(2,1)S(1)}, u32[]{:S(2)}, u32[]{:S(2)}) collective-permute-start(bf16[256,512]{1,0:T(8,128)(2,1)S(1)} %slice.9), channel_id=1, source_target_pairs={{0,12},{4,0},{8,4},{12,8},{1,13},{5,1},{9,5},{13,9},{2,14},{6,2},{... | collective-permute-start | bytes 786440 | tf_op jit(solution)/shard_map/ppermute | solution.py:341
  55.5 11.0 %copy-start.4 = (bf16[512,512]{1,0:T(8,128)(2,1)}, bf16[512,512]{1,0:T(8,128)(2,1)S(1)}, u32[]{:S(2)}) copy-start(bf16[512,512]{1,0:T(8,128)(2,1)S(1)} %collective-permute-done.e1) | copy-start | bytes 1572868
  55.6 8.8 %collective-permute-start.2 = (bf16[256,512]{1,0:T(8,128)(2,1)S(1)}, bf16[256,512]{1,0:T(8,128)(2,1)S(1)}, u32[]{:S(2)}, u32[]{:S(2)}) collective-permute-start(bf16[256,512]{1,0:T(8,128)(2,1)S(1)} %slice.8), channel_id=1, source_target_pairs={{0,4},{4,8},{8,12},{12,0},{1,5},{5,9},{9,13},{13,1},{2,6},{6,10},{... | collective-permute-start | bytes 786440 | tf_op jit(solution)/shard_map/ppermute | solution.py:340
  60.6 5.9 %copy-start.5 = (bf16[256,512]{1,0:T(8,128)(2,1)}, bf16[256,512]{1,0:T(8,128)(2,1)S(1)}, u32[]{:S(2)}) copy-start(bf16[256,512]{1,0:T(8,128)(2,1)S(1)} %collective-permute-done.3.e3b) | copy-start | bytes 786436
  64.3 2.2 %copy-start.6 = (bf16[256,512]{1,0:T(8,128)(2,1)}, bf16[256,512]{1,0:T(8,128)(2,1)S(1)}, u32[]{:S(2)}) copy-start(bf16[256,512]{1,0:T(8,128)(2,1)S(1)} %collective-permute-done.2.e3a) | copy-start | bytes 786436
  73.2 34.0 %all-to-all-start.1 = ((bf16[16,128,256]{2,1,0:T(8,128)(2,1)}), bf16[16,128,256]{2,1,0:T(8,128)(2,1)S(1)}, u32[]{:S(2)}, u32[]{:S(2)}) async-start(bf16[16,128,256]{2,1,0:T(8,128)(2,1)} %first_stage.2), calls=%async_computation.1 | async-start | bytes 2097152 | tf_op jit(solution)/shard_map/all_to_all | solution.py:350
  107.2 31.4 %all-to-all-start.2 = ((bf16[16,128,256]{2,1,0:T(8,128)(2,1)}), bf16[16,128,256]{2,1,0:T(8,128)(2,1)S(1)}, u32[]{:S(2)}, u32[]{:S(2)}) async-start(bf16[16,128,256]{2,1,0:T(8,128)(2,1)} %first_stage.3), calls=%async_computation.3 | async-start | bytes 2097152 | tf_op jit(solution)/shard_map/all_to_all | solution.py:350
  110.7 52.9 %reduce-scatter.2.cloned.1.call-start = ((), (), s32[]{:S(2)}) async-start(), calls=%async_computation.5 | async-start | bytes 1310720 | tf_op jit(solution)/shard_map/reduce_scatter | solution.py:352
  114.4 4.6 %copy-start = (s32[2048]{0:T(1024)S(1)}, s32[2048]{0:T(1024)}, u32[]{:S(2)}) copy-start(s32[2048]{0:T(1024)} %left_s.9) | copy-start | bytes 24580
  114.4 4.6 %copy-start.1 = (s32[2048]{0:T(1024)S(1)}, s32[2048]{0:T(1024)}, u32[]{:S(2)}) copy-start(s32[2048]{0:T(1024)} %right_s.9) | copy-start | bytes 24580
Sparse Core Ops, SparseCore 0:
  9.2 52.9 all-gather.4
  66.6 47.7 all-gather.6
  126.2 26.0 reduce-scatter.1

commit v7 on v6

--- a/solution.py
+++ b/solution.py
@@ -68,7 +68,7 @@
 
 
 def first_kernel(
-    start, left_s, right_s, e0, e1, e2, e3a, e3b, gathered, left, right, spread,
+    start, left_s, right_s, e0, e1, e2, e3, e4, e5, e6, e7, gathered, left, right, spread,
     out, env, planes, table, column, acc, parts, results, sems, out_sems,
 ):
     y = lax.axis_index("ket")
@@ -78,10 +78,9 @@
     copies = [(gathered.at[:, pl.ds(start // 128, tiles)], planes)]
     for h in range(2):
         cut = pl.ds(h * 256, 256)
-        copies += [(e.at[:, cut], env.at[2 * blocks[i] + h]) for i, e in enumerate((e0, e1, e2))]
         copies += [
-            (e.at[:, cut], env.at[2 * blocks[3] + h, pl.ds(n * 256, 256)])
-            for n, e in enumerate((e3a, e3b))
+            (e.at[:, cut], env.at[2 * blocks[n // 2] + h, pl.ds(n % 2 * 256, 256)])
+            for n, e in enumerate((e0, e1, e2, e3, e4, e5, e6, e7))
         ]
     copies.append((spread, table))
     copies = begin(copies, sems)
@@ -253,7 +252,7 @@
             pltpu.VMEM((512, WIDTH), F32),
             pltpu.VMEM((4, 512, WIDTH), BF16),
             pltpu.VMEM((2, 16, 64, WIDTH), BF16),
-            pltpu.SemaphoreType.DMA((12,)),
+            pltpu.SemaphoreType.DMA((18,)),
             pltpu.SemaphoreType.DMA((2,)),
         ],
         cost_estimate=pl.CostEstimate(
@@ -335,12 +334,15 @@
     env = env.reshape(512, 512)
     up = [(i, (i + 1) % 4) for i in range(4)]
     down = [(i, (i + 3) % 4) for i in range(4)]
-    env_below = lax.ppermute(env, "ket", up)
-    env_above = lax.ppermute(env, "ket", down)
-    far_a = lax.ppermute(env_below[:256], "ket", up)
-    far_b = lax.ppermute(env_above[256:], "ket", down)
+    low, high = env[:256], env[256:]
+    below_low = lax.ppermute(low, "ket", up)
+    above_high = lax.ppermute(high, "ket", down)
+    below_high = lax.ppermute(high, "ket", up)
+    above_low = lax.ppermute(low, "ket", down)
+    far_low = lax.ppermute(below_low, "ket", up)
+    far_high = lax.ppermute(above_high, "ket", down)
     spread = spread_coupling(op_in, op_out, op_bra, op_ket, op_code)
-    pieces = (env, env_below, env_above, far_a, far_b)
+    pieces = (low, high, below_low, below_high, above_low, above_high, far_low, far_high)
     gathered, spread, pieces = lax.optimization_barrier((gathered, spread, pieces))
     bra_gathered = lax.all_gather(cut_bra(gathered), "ket", axis=0)
     masked = mask_bra(charge_left, charge_right, bra_gathered, left, right)

time: 173 us -> 171 us (0.988)
  waiting for transfers between devices: 54.1 us -> 49.2 us
  Pallas kernels: 34.8 us -> 36.8 us
    ppermute x4 -> x6, waiting for transfers between devices: 16.4 us -> 9.47 us  [the longest x1 4.69 us: local(): far_low = lax.ppermute(below_low, 'ket', up)]
    all_to_all x2, waiting for transfers between devices: 33.9 us -> 30.5 us  [local(): got = lax.all_to_all(mixed, 'chan', 0, 0, tiled=True)]
    all_gather x1, waiting for transfers between devices: 0.01 us -> 3.27 us  [local(): gathered = lax.all_gather(planes, 'chan', axis=0)]
    all_gather x1, waiting for transfers between devices: 3.63 us -> 5.88 us  [local(): bra_gathered = lax.all_gather(cut_bra(gathered), 'ket', axis=0)]
    ppermute x4 -> x6, starting transfers between devices: 6.56 us -> 8.11 us  [the longest x1 2.85 us: local(): far_high = lax.ppermute(above_high, 'ket', down)]
  transfers between devices with their start and end apart: 9 -> 11, of which waited for: 7 -> 8; matrix products, arithmetic and copies ran while one was open for 2% -> 2% of each run, Pallas kernels for 18% -> 19%
where the time goes in v7:
time: 171 us; the launch traced here: 170 us
  blocking collectives  49.7 us (29%)
  waiting for transfers between devices  49.2 us (29%)
  Pallas kernels  36.8 us (22%)
  starting transfers between devices  16.5 us (10%)
  between operations  13.3 us (8%)
  other arithmetic  3.62 us (2%)
    all_to_all x2, waiting for transfers between devices, local(): got = lax.all_to_all(mixed, 'chan', 0, 0, tiled=True)  30.5 us
    all_to_all x1, blocking collectives, local(): lax.all_to_all(environment.reshape(16, 32, 512), 'chan', 0, 0, tiled=True)  30 us
    all_to_all x1, blocking collectives, local(): lax.all_to_all(terms[1].reshape(4, 512, WIDTH), 'bra', 0, 0, tiled=True)  19.8 us
    pallas_call x2, Pallas kernels, second_stage(): pl.pallas_call(second_kernel, out_shape=jax.ShapeDtypeStruct((2048, WIDTH...  13.9 us
    pallas_call x2, Pallas kernels, first_stage(): pl.pallas_call(functools.partial(first_kernel, start), out_shape=jax.Shap...  13.9 us
    all_to_all x2, starting transfers between devices, local(): got = lax.all_to_all(mixed, 'chan', 0, 0, tiled=True)  8.28 us
    all_gather x1, waiting for transfers between devices, local(): bra_gathered = lax.all_gather(cut_bra(gathered), 'ket', axis=0)  5.88 us
    pallas_call x1, Pallas kernels, mask_bra(): pl.pallas_call(mask_kernel, out_shape=pltpu.HBM((4, 8, 512, 256), BF16),...  4.94 us
  transfers between devices with their start and end apart: 11, of which 8 were waited for; matrix products, arithmetic and copies ran while one was open for 2% of the time, Pallas kernels for 19%

profile of v7, /device:TPU:1, one launch (start us, length us, event | category | flops | bytes accessed | tf_op | source)
XLA Modules:
  0.0 170.4 jit_solution(7216463080973683535)
XLA Ops:
  6.5 2.1 %pack.1 = bf16[5,2,128,128]{3,2,1,0:T(8,128)(2,1)} custom-call(bf16[4,128,512]{2,1,0:T(8,128)(2,1)} %ket.1, bf16[4,512,128]{2,1,0:T(8,128)(2,1)} %bra.1, s32[16,128]{1,0:T(8,128)} %bitcast.11, s32[16,128]{1,0:T(8,128)} %bitcast.15), custom_call_target="tpu_custom_call" | custom-call | tf_op jit(solution)/shard_map/pack/pallas_call | solution.py:232
  8.7 30.0 %all_to_all.20 = bf16[16,32,512]{2,1,0:T(8,128)(2,1)S(1)} all-to-all(bf16[16,32,512]{2,1,0:T(8,128)(2,1)} %bitcast.31), channel_id=1, replica_groups=mesh['chan'=16,'ket'=4,'bra'=4] {'chan'}, dimensions={0} | all-to-all | bytes 1048576 | tf_op jit(solution)/shard_map/all_to_all | solution.py:333
  38.7 1.4 collective-permute-start
  40.1 1.6 collective-permute-start.3
  41.8 0.7 convert_multiply_fusion
  42.4 0.7 multiply_add_fusion
  43.2 1.4 collective-permute-start.2
  44.5 0.1 collective-permute-start.1
  44.6 2.3 %collective-permute-done.e2 = bf16[256,512]{1,0:T(8,128)(2,1)S(1)} collective-permute-done((bf16[256,512]{1,0:T(8,128)(2,1)S(1)}, bf16[256,512]{1,0:T(8,128)(2,1)S(1)}, u32[]{:S(2)}, u32[]{:S(2)}) %collective-permute-start) | collective-permute-done | bytes 262176 | tf_op jit(solution)/shard_map/ppermute | solution.py:338
  46.9 0.7 collective-permute-start.4
  47.6 0.9 collective-permute-done.3.e5
  48.6 2.9 %collective-permute-start.5 = (bf16[256,512]{1,0:T(8,128)(2,1)S(1)}, bf16[256,512]{1,0:T(8,128)(2,1)S(1)}, u32[]{:S(2)}, u32[]{:S(2)}) collective-permute-start(bf16[256,512]{1,0:T(8,128)(2,1)S(1)} %collective-permute-done.3.e5), channel_id=1, source_target_pairs={{0,12},{4,0},{8,4},{12,8},{1,13},{5,1},{9,5},{13,9},{2,14},{6,2},{... | collective-permute-start | bytes 786440 | tf_op jit(solution)/shard_map/ppermute | solution.py:343
  51.4 1.2 fusion.spread
  52.6 1.6 collective-permute-done.2.e4
  54.2 4.7 %collective-permute-done.4.e6 = bf16[256,512]{1,0:T(8,128)(2,1)S(1)} collective-permute-done((bf16[256,512]{1,0:T(8,128)(2,1)S(1)}, bf16[256,512]{1,0:T(8,128)(2,1)S(1)}, u32[]{:S(2)}, u32[]{:S(2)}) %collective-permute-start.4) | collective-permute-done | bytes 262176 | tf_op jit(solution)/shard_map/ppermute | solution.py:342
  58.9 3.3 %all-gather.5.cloned.1.call-done = bf16[80,2,128,128]{3,2,1,0:T(8,128)(2,1)} async-done(((bf16[5,2,128,128]{3,2,1,0:T(8,128)(2,1)}), bf16[80,2,128,128]{3,2,1,0:T(8,128)(2,1)}) %all-gather.5.cloned.1.call-update) | async-done | bytes 5242896 | tf_op jit(solution)/shard_map/all_gather | solution.py:331
  62.2 2.0 %cut_bra.1 = bf16[16,2,128,128]{3,2,1,0:T(8,128)(2,1)} custom-call(bf16[16,5,2,128,128]{4,3,2,1,0:T(8,128)(2,1)} %bitcast.19), custom_call_target="tpu_custom_call" | custom-call | tf_op jit(solution)/shard_map/cut_bra/pallas_call | solution.py:266
  64.3 7.0 %first_stage.2 = bf16[16,128,256]{2,1,0:T(8,128)(2,1)} custom-call(s32[2048]{0:T(1024)} %left_s.9, s32[2048]{0:T(1024)} %right_s.9, bf16[256,512]{1,0:T(8,128)(2,1)} %bitcast.29, bf16[256,512]{1,0:T(8,128)(2,1)} %bitcast.25, bf16[256,512]{1,0:T(8,128)(2,1)} %copy-done.4, bf16[256,512]{1,0:T(8,128)(2,1)} %copy-done.7, bf16[256,512]{1,0:T(8,128)(2,1)} %copy-done.6, ...), custom_call_target="tpu_custom_call" | custom-call | flops 1073741824 | bytes 8388608 | tf_op jit(solution)/shard_map/first_stage/pallas_call | solution.py:242
  71.3 4.7 %all-to-all-start.1 = ((bf16[16,128,256]{2,1,0:T(8,128)(2,1)}), bf16[16,128,256]{2,1,0:T(8,128)(2,1)S(1)}, u32[]{:S(2)}, u32[]{:S(2)}) async-start(bf16[16,128,256]{2,1,0:T(8,128)(2,1)} %first_stage.2), calls=%async_computation.1 | async-start | bytes 2097152 | tf_op jit(solution)/shard_map/all_to_all | solution.py:352
  76.0 6.9 %first_stage.3 = bf16[16,128,256]{2,1,0:T(8,128)(2,1)} custom-call(s32[2048]{0:T(1024)} %left_s.9, s32[2048]{0:T(1024)} %right_s.9, bf16[256,512]{1,0:T(8,128)(2,1)} %bitcast.30, bf16[256,512]{1,0:T(8,128)(2,1)} %bitcast.26, bf16[256,512]{1,0:T(8,128)(2,1)} %copy-done.4, bf16[256,512]{1,0:T(8,128)(2,1)} %copy-done.7, bf16[256,512]{1,0:T(8,128)(2,1)} %copy-done.6, ...), custom_call_target="tpu_custom_call" | custom-call | flops 1073741824 | bytes 8388608 | tf_op jit(solution)/shard_map/first_stage/pallas_call | solution.py:242
  82.9 21.1 %all-to-all-done.1.got = bf16[16,128,256]{2,1,0:T(8,128)(2,1)S(1)} async-done(((bf16[16,128,256]{2,1,0:T(8,128)(2,1)}), bf16[16,128,256]{2,1,0:T(8,128)(2,1)S(1)}, u32[]{:S(2)}, u32[]{:S(2)}) %all-to-all-start.1) | async-done | bytes 1048608 | tf_op jit(solution)/shard_map/all_to_all | solution.py:352
  104.0 3.6 %all-to-all-start.2 = ((bf16[16,128,256]{2,1,0:T(8,128)(2,1)}), bf16[16,128,256]{2,1,0:T(8,128)(2,1)S(1)}, u32[]{:S(2)}, u32[]{:S(2)}) async-start(bf16[16,128,256]{2,1,0:T(8,128)(2,1)} %first_stage.3), calls=%async_computation.3 | async-start | bytes 2097152 | tf_op jit(solution)/shard_map/all_to_all | solution.py:352
  107.6 0.0 reduce-scatter.2.cloned.1.call-start
  107.6 5.9 %all-gather.7.cloned.1.call-done = bf16[64,2,128,128]{3,2,1,0:T(8,128)(2,1)} async-done(((bf16[16,2,128,128]{3,2,1,0:T(8,128)(2,1)}), bf16[64,2,128,128]{3,2,1,0:T(8,128)(2,1)}) %all-gather.7.cloned.1.call-update) | async-done | bytes 4194320 | tf_op jit(solution)/shard_map/all_gather | solution.py:347
  113.5 4.9 %mask_bra.1.masked = bf16[4,8,512,256]{3,2,1,0:T(8,128)(2,1)} custom-call(s32[2048]{0:T(1024)} %left_s.9, s32[2048]{0:T(1024)} %right_s.9, bf16[4,16,2,128,128]{4,3,2,1,0:T(8,128)(2,1)} %bitcast.22, s32[16,128]{1,0:T(8,128)} %bitcast.14, s32[16,128]{1,0:T(8,128)} %bitcast.18), custom_call_target="tpu_custom_call" | custom-call | tf_op jit(solution)/shard_map/mask_bra/pallas_call | solution.py:281
  118.5 7.5 %second_stage.2 = bf16[2048,256]{1,0:T(8,128)(2,1)} custom-call(s32[2048]{0:T(1024)S(1)} %copy-done, s32[2048]{0:T(1024)S(1)} %copy-done.1, bf16[16,128,256]{2,1,0:T(8,128)(2,1)S(1)} %all-to-all-done.1.got, bf16[4,8,512,256]{3,2,1,0:T(8,128)(2,1)} %mask_bra.1.masked), custom_call_target="tpu_custom_call" | custom-call | flops 1073741824 | bytes 2097152 | tf_op jit(solution)/shard_map/second_stage/pallas_call | solution.py:298
  126.0 9.4 %all-to-all-done.2.got = bf16[16,128,256]{2,1,0:T(8,128)(2,1)S(1)} async-done(((bf16[16,128,256]{2,1,0:T(8,128)(2,1)}), bf16[16,128,256]{2,1,0:T(8,128)(2,1)S(1)}, u32[]{:S(2)}, u32[]{:S(2)}) %all-to-all-start.2) | async-done | bytes 1048608 | tf_op jit(solution)/shard_map/all_to_all | solution.py:352
  135.4 6.4 %second_stage.3 = bf16[2048,256]{1,0:T(8,128)(2,1)S(1)} custom-call(s32[2048]{0:T(1024)S(1)} %copy-done, s32[2048]{0:T(1024)S(1)} %copy-done.1, bf16[16,128,256]{2,1,0:T(8,128)(2,1)S(1)} %all-to-all-done.2.got, bf16[4,8,512,256]{3,2,1,0:T(8,128)(2,1)} %mask_bra.1.masked), custom_call_target="tpu_custom_call" | custom-call | flops 1073741824 | bytes 2097152 | tf_op jit(solution)/shard_map/second_stage/pallas_call | solution.py:298
  141.8 19.8 %all_to_all.21 = bf16[4,512,256]{2,1,0:T(8,128)(2,1)S(1)} all-to-all(bf16[4,512,256]{2,1,0:T(8,128)(2,1)S(1)} %bitcast.10), channel_id=1, replica_groups=mesh['chan'=16,'ket'=4,'bra'=4] {'bra'}, dimensions={0} | all-to-all | bytes 2097152 | tf_op jit(solution)/shard_map/all_to_all | solution.py:355
  161.6 0.1 convert_reduce_fusion
  161.8 1.0 convert_element_type.19
  162.8 1.1 maximum_bitcast_fusion
  (30 shorter events, 0.2 us)
Async XLA Ops:
  6.5 55.6 %all-gather.5.cloned.1.call-start = ((), (), s32[]{:S(2)}) async-start(), calls=%async_computation.6 | async-start | bytes 5570560 | tf_op jit(solution)/shard_map/all_gather | solution.py:331
  8.7 104.8 %all-gather.7.cloned.1.call-start = ((), (), s32[]{:S(2)}) async-start(), calls=%async_computation.7 | async-start | bytes 5242880 | tf_op jit(solution)/shard_map/all_gather | solution.py:347
  38.7 25.5 %copy-start.2 = (bf16[8,32,512]{2,1,0:T(8,128)(2,1)}, bf16[8,32,512]{2,1,0:T(8,128)(2,1)S(1)}, u32[]{:S(2)}) copy-start(bf16[8,32,512]{2,1,0:T(8,128)(2,1)S(1)} %get-tuple-element.25) | copy-start | bytes 786436
  38.7 25.5 %copy-start.3 = (bf16[8,32,512]{2,1,0:T(8,128)(2,1)}, bf16[8,32,512]{2,1,0:T(8,128)(2,1)S(1)}, u32[]{:S(2)}) copy-start(bf16[8,32,512]{2,1,0:T(8,128)(2,1)S(1)} %get-tuple-element.26) | copy-start | bytes 786436
  38.7 8.2 %collective-permute-start = (bf16[256,512]{1,0:T(8,128)(2,1)S(1)}, bf16[256,512]{1,0:T(8,128)(2,1)S(1)}, u32[]{:S(2)}, u32[]{:S(2)}) collective-permute-start(bf16[256,512]{1,0:T(8,128)(2,1)S(1)} %bitcast.27), channel_id=1, source_target_pairs={{0,4},{4,8},{8,12},{12,0},{1,5},{5,9},{9,13},{13,1},{2,6},{6,10},{... | collective-permute-start | bytes 786440 | tf_op jit(solution)/shard_map/ppermute | solution.py:338
  40.1 8.4 %collective-permute-start.3 = (bf16[256,512]{1,0:T(8,128)(2,1)S(1)}, bf16[256,512]{1,0:T(8,128)(2,1)S(1)}, u32[]{:S(2)}, u32[]{:S(2)}) collective-permute-start(bf16[256,512]{1,0:T(8,128)(2,1)S(1)} %bitcast.23), channel_id=1, source_target_pairs={{0,12},{4,0},{8,4},{12,8},{1,13},{5,1},{9,5},{13,9},{2,14},{6,2},{... | collective-permute-start | bytes 786440 | tf_op jit(solution)/shard_map/ppermute | solution.py:339
  43.2 11.0 %collective-permute-start.2 = (bf16[256,512]{1,0:T(8,128)(2,1)S(1)}, bf16[256,512]{1,0:T(8,128)(2,1)S(1)}, u32[]{:S(2)}, u32[]{:S(2)}) collective-permute-start(bf16[256,512]{1,0:T(8,128)(2,1)S(1)} %bitcast.28), channel_id=1, source_target_pairs={{0,12},{4,0},{8,4},{12,8},{1,13},{5,1},{9,5},{13,9},{2,14},{6,2},{... | collective-permute-start | bytes 786440 | tf_op jit(solution)/shard_map/ppermute | solution.py:341
  44.5 9.7 %collective-permute-start.1 = (bf16[256,512]{1,0:T(8,128)(2,1)S(1)}, bf16[256,512]{1,0:T(8,128)(2,1)S(1)}, u32[]{:S(2)}, u32[]{:S(2)}) collective-permute-start(bf16[256,512]{1,0:T(8,128)(2,1)S(1)} %bitcast.24), channel_id=1, source_target_pairs={{0,4},{4,8},{8,12},{12,0},{1,5},{5,9},{9,13},{13,1},{2,6},{6,10},{... | collective-permute-start | bytes 786440 | tf_op jit(solution)/shard_map/ppermute | solution.py:340
  46.9 17.3 %copy-start.4 = (bf16[256,512]{1,0:T(8,128)(2,1)}, bf16[256,512]{1,0:T(8,128)(2,1)S(1)}, u32[]{:S(2)}) copy-start(bf16[256,512]{1,0:T(8,128)(2,1)S(1)} %collective-permute-done.e2) | copy-start | bytes 786436
  46.9 12.0 %collective-permute-start.4 = (bf16[256,512]{1,0:T(8,128)(2,1)S(1)}, bf16[256,512]{1,0:T(8,128)(2,1)S(1)}, u32[]{:S(2)}, u32[]{:S(2)}) collective-permute-start(bf16[256,512]{1,0:T(8,128)(2,1)S(1)} %collective-permute-done.e2), channel_id=1, source_target_pairs={{0,4},{4,8},{8,12},{12,0},{1,5},{5,9},{9,13},{13,1},{2,6},{6,10},{... | collective-permute-start | bytes 786440 | tf_op jit(solution)/shard_map/ppermute | solution.py:342
  48.6 15.7 %copy-start.5 = (bf16[256,512]{1,0:T(8,128)(2,1)}, bf16[256,512]{1,0:T(8,128)(2,1)S(1)}, u32[]{:S(2)}) copy-start(bf16[256,512]{1,0:T(8,128)(2,1)S(1)} %collective-permute-done.3.e5) | copy-start | bytes 786436
  48.6 10.3 %collective-permute-start.5 = (bf16[256,512]{1,0:T(8,128)(2,1)S(1)}, bf16[256,512]{1,0:T(8,128)(2,1)S(1)}, u32[]{:S(2)}, u32[]{:S(2)}) collective-permute-start(bf16[256,512]{1,0:T(8,128)(2,1)S(1)} %collective-permute-done.3.e5), channel_id=1, source_target_pairs={{0,12},{4,0},{8,4},{12,8},{1,13},{5,1},{9,5},{13,9},{2,14},{6,2},{... | collective-permute-start | bytes 786440 | tf_op jit(solution)/shard_map/ppermute | solution.py:343
  54.2 10.1 %copy-start.6 = (bf16[256,512]{1,0:T(8,128)(2,1)}, bf16[256,512]{1,0:T(8,128)(2,1)S(1)}, u32[]{:S(2)}) copy-start(bf16[256,512]{1,0:T(8,128)(2,1)S(1)} %collective-permute-done.2.e4) | copy-start | bytes 786436
  54.2 10.1 %copy-start.7 = (bf16[256,512]{1,0:T(8,128)(2,1)}, bf16[256,512]{1,0:T(8,128)(2,1)S(1)}, u32[]{:S(2)}) copy-start(bf16[256,512]{1,0:T(8,128)(2,1)S(1)} %collective-permute-done.1.e3) | copy-start | bytes 786436
  58.9 5.4 %copy-start.8 = (bf16[256,512]{1,0:T(8,128)(2,1)}, bf16[256,512]{1,0:T(8,128)(2,1)S(1)}, u32[]{:S(2)}) copy-start(bf16[256,512]{1,0:T(8,128)(2,1)S(1)} %collective-permute-done.4.e6) | copy-start | bytes 786436
  58.9 5.4 %copy-start.9 = (bf16[256,512]{1,0:T(8,128)(2,1)}, bf16[256,512]{1,0:T(8,128)(2,1)S(1)}, u32[]{:S(2)}) copy-start(bf16[256,512]{1,0:T(8,128)(2,1)S(1)} %collective-permute-done.5.e7) | copy-start | bytes 786436
  71.3 32.7 %all-to-all-start.1 = ((bf16[16,128,256]{2,1,0:T(8,128)(2,1)}), bf16[16,128,256]{2,1,0:T(8,128)(2,1)S(1)}, u32[]{:S(2)}, u32[]{:S(2)}) async-start(bf16[16,128,256]{2,1,0:T(8,128)(2,1)} %first_stage.2), calls=%async_computation.1 | async-start | bytes 2097152 | tf_op jit(solution)/shard_map/all_to_all | solution.py:352
  104.0 31.4 %all-to-all-start.2 = ((bf16[16,128,256]{2,1,0:T(8,128)(2,1)}), bf16[16,128,256]{2,1,0:T(8,128)(2,1)S(1)}, u32[]{:S(2)}, u32[]{:S(2)}) async-start(bf16[16,128,256]{2,1,0:T(8,128)(2,1)} %first_stage.3), calls=%async_computation.3 | async-start | bytes 2097152 | tf_op jit(solution)/shard_map/all_to_all | solution.py:352
  107.6 54.2 %reduce-scatter.2.cloned.1.call-start = ((), (), s32[]{:S(2)}) async-start(), calls=%async_computation.5 | async-start | bytes 1310720 | tf_op jit(solution)/shard_map/reduce_scatter | solution.py:354
  113.5 5.0 %copy-start = (s32[2048]{0:T(1024)S(1)}, s32[2048]{0:T(1024)}, u32[]{:S(2)}) copy-start(s32[2048]{0:T(1024)} %left_s.9) | copy-start | bytes 24580
  113.5 5.0 %copy-start.1 = (s32[2048]{0:T(1024)S(1)}, s32[2048]{0:T(1024)}, u32[]{:S(2)}) copy-start(s32[2048]{0:T(1024)} %right_s.9) | copy-start | bytes 24580
Sparse Core Ops, SparseCore 0:
  9.2 52.9 all-gather.4
  64.3 49.1 all-gather.6
  126.1 26.8 reduce-scatter.1
